TPU v7x, 32 devices: a whole 2x2x4 slice. The times are simulated.
32 devices in a mesh: shard: 4 (over x, core), rep: 8 (over z, y).
Axes of the slice: x: 2, y: 2, z: 4, core: 2. Of those that a mesh axis runs over, the one named last changes fastest.
Arguments:
- tokens: bfloat16 [64, 512, 1024], P(('shard', 'rep')), may hold values from -6 to 6
- piece_start: int32 [64], P(('shard', 'rep')), may hold values from 0 to 256, as said below
- ln1_gain: bfloat16 [1024], P('shard'), may hold values from 0.5 to 1.5
- ln1_bias: bfloat16 [1024], P('shard'), may hold values from -1 to 1
- query_key_value_weight: bfloat16 [1024, 3072], P('shard'), may hold values from -0.1875 to 0.1875
- b_qv: bfloat16 [2048], P('shard'), may hold values from -1 to 1
- attention_out_weight: bfloat16 [1024, 1024], P('shard'), may hold values from -0.75 to 0.75
- attention_out_bias: bfloat16 [1024], P('shard'), may hold values from -1 to 1
- ln2_gain: bfloat16 [1024], P('shard'), may hold values from 0.5 to 1.5
- ln2_bias: bfloat16 [1024], P('shard'), may hold values from -1 to 1
- up_weight: bfloat16 [1024, 4096], P('shard'), may hold values from -0.1875 to 0.1875
- up_bias: bfloat16 [4096], P('shard'), may hold values from -1 to 1
- down_weight: bfloat16 [4096, 1024], P('shard'), may hold values from -0.09375 to 0.09375
- down_bias: bfloat16 [1024], P('shard'), may hold values from -1 to 1
- cotangent: bfloat16 [64, 512, 1024], P(('shard', 'rep')), may hold values from -6 to 6
Outputs:
- block_out: bfloat16 [64, 512, 1024], P(('shard', 'rep'))
- input_grad: float32 [64, 512, 1024], P(('shard', 'rep'))
- grad_ln1_gain: float32 [1024], P('shard')
- grad_ln1_bias: float32 [1024], P('shard')
- grad_w_qkv: float32 [1024, 3072], P('shard')
- grad_b_qv: float32 [2048], P('shard')
- grad_w_out: float32 [1024, 1024], P('shard')
- grad_b_out: float32 [1024], P('shard')
- grad_ln2_gain: float32 [1024], P('shard')
- grad_ln2_bias: float32 [1024], P('shard')
- grad_w_up: float32 [1024, 4096], P('shard')
- grad_b_up: float32 [4096], P('shard')
- grad_w_down: float32 [4096, 1024], P('shard')
- grad_b_down: float32 [1024], P('shard')
Inputs may be any that keep to these rules, and one draw needn't show every extreme that they name: `piece_start`: some sequence's piece starts at 0 and some at 256.
All inputs are finite; a program needn't handle non-finite values.
Results may differ from a plain program's by a relative error of at most 0.014.
Values may be sent and summed in bfloat16 or wider, within the bound.
No kernel may reach another device: no remote copies, remote signals or barrier semaphores. Data moves between devices by JAX's collectives and lax.ppermute only.
A program may use at most 256 MiB of HBM per device.

v0:
```python
import math

import jax
import jax.numpy as jnp
from jax import lax
from jax.sharding import PartitionSpec as P

HEADS = 16
PIECE = 256
MICRO = 2


eps_norm = 1e-05
masked_fill = -1e30


def contract_rows(left, right):
    return lax.dot_general(
        left, right, (((0,), (0,)), ((), ())), preferred_element_type=jnp.float32
    )


def contract_cols(left, right):
    return lax.dot_general(
        left, right, (((1,), (1,)), ((), ())), preferred_element_type=jnp.float32
    )


def normalize(values_in, gain_vec, shift_vec):
    center = values_in - jnp.mean(values_in, axis=-1, keepdims=True)
    spread_sq = jnp.mean(center * center, axis=-1, keepdims=True)
    return center * lax.rsqrt(spread_sq + eps_norm) * gain_vec + shift_vec


def gelu_tanh(pre_act):
    return (
        0.5
        * pre_act
        * (1.0 + jnp.tanh(0.7978845608028654 * (pre_act + 0.044715 * pre_act * pre_act * pre_act)))
    )


def visible_bias(start_at, seq_len, piece_len, head_count):
    position = jnp.arange(seq_len, dtype=jnp.int32)
    inside = (position >= start_at) & (position < start_at + piece_len)
    allowed = (position[None, :] <= position[:, None]) | inside[:, None] & inside[None, :]
    distance = jnp.abs(position[:, None] - position[None, :]).astype(jnp.float32)
    slopes = jnp.exp2(-8.0 * (jnp.arange(head_count, dtype=jnp.float32) + 1.0) / head_count)
    return (allowed, -slopes[:, None, None] * distance[None, :, :])


def masked_scores(queries, key_rows, start_at):
    seq_len, head_count, head_dim = queries.shape
    allowed, alibi_bias = visible_bias(start_at, seq_len, PIECE, head_count)
    scores = (
        jnp.einsum("qhd,khd->hqk", queries, key_rows, preferred_element_type=jnp.float32)
        * (1.0 / math.sqrt(head_dim))
        + alibi_bias
    )
    return jnp.where(allowed[None, :, :], scores, masked_fill)


def attend_forward(seq_item):
    queries, key_rows, value_rows, start_at = seq_item
    scores = masked_scores(queries, key_rows, start_at)
    row_top = jnp.max(scores, axis=-1, keepdims=True)
    exponent = jnp.exp(scores - row_top)
    row_total = jnp.sum(exponent, axis=-1, keepdims=True)
    probs_low = (exponent / row_total).astype(jnp.bfloat16)
    attention_result = jnp.einsum(
        "hqk,khd->qhd", probs_low, value_rows, preferred_element_type=jnp.float32
    )
    return (attention_result.astype(jnp.bfloat16), row_top + jnp.log(row_total))


def attend_backward(seq_item):
    queries, key_rows, value_rows, start_at, grad_out, log_total = seq_item
    scale_qk = 1.0 / math.sqrt(queries.shape[2])
    probs = jnp.exp(masked_scores(queries, key_rows, start_at) - log_total)
    grad_probs = jnp.einsum(
        "qhd,khd->hqk", grad_out, value_rows, preferred_element_type=jnp.float32
    )
    inner_sum = jnp.sum(probs * grad_probs, axis=-1, keepdims=True)
    grad_scores = (probs * (grad_probs - inner_sum)).astype(jnp.bfloat16)
    grad_query = (
        jnp.einsum("hqk,khd->qhd", grad_scores, key_rows, preferred_element_type=jnp.float32)
        * scale_qk
    )
    grad_key = (
        jnp.einsum("hqk,qhd->khd", grad_scores, queries, preferred_element_type=jnp.float32)
        * scale_qk
    )
    grad_value = jnp.einsum(
        "hqk,qhd->khd", probs.astype(jnp.bfloat16), grad_out, preferred_element_type=jnp.float32
    )
    return (
        grad_query.astype(jnp.bfloat16),
        grad_key.astype(jnp.bfloat16),
        grad_value.astype(jnp.bfloat16),
    )


def forward_pass(token_block, start_vec, attn_weights, mlp_weights):
    gain_one, shift_one, w_joined, bias_qv, w_proj, bias_proj = attn_weights
    gain_two, shift_two, w_in, bias_in, w_back, bias_back = mlp_weights
    seq_count, seq_len, width = token_block.shape
    tokens_f = token_block.astype(jnp.float32).reshape(seq_count * seq_len, width)
    first_normed = normalize(
        tokens_f, gain_one.astype(jnp.float32), shift_one.astype(jnp.float32)
    ).astype(jnp.bfloat16)
    joined_heads = jnp.dot(first_normed, w_joined, preferred_element_type=jnp.float32)
    bias_qv_f = bias_qv.astype(jnp.float32)
    queries = (joined_heads[:, :width] + bias_qv_f[:width]).astype(jnp.bfloat16)
    key_rows = joined_heads[:, width : 2 * width].astype(jnp.bfloat16)
    value_rows = (joined_heads[:, 2 * width :] + bias_qv_f[width:]).astype(jnp.bfloat16)
    split_shape = (seq_count, seq_len, HEADS, width // HEADS)
    attention_result, log_total = lax.map(
        attend_forward,
        (
            queries.reshape(split_shape),
            key_rows.reshape(split_shape),
            value_rows.reshape(split_shape),
            start_vec,
        ),
    )
    attention_result = attention_result.reshape(seq_count * seq_len, width)
    middle = (
        tokens_f
        + jnp.dot(attention_result, w_proj, preferred_element_type=jnp.float32)
        + bias_proj.astype(jnp.float32)
    )
    second_normed = normalize(
        middle, gain_two.astype(jnp.float32), shift_two.astype(jnp.float32)
    ).astype(jnp.bfloat16)
    hidden_before_gelu = jnp.dot(
        second_normed, w_in, preferred_element_type=jnp.float32
    ) + bias_in.astype(jnp.float32)
    hidden_activation = gelu_tanh(hidden_before_gelu).astype(jnp.bfloat16)
    block_rows = (
        middle
        + jnp.dot(hidden_activation, w_back, preferred_element_type=jnp.float32)
        + bias_back.astype(jnp.float32)
    )
    kept = (
        tokens_f,
        first_normed,
        queries,
        key_rows,
        value_rows,
        attention_result,
        log_total,
        middle,
        second_normed,
        hidden_before_gelu,
        hidden_activation,
    )
    return (block_rows.reshape(seq_count, seq_len, width).astype(jnp.bfloat16), kept)


def backward_pass(kept, cot_block, start_vec, attn_weights, mlp_weights):
    (
        tokens_f,
        first_normed,
        queries,
        key_rows,
        value_rows,
        attention_result,
        log_total,
        middle,
        second_normed,
        hidden_before_gelu,
        hidden_activation,
    ) = kept
    gain_one, shift_one, w_joined, bias_qv, w_proj, bias_proj = attn_weights
    gain_two, shift_two, w_in, bias_in, w_back, bias_back = mlp_weights
    seq_count, seq_len, width = cot_block.shape
    cot_f = cot_block.astype(jnp.float32).reshape(seq_count * seq_len, width)
    d_two = cot_block.reshape(seq_count * seq_len, width)
    grad_w_back = contract_rows(hidden_activation, d_two)
    grad_b_back = jnp.sum(cot_f, axis=0)
    d_hidden = contract_cols(d_two, w_back)
    gelu_pull = jax.vjp(gelu_tanh, hidden_before_gelu)[1]
    d_pre = gelu_pull(d_hidden)[0].astype(jnp.bfloat16)
    grad_w_in = contract_rows(second_normed, d_pre)
    grad_b_in = jnp.sum(d_pre.astype(jnp.float32), axis=0)
    d_normed_two = contract_cols(d_pre, w_in)
    norm_pull_two = jax.vjp(
        normalize, middle, gain_two.astype(jnp.float32), shift_two.astype(jnp.float32)
    )[1]
    d_middle_norm, grad_gain_two, grad_shift_two = norm_pull_two(d_normed_two)
    d_middle = cot_f + d_middle_norm
    d_one = d_middle.astype(jnp.bfloat16)
    grad_w_proj = contract_rows(attention_result, d_one)
    grad_b_proj = jnp.sum(d_one.astype(jnp.float32), axis=0)
    d_attended = contract_cols(d_one, w_proj).astype(jnp.bfloat16)
    split_shape = (seq_count, seq_len, HEADS, width // HEADS)
    grad_query, grad_key, grad_value = lax.map(
        attend_backward,
        (
            queries.reshape(split_shape),
            key_rows.reshape(split_shape),
            value_rows.reshape(split_shape),
            start_vec,
            d_attended.reshape(split_shape),
            log_total,
        ),
    )
    row_count = seq_count * seq_len
    grad_query = grad_query.reshape(row_count, width)
    grad_value = grad_value.reshape(row_count, width)
    d_joined = jnp.concatenate([grad_query, grad_key.reshape(row_count, width), grad_value], axis=1)
    grad_w_joined = contract_rows(first_normed, d_joined)
    grad_b_qv = jnp.concatenate(
        [
            jnp.sum(grad_query.astype(jnp.float32), axis=0),
            jnp.sum(grad_value.astype(jnp.float32), axis=0),
        ]
    )
    d_normed = contract_cols(d_joined, w_joined)
    norm_pull_one = jax.vjp(
        normalize, tokens_f, gain_one.astype(jnp.float32), shift_one.astype(jnp.float32)
    )[1]
    d_tokens_norm, grad_gain_one, grad_shift_one = norm_pull_one(d_normed)
    input_rows = (d_middle + d_tokens_norm).reshape(seq_count, seq_len, width)
    grads = (
        grad_gain_one,
        grad_shift_one,
        grad_w_joined,
        grad_b_qv,
        grad_w_proj,
        grad_b_proj,
        grad_gain_two,
        grad_shift_two,
        grad_w_in,
        grad_b_in,
        grad_w_back,
        grad_b_back,
    )
    return (input_rows, grads)


def add_up(running, fresh):
    if running is None:
        return fresh
    return tuple((total + part for total, part in zip(running, fresh)))


def body(
    tokens,
    piece_start,
    ln1_gain,
    ln1_bias,
    query_key_value_weight,
    b_qv,
    attention_out_weight,
    attention_out_bias,
    ln2_gain,
    ln2_bias,
    up_weight,
    up_bias,
    down_weight,
    down_bias,
    cotangent,
):
    per_batch = tokens.shape[0] // MICRO
    full_total = None
    shard_total = None
    out_parts = []
    grad_parts = []
    for micro_step in range(MICRO):
        first_row = micro_step * per_batch
        token_block = tokens[first_row : first_row + per_batch]
        cot_block = cotangent[first_row : first_row + per_batch]
        start_vec = piece_start[first_row : first_row + per_batch]
        attn_fwd_w = (
            lax.all_gather(ln1_gain, "shard", axis=0, tiled=True),
            lax.all_gather(ln1_bias, "shard", axis=0, tiled=True),
            lax.all_gather(query_key_value_weight, "shard", axis=0, tiled=True),
            lax.all_gather(b_qv, "shard", axis=0, tiled=True),
            lax.all_gather(attention_out_weight, "shard", axis=0, tiled=True),
            lax.all_gather(attention_out_bias, "shard", axis=0, tiled=True),
        )
        mlp_fwd_w = (
            lax.all_gather(ln2_gain, "shard", axis=0, tiled=True),
            lax.all_gather(ln2_bias, "shard", axis=0, tiled=True),
            lax.all_gather(up_weight, "shard", axis=0, tiled=True),
            lax.all_gather(up_bias, "shard", axis=0, tiled=True),
            lax.all_gather(down_weight, "shard", axis=0, tiled=True),
            lax.all_gather(down_bias, "shard", axis=0, tiled=True),
        )
        block_rows, kept = forward_pass(token_block, start_vec, attn_fwd_w, mlp_fwd_w)
        out_parts.append(block_rows)
        attn_back_w = (
            lax.all_gather(ln1_gain, "shard", axis=0, tiled=True),
            lax.all_gather(ln1_bias, "shard", axis=0, tiled=True),
            lax.all_gather(query_key_value_weight, "shard", axis=0, tiled=True),
            lax.all_gather(b_qv, "shard", axis=0, tiled=True),
            lax.all_gather(attention_out_weight, "shard", axis=0, tiled=True),
            lax.all_gather(attention_out_bias, "shard", axis=0, tiled=True),
        )
        mlp_back_w = (
            lax.all_gather(ln2_gain, "shard", axis=0, tiled=True),
            lax.all_gather(ln2_bias, "shard", axis=0, tiled=True),
            lax.all_gather(up_weight, "shard", axis=0, tiled=True),
            lax.all_gather(up_bias, "shard", axis=0, tiled=True),
            lax.all_gather(down_weight, "shard", axis=0, tiled=True),
            lax.all_gather(down_bias, "shard", axis=0, tiled=True),
        )
        input_rows, grads = backward_pass(kept, cot_block, start_vec, attn_back_w, mlp_back_w)
        grad_parts.append(input_rows)
        full_total = add_up(full_total, grads)
    shard_total = (
        lax.psum_scatter(
            full_total[0].astype(jnp.bfloat16), "shard", scatter_dimension=0, tiled=True
        ).astype(jnp.float32),
        lax.psum_scatter(
            full_total[1].astype(jnp.bfloat16), "shard", scatter_dimension=0, tiled=True
        ).astype(jnp.float32),
        lax.psum_scatter(
            full_total[2].astype(jnp.bfloat16), "shard", scatter_dimension=0, tiled=True
        ).astype(jnp.float32),
        lax.psum_scatter(
            full_total[3].astype(jnp.bfloat16), "shard", scatter_dimension=0, tiled=True
        ).astype(jnp.float32),
        lax.psum_scatter(
            full_total[4].astype(jnp.bfloat16), "shard", scatter_dimension=0, tiled=True
        ).astype(jnp.float32),
        lax.psum_scatter(
            full_total[5].astype(jnp.bfloat16), "shard", scatter_dimension=0, tiled=True
        ).astype(jnp.float32),
        lax.psum_scatter(
            full_total[6].astype(jnp.bfloat16), "shard", scatter_dimension=0, tiled=True
        ).astype(jnp.float32),
        lax.psum_scatter(
            full_total[7].astype(jnp.bfloat16), "shard", scatter_dimension=0, tiled=True
        ).astype(jnp.float32),
        lax.psum_scatter(
            full_total[8].astype(jnp.bfloat16), "shard", scatter_dimension=0, tiled=True
        ).astype(jnp.float32),
        lax.psum_scatter(
            full_total[9].astype(jnp.bfloat16), "shard", scatter_dimension=0, tiled=True
        ).astype(jnp.float32),
        lax.psum_scatter(
            full_total[10].astype(jnp.bfloat16), "shard", scatter_dimension=0, tiled=True
        ).astype(jnp.float32),
        lax.psum_scatter(
            full_total[11].astype(jnp.bfloat16), "shard", scatter_dimension=0, tiled=True
        ).astype(jnp.float32),
    )
    summed = lax.psum(
        (
            shard_total[0],
            shard_total[1],
            shard_total[2],
            shard_total[3],
            shard_total[4],
            shard_total[5],
            shard_total[6],
            shard_total[7],
            shard_total[8],
            shard_total[9],
            shard_total[10],
            shard_total[11],
        ),
        "rep",
    )
    block_out = jnp.concatenate(out_parts, axis=0)
    input_grad = jnp.concatenate(grad_parts, axis=0)
    return (
        block_out,
        input_grad,
        summed[0],
        summed[1],
        summed[2],
        summed[3],
        summed[4],
        summed[5],
        summed[6],
        summed[7],
        summed[8],
        summed[9],
        summed[10],
        summed[11],
    )


def solution(mesh):
    in_specs = (
        P(("shard", "rep"), None, None),
        P(("shard", "rep")),
        P("shard"),
        P("shard"),
        P("shard", None),
        P("shard"),
        P("shard", None),
        P("shard"),
        P("shard"),
        P("shard"),
        P("shard", None),
        P("shard"),
        P("shard", None),
        P("shard"),
        P(("shard", "rep"), None, None),
    )
    out_specs = (
        P(("shard", "rep"), None, None),
        P(("shard", "rep"), None, None),
        P("shard"),
        P("shard"),
        P("shard", None),
        P("shard"),
        P("shard", None),
        P("shard"),
        P("shard"),
        P("shard"),
        P("shard", None),
        P("shard"),
        P("shard", None),
        P("shard"),
    )
    return jax.shard_map(body, mesh=mesh, in_specs=in_specs, out_specs=out_specs, check_vma=False)
```

profile of v0, /device:TPU:0, one launch (start us, length us, event | category | flops | bytes accessed | tf_op | source)
XLA Modules:
  0.0 1084.9 jit_solution(5710278252859314554)
XLA Ops:
  14.6 6.0 all-gather.5
  20.6 5.4 all-gather.4
  25.9 5.1 all-gather.3
  31.0 5.1 all-gather.1
  36.1 5.1 all-gather
  42.8 5.2 all-gather.2
  48.0 5.2 all_gather.33
  54.3 4.5 all-gather.12.cloned.1.call-done
  58.9 5.7 fusion.107
  70.0 6.1 fusion.104
  82.3 6.3 fusion.56
  98.6 12.3 %fusion.122 = (f32[16,512]{1,0:T(8,128)S(1)}, f32[16,512,512]{1,2,0:T(8,128)}) fusion(f32[512,512]{0,1:T(8,128)} %abs_convert_fusion, f32[16]{0:T(128)S(1)} %exponential_negate_fusion, bf16[512,16,64]{0,2,1:T(8,128)(2,1)} %bitcast.231, bf16[512,16,64]{0,2,1:T(8,128)(2,1)} %bitcast.225, pred[512,512]{0,1:T(8,128)(4,1)} %fusion.87), kind=kOutput, calls=%fused_computation.221 | convolution fusion | flops 557834240 | bytes 20217920 | tf_op jit(solution)/shard_map/while/body/eval_jaxpr/qhd,khd->hqk/dot_general | solution.py:56
  110.9 8.4 fusion.2
  119.4 8.6 fusion.61
  127.9 3.4 fusion.123
  133.1 8.7 fusion.120
  141.8 8.4 fusion.3
  150.2 10.2 fusion.60
  164.7 12.1 %fusion.112 = f32[512,4096]{1,0:T(8,128)} fusion(bf16[1024,4096]{1,0:T(8,128)(2,1)} %all-gather.16.cloned.1.call-done, f32[512,1024]{1,0:T(8,128)} %copy-done.11, f32[1024]{0:T(1024)S(1)} %bitcast.268, f32[1024]{0:T(1024)S(1)} %bitcast.260, f32[512]{0:T(512)S(1)} %fusion.96, f32[512]{0:T(512)S(1)} %broadcast_multiply_fusion.2), kind=kOutput, calls=%fused_computation.213 | convolution fusion | flops 4297588736 | bytes 18886656 | tf_op jit(solution)/shard_map/dot_general | solution.py:135
  176.8 7.3 fusion.113
  184.1 18.6 %all-gather.18.cloned.1.call-done = bf16[4096,1024]{1,0:T(8,128)(2,1)} async-done(((bf16[1024,1024]{1,0:T(8,128)(2,1)}), bf16[4096,1024]{1,0:T(8,128)(2,1)}) %all-gather.18.cloned.1.call-update) | async-done | bytes 8388624 | tf_op jit(solution)/shard_map/all_gather | solution.py:288
  202.7 15.2 %convert_reduce_fusion.1 = (f32[4096]{0:T(1024)}, bf16[512,4096]{1,0:T(8,128)(2,1)S(1)}) fusion(bf16[4096,1024]{1,0:T(8,128)(2,1)} %all-gather.18.cloned.1.call-done, bf16[2,512,1024]{2,1,0:T(8,128)(2,1)S(1)} %copy-done.4, f32[512,4096]{1,0:T(8,128)} %fusion.112, f32[4096]{0:T(1024)S(1)} %convert_element_type.321), kind=kOutput, calls=%fused_computation.44 | convolution fusion | flops 4351586304 | bytes 22052864 | tf_op jit(solution)/shard_map/dot_general | solution.py:24
  217.8 16.6 %convert_reduce_fusion = (f32[4096]{0:T(1024)}, bf16[512,4096]{1,0:T(8,128)(2,1)}) fusion(bf16[4096,1024]{1,0:T(8,128)(2,1)S(1)} %copy-done.101, bf16[2,512,1024]{2,1,0:T(8,128)(2,1)S(1)} %copy-done.4, f32[512,4096]{1,0:T(8,128)} %fusion.113, f32[4096]{0:T(1024)S(1)} %convert_element_type.321), kind=kOutput, calls=%fused_computation.43 | convolution fusion | flops 4351586304 | bytes 22052864 | tf_op jit(solution)/shard_map/dot_general | solution.py:24
  234.4 8.8 fusion.124
  243.2 8.4 multiply_reduce_fusion.3
  255.7 3.3 fusion.125
  260.9 14.4 %multiply_reduce_fusion.1 = (f32[16,512]{1,0:T(8,128)}, f32[16,512,512]{1,2,0:T(8,128)}) fusion(f32[16,512,512]{1,2,0:T(8,128)} %get-tuple-element.190, f32[16,512]{1,0:T(8,128)} %log_add_fusion.1, bf16[512,16,64]{0,2,1:T(8,128)(2,1)S(1)} %bitcast.219, bf16[512,16,64]{0,2,1:T(8,128)(2,1)} %bitcast.233), kind=kOutput, calls=%fused_computation.10 | convolution fusion | flops 549445632 | bytes 35717120 | tf_op jit(solution)/shard_map/while/body/eval_jaxpr/qhd,khd->hqk/dot_general | solution.py:80
  277.7 10.6 multiply_convert_fusion.1
  288.3 7.5 multiply_convert_fusion.6
  300.9 16.6 %multiply_reduce_fusion = (f32[16,512]{1,0:T(8,128)}, f32[16,512,512]{1,2,0:T(8,128)}) fusion(f32[16,512,512]{1,2,0:T(8,128)} %get-tuple-element.186, f32[16,512]{1,0:T(8,128)} %log_add_fusion, bf16[512,16,64]{0,2,1:T(8,128)(2,1)} %bitcast.221, bf16[512,16,64]{0,2,1:T(8,128)(2,1)} %bitcast.229), kind=kOutput, calls=%fused_computation.7 | convolution fusion | flops 549445632 | bytes 35717120 | tf_op jit(solution)/shard_map/while/body/eval_jaxpr/qhd,khd->hqk/dot_general | solution.py:80
  317.5 10.5 multiply_convert_fusion
  328.0 7.5 multiply_convert_fusion.4
  341.5 9.5 convert_reduce_fusion.8
  351.1 9.6 convert_reduce_fusion.10
  360.8 9.7 fusion.73
  370.6 11.7 %add_convert_fusion.2 = bf16[1024,3072]{1,0:T(8,128)(2,1)} fusion(f32[1024,3072]{1,0:T(8,128)} %fusion.73, bf16[512,1024]{0,1:T(8,128)(2,1)S(1)} %bitcast.247, bf16[512,1024]{0,1:T(8,128)(2,1)S(1)} %bitcast.244, bf16[512,1024]{0,1:T(8,128)(2,1)S(1)} %bitcast.239, f32[512]{0:T(512)S(1)} %copy-done.65, f32[512]{0:T(512)S(1)} %copy-done.57, ...), kind=kOutput, calls=%fused_computation.20 | convolution fusion | flops 3240099840 | bytes 23080960 | tf_op jit(solution)/shard_map/dot_general | solution.py:18
  383.0 16.3 %fusion.80 = f32[4096,1024]{1,0:T(8,128)} fusion(bf16[2,512,1024]{2,1,0:T(8,128)(2,1)} %param.29, f32[512,4096]{1,0:T(8,128)} %fusion.112, f32[4096]{0:T(1024)S(1)} %copy-done.83), kind=kOutput, calls=%fused_computation.146 | convolution fusion | flops 4315938816 | bytes 26230784 | tf_op jit(solution)/shard_map/dot_general | solution.py:18
  399.3 14.8 %add_convert_fusion = bf16[4096,1024]{1,0:T(8,128)(2,1)} fusion(f32[4096,1024]{1,0:T(8,128)} %fusion.80, bf16[2,512,1024]{2,1,0:T(8,128)(2,1)S(1)} %copy-done.5, f32[512,4096]{1,0:T(8,128)} %fusion.113, f32[4096]{0:T(1024)S(1)} %copy-done.83), kind=kOutput, calls=%fused_computation.4 | convolution fusion | flops 4324327424 | bytes 34619392 | tf_op jit(solution)/shard_map/dot_general | solution.py:18
  414.7 13.4 %fusion.111 = f32[1024,4096]{1,0:T(8,128)} fusion(bf16[512,4096]{1,0:T(8,128)(2,1)} %copy-done.110, f32[512,1024]{1,0:T(8,128)} %copy-done.11, f32[1024]{0:T(1024)S(1)} %bitcast.270, f32[1024]{0:T(1024)S(1)} %bitcast.264, f32[512]{0:T(512)S(1)} %copy-done.89, f32[512]{0:T(512)S(1)} %copy-done.71), kind=kOutput, calls=%fused_computation.212 | convolution fusion | flops 4297588736 | bytes 23080960 | tf_op jit(solution)/shard_map/dot_general | solution.py:18
  428.1 15.8 %add_convert_fusion.1 = bf16[1024,4096]{1,0:T(8,128)(2,1)} fusion(f32[1024,4096]{1,0:T(8,128)} %fusion.111, bf16[512,4096]{1,0:T(8,128)(2,1)} %get-tuple-element.210, f32[512,1024]{1,0:T(8,128)} %copy-done.13, f32[512]{0:T(512)S(1)} %copy-done.87, f32[512]{0:T(512)S(1)} %copy-done.73, f32[1024]{0:T(1024)S(1)} %bitcast.271, f32[1024]{0:T(1024)S(1)} %bitcast.265), kind=kOutput, calls=%fused_computation.5 | convolution fusion | flops 4305977344 | bytes 31469568 | tf_op jit(solution)/shard_map/dot_general | solution.py:18
  447.1 5.3 all-gather.6
  455.1 8.1 fusion.72
  463.4 8.1 fusion.49
  474.0 12.5 %all-reduce.9 = (bf16[1024]{0:T(1024)(128)(2,1)S(1)}, bf16[1024]{0:T(1024)(128)(2,1)S(1)}, bf16[2048]{0:T(1024)(128)(2,1)S(1)}, bf16[1024]{0:T(1024)(128)(2,1)S(...) all-reduce(bf16[1024]{0:T(1024)(128)(2,1)S(1)} %add_convert_fusion., ...), channel_id=2, replica_groups=mesh['shard'=4,'rep'=8] {'shard'}, use_global_device_ids=true, to_apply=%region_24.25.clone | all-reduce | flops 12288 | bytes 49152
  487.0 12.2 %fusion.68 = bf16[1,512,1024]{2,1,0:T(8,128)(2,1)S(1)} fusion(f32[512,1024]{1,0:T(8,128)} %copy-done.11, bf16[4096,1024]{1,0:T(8,128)(2,1)} %all-gather.18.cloned.1.call-done, f32[1024]{0:T(1024)S(1)} %bitcast.276, f32[512,4096]{1,0:T(8,128)} %fusion.112, f32[4096]{0:T(1024)S(1)} %copy-done.83), kind=kOutput, calls=%fused_computation.136 | convolution fusion | flops 4317511680 | bytes 19943424 | tf_op jit(solution)/shard_map/dot_general | solution.py:141
  499.3 11.5 %fusion.69 = bf16[1,512,1024]{2,1,0:T(8,128)(2,1)S(1)} fusion(f32[512,1024]{1,0:T(8,128)S(1)} %copy-done.16, bf16[4096,1024]{1,0:T(8,128)(2,1)} %all-gather.18.cloned.1.call-done, f32[1024]{0:T(1024)S(1)} %bitcast.277, f32[512,4096]{1,0:T(8,128)} %fusion.113, f32[4096]{0:T(1024)S(1)} %copy-done.83), kind=kOutput, calls=%fused_computation.137 | convolution fusion | flops 4317511680 | bytes 19943424 | tf_op jit(solution)/shard_map/dot_general | solution.py:141
  518.2 71.8 %reduce-scatter.9.cloned.1.call-done = bf16[256,4096]{1,0:T(8,128)(2,1)} async-done(((bf16[1024,4096]{1,0:T(8,128)(2,1)}), bf16[256,4096]{1,0:T(8,128)(2,1)}) %reduce-scatter.9.cloned.1.call-update) | async-done | bytes 2097168 | tf_op jit(solution)/shard_map/reduce_scatter | solution.py:337
  590.0 487.6 %all-reduce.11 = (f32[256]{0:T(256)}, f32[256]{0:T(256)}, f32[256,3072]{1,0:T(8,128)}, f32[512]{0:T(512)}, f32[256,1024]{1,0:T(8,128)}, /*index=5*/f32[256]{0:T(...) all-reduce(f32[256]{0:T(256)S(1)} %dynamic-slice_convert_fusion.7, ...), channel_id=1, replica_groups=mesh['shard'=4,'rep'=8] {'rep'}, use_global_device_ids=true, to_apply=%region_25.26 | all-reduce | flops 3148800 | bytes 18898944 | tf_op jit(solution)/shard_map/psum | solution.py:350
  (348 shorter events, 70.9 us)
Async XLA Ops:
  7.2 51.7 %all-gather.12.cloned.1.call-start = ((), (), s32[]{:S(2)}) async-start(), calls=%async_computation.4 | async-start | bytes 7864320 | tf_op jit(solution)/shard_map/all_gather | solution.py:278
  8.0 33.1 %copy-start.2 = (bf16[2,512,1024]{2,1,0:T(8,128)(2,1)S(1)}, bf16[2,512,1024]{2,1,0:T(8,128)(2,1)}, u32[]{:S(2)}) copy-start(bf16[2,512,1024]{2,1,0:T(8,128)(2,1)} %param.15) | copy-start | bytes 6291460
  8.0 119.9 %all-gather.14.cloned.1.call-start = ((), (), s32[]{:S(2)}) async-start(), calls=%async_computation.5 | async-start | bytes 2621440 | tf_op jit(solution)/shard_map/all_gather | solution.py:280
  8.7 155.9 %all-gather.16.cloned.1.call-start = ((), (), s32[]{:S(2)}) async-start(), calls=%async_computation.6 | async-start | bytes 10485760 | tf_op jit(solution)/shard_map/all_gather | solution.py:286
  9.5 193.2 %all-gather.18.cloned.1.call-start = ((), (), s32[]{:S(2)}) async-start(), calls=%async_computation.7 | async-start | bytes 10485760 | tf_op jit(solution)/shard_map/all_gather | solution.py:288
  10.1 37.9 %copy-start.98 = (bf16[1024]{0:T(1024)(128)(2,1)S(1)}, bf16[1024]{0:T(1024)(128)(2,1)}, u32[]{:S(2)}) copy-start(bf16[1024]{0:T(1024)(128)(2,1)} %param.26) | copy-start | bytes 6148
  10.1 508.1 %reduce-scatter.7.cloned.1.call-start = ((), (), s32[]{:S(2)}) async-start(), calls=%async_computation.9 | async-start | bytes 2621440 | tf_op jit(solution)/shard_map/reduce_scatter | solution.py:325
  20.6 156.2 %copy-start.90 = (f32[4,1,256]{2,1,0:T(1,128)}, f32[4,1,256]{2,1,0:T(1,128)S(1)}, u32[]{:S(2)}) copy-start(f32[4,1,256]{2,1,0:T(1,128)S(1)} %convert_element_type.398) | copy-start | bytes 12292
  25.9 225.8 %copy-start.78 = (f32[4,1,256]{2,1,0:T(1,128)}, f32[4,1,256]{2,1,0:T(1,128)S(1)}, u32[]{:S(2)}) copy-start(f32[4,1,256]{2,1,0:T(1,128)S(1)} %convert_element_type.397) | copy-start | bytes 12292
  36.1 33.9 %copy-start.92 = (f32[4,1,256]{2,1,0:T(1,128)}, f32[4,1,256]{2,1,0:T(1,128)S(1)}, u32[]{:S(2)}) copy-start(f32[4,1,256]{2,1,0:T(1,128)S(1)} %convert_element_type.394) | copy-start | bytes 12292
  41.1 28.9 %copy-start.51 = (f32[4,1,256]{2,1,0:T(1,128)}, f32[4,1,256]{2,1,0:T(1,128)S(1)}, u32[]{:S(2)}) copy-start(f32[4,1,256]{2,1,0:T(1,128)S(1)} %convert_element_type.393) | copy-start | bytes 12292
  41.5 23.1 %copy-start.56 = (f32[512]{0:T(512)}, f32[512]{0:T(512)S(1)}, u32[]{:S(2)}) copy-start(f32[512]{0:T(512)S(1)} %get-tuple-element.211) | copy-start | bytes 6148
  41.5 28.5 %copy-start.58 = (f32[512]{0:T(512)}, f32[512]{0:T(512)S(1)}, u32[]{:S(2)}) copy-start(f32[512]{0:T(512)S(1)} %get-tuple-element.212) | copy-start | bytes 6148
  42.2 27.8 %copy-start.61 = (f32[512]{0:T(512)}, f32[512]{0:T(512)S(1)}, u32[]{:S(2)}) copy-start(f32[512]{0:T(512)S(1)} %fusion.95) | copy-start | bytes 6148
  42.8 21.8 %copy-start.64 = (f32[512]{0:T(512)}, f32[512]{0:T(512)S(1)}, u32[]{:S(2)}) copy-start(f32[512]{0:T(512)S(1)} %fusion.97) | copy-start | bytes 6148
  53.2 164.6 %copy-start.82 = (f32[4096]{0:T(1024)}, f32[4096]{0:T(1024)S(1)}, u32[]{:S(2)}) copy-start(f32[4096]{0:T(1024)S(1)} %convert_element_type.321) | copy-start | bytes 49156
  70.0 63.0 %copy-start.25 = (bf16[512,1024]{0,1:T(8,128)(2,1)}, bf16[512,1024]{0,1:T(8,128)(2,1)S(1)}, u32[]{:S(2)}) copy-start(bf16[512,1024]{0,1:T(8,128)(2,1)S(1)} %copy.75) | copy-start | bytes 3145732
  131.4 120.3 %copy-start.70 = (f32[512]{0:T(512)}, f32[512]{0:T(512)S(1)}, u32[]{:S(2)}) copy-start(f32[512]{0:T(512)S(1)} %broadcast_multiply_fusion.2) | copy-start | bytes 6148
  161.8 90.0 %copy-start.72 = (f32[512]{0:T(512)}, f32[512]{0:T(512)S(1)}, u32[]{:S(2)}) copy-start(f32[512]{0:T(512)S(1)} %broadcast_multiply_fusion) | copy-start | bytes 6148
  163.4 88.3 %copy-start.88 = (f32[512]{0:T(512)}, f32[512]{0:T(512)S(1)}, u32[]{:S(2)}) copy-start(f32[512]{0:T(512)S(1)} %fusion.96) | copy-start | bytes 6148
  163.4 88.3 %copy-start.86 = (f32[512]{0:T(512)}, f32[512]{0:T(512)S(1)}, u32[]{:S(2)}) copy-start(f32[512]{0:T(512)S(1)} %fusion.98) | copy-start | bytes 6148
  164.7 12.1 %copy-start.14 = (f32[512,1024]{1,0:T(8,128)S(1)}, f32[512,1024]{1,0:T(8,128)}, u32[]{:S(2)}) copy-start(f32[512,1024]{1,0:T(8,128)} %copy-done.13) | copy-start | bytes 6291460
  164.7 12.1 %copy-start.102 = (bf16[1024,4096]{1,0:T(8,128)(2,1)S(1)}, bf16[1024,4096]{1,0:T(8,128)(2,1)}, u32[]{:S(2)}) copy-start(bf16[1024,4096]{1,0:T(8,128)(2,1)} %all-gather.16.cloned.1.call-done) | copy-start | bytes 25165828
  176.8 25.9 %copy-start.4 = (bf16[2,512,1024]{2,1,0:T(8,128)(2,1)S(1)}, bf16[2,512,1024]{2,1,0:T(8,128)(2,1)}, u32[]{:S(2)}) copy-start(bf16[2,512,1024]{2,1,0:T(8,128)(2,1)} %param.29) | copy-start | bytes 6291460
  202.7 15.2 %copy-start.101 = (bf16[4096,1024]{1,0:T(8,128)(2,1)S(1)}, bf16[4096,1024]{1,0:T(8,128)(2,1)}, u32[]{:S(2)}) copy-start(bf16[4096,1024]{1,0:T(8,128)(2,1)} %all-gather.18.cloned.1.call-done) | copy-start | bytes 25165828
  217.8 25.4 %copy-start.110 = (bf16[512,4096]{1,0:T(8,128)(2,1)}, bf16[512,4096]{1,0:T(8,128)(2,1)S(1)}, u32[]{:S(2)}) copy-start(bf16[512,4096]{1,0:T(8,128)(2,1)S(1)} %get-tuple-element.208) | copy-start | bytes 12582916
  260.9 14.4 %slice-start = ((s8[16777216]{0:T(1024)(128)(4,1)}), s8[4194304]{0:T(1024)(128)(4,1)S(1)}, s32[]{:S(2)}) async-start(s8[16777216]{0:T(1024)(128)(4,1)} %bitcast.215), calls=%async_computation.12 | async-start | bytes 8388608
  260.9 14.4 %slice-start.1 = ((s8[16777216]{0:T(1024)(128)(4,1)}), s8[4194304]{0:T(1024)(128)(4,1)S(1)}, s32[]{:S(2)}) async-start(s8[16777216]{0:T(1024)(128)(4,1)} %bitcast.215), calls=%async_computation.13 | async-start | bytes 8388608
  260.9 15.6 %slice-start.2 = ((s8[16777216]{0:T(1024)(128)(4,1)}), s8[4194304]{0:T(1024)(128)(4,1)S(1)}, s32[]{:S(2)}) async-start(s8[16777216]{0:T(1024)(128)(4,1)} %bitcast.215), calls=%async_computation.14 | async-start | bytes 8388608
  260.9 16.8 %slice-start.3 = ((s8[16777216]{0:T(1024)(128)(4,1)}), s8[4194304]{0:T(1024)(128)(4,1)S(1)}, s32[]{:S(2)}) async-start(s8[16777216]{0:T(1024)(128)(4,1)} %bitcast.215), calls=%async_computation.15 | async-start | bytes 8388608
  300.8 16.6 %slice-start.4 = ((s8[16777216]{0:T(1024)(128)(4,1)}), s8[4194304]{0:T(1024)(128)(4,1)S(1)}, s32[]{:S(2)}) async-start(s8[16777216]{0:T(1024)(128)(4,1)} %bitcast.217), calls=%async_computation.16 | async-start | bytes 8388608
  300.8 16.6 %slice-start.5 = ((s8[16777216]{0:T(1024)(128)(4,1)}), s8[4194304]{0:T(1024)(128)(4,1)S(1)}, s32[]{:S(2)}) async-start(s8[16777216]{0:T(1024)(128)(4,1)} %bitcast.217), calls=%async_computation.17 | async-start | bytes 8388608
  300.8 16.6 %slice-start.6 = ((s8[16777216]{0:T(1024)(128)(4,1)}), s8[4194304]{0:T(1024)(128)(4,1)S(1)}, s32[]{:S(2)}) async-start(s8[16777216]{0:T(1024)(128)(4,1)} %bitcast.217), calls=%async_computation.18 | async-start | bytes 8388608
  300.8 16.6 %slice-start.7 = ((s8[16777216]{0:T(1024)(128)(4,1)}), s8[4194304]{0:T(1024)(128)(4,1)S(1)}, s32[]{:S(2)}) async-start(s8[16777216]{0:T(1024)(128)(4,1)} %bitcast.217), calls=%async_computation.19 | async-start | bytes 8388608
  341.3 176.9 %reduce-scatter.5.cloned.1.call-start = ((), (), s32[]{:S(2)}) async-start(), calls=%async_computation.8 | async-start | bytes 7864320 | tf_op jit(solution)/shard_map/reduce_scatter | solution.py:319
  351.0 19.5 %copy-start.46 = (bf16[16,64,512]{2,1,0:T(8,128)(2,1)}, bf16[16,64,512]{2,1,0:T(8,128)(2,1)S(1)}, u32[]{:S(2)}) copy-start(bf16[16,64,512]{2,1,0:T(8,128)(2,1)S(1)} %get-tuple-element.204) | copy-start | bytes 3145732
  382.3 135.9 %reduce-scatter.11.cloned.1.call-start = ((), (), s32[]{:S(2)}) async-start(), calls=%async_computation.11 | async-start | bytes 10485760 | tf_op jit(solution)/shard_map/reduce_scatter | solution.py:343
  383.0 16.3 %copy-start.5 = (bf16[2,512,1024]{2,1,0:T(8,128)(2,1)S(1)}, bf16[2,512,1024]{2,1,0:T(8,128)(2,1)}, u32[]{:S(2)}) copy-start(bf16[2,512,1024]{2,1,0:T(8,128)(2,1)} %param.29) | copy-start | bytes 6291460
  414.1 14.1 %copy-start.73 = (f32[512]{0:T(512)S(1)}, f32[512]{0:T(512)}, u32[]{:S(2)}) copy-start(f32[512]{0:T(512)} %copy-done.72) | copy-start | bytes 6148
  414.1 14.0 %copy-start.87 = (f32[512]{0:T(512)S(1)}, f32[512]{0:T(512)}, u32[]{:S(2)}) copy-start(f32[512]{0:T(512)} %copy-done.86) | copy-start | bytes 6148
  414.1 176.0 %reduce-scatter.9.cloned.1.call-start = ((), (), s32[]{:S(2)}) async-start(), calls=%async_computation.10 | async-start | bytes 10485760 | tf_op jit(solution)/shard_map/reduce_scatter | solution.py:337
  443.9 10.9 %copy-start.54 = (f32[16,64]{1,0:T(8,128)S(1)}, f32[16,64]{1,0:T(8,128)}, u32[]{:S(2)}) copy-start(f32[16,64]{1,0:T(8,128)} %get-tuple-element.203) | copy-start | bytes 12292
  443.9 11.0 %copy-start.55 = (f32[16,64]{1,0:T(8,128)S(1)}, f32[16,64]{1,0:T(8,128)}, u32[]{:S(2)}) copy-start(f32[16,64]{1,0:T(8,128)} %get-tuple-element.199) | copy-start | bytes 12292
  443.9 11.1 %copy-start.53 = (f32[16,64]{1,0:T(8,128)S(1)}, f32[16,64]{1,0:T(8,128)}, u32[]{:S(2)}) copy-start(f32[16,64]{1,0:T(8,128)} %get-tuple-element.205) | copy-start | bytes 12292
  487.0 12.2 %copy-start.16 = (f32[512,1024]{1,0:T(8,128)S(1)}, f32[512,1024]{1,0:T(8,128)}, u32[]{:S(2)}) copy-start(f32[512,1024]{1,0:T(8,128)} %copy-done.13) | copy-start | bytes 6291460
  499.2 13.0 %copy-start.10 = (f32[512,1024]{1,0:T(8,128)S(1)}, f32[512,1024]{1,0:T(8,128)}, u32[]{:S(2)}) copy-start(f32[512,1024]{1,0:T(8,128)} %copy-done.9) | copy-start | bytes 6291460
  499.2 13.0 %copy-start.19 = (f32[512,1024]{1,0:T(8,128)S(1)}, f32[512,1024]{1,0:T(8,128)}, u32[]{:S(2)}) copy-start(f32[512,1024]{1,0:T(8,128)} %copy-done.18) | copy-start | bytes 6291460
  499.2 13.0 %copy-start.21 = (f32[512,1024]{1,0:T(8,128)S(1)}, f32[512,1024]{1,0:T(8,128)}, u32[]{:S(2)}) copy-start(f32[512,1024]{1,0:T(8,128)} %copy-done.20) | copy-start | bytes 6291460
  (79 other events, 423.8 us)
Sparse Core Ops, SparseCore 0:
  9.6 49.2 all-gather.11
  60.4 22.5 all-gather.13
  84.6 58.2 all-gather.15
  144.3 58.2 all-gather.17
  341.4 31.4 reduce-scatter.6
  382.4 58.1 reduce-scatter.4
  443.2 72.2 reduce-scatter.10
  518.2 71.7 reduce-scatter.8
where the time goes:
time: 1090 us; the launch traced here: 1080 us
  blocking collectives  542 us (50%)
  matrix products  325 us (30%)
  waiting for transfers between devices  97.6 us (9%)
  other arithmetic  66 us (6%)
  local copies, waits for them, and re-layouts  33.6 us (3%)
  between operations  19.3 us (2%)
    psum x1, blocking collectives, body(): lax.psum((shard_total[0], shard_total[1], shard_total[2], shard_total[3],...  488 us
    dot_general x8, matrix products, contract_rows(): lax.dot_general(left, right, (((0,), (0,)), ((), ())), preferred_element_...  87.5 us
    reduce_scatter x1, waiting for transfers between devices, body(): lax.psum_scatter(full_total[8].astype(jnp.bfloat16), 'shard', scatter_dim...  71.8 us
    dot_general x8, matrix products, contract_cols(): lax.dot_general(left, right, (((1,), (1,)), ((), ())), preferred_element_...  67.7 us
    dot_general x2, matrix products, attend_backward(): jnp.einsum('qhd,khd->hqk', grad_out, value_rows, preferred_element_type=j...  31 us
    dot_general x2, matrix products, forward_pass(): jnp.dot(hidden_activation, w_back, preferred_element_type=jnp.float32)  23.6 us
  transfers between devices with their start and end apart: 8, of which 3 were waited for; matrix products, arithmetic and copies ran while one was open for 25% of the time, Pallas kernels for 0%

commit v1 on v0

v1 whole, which is shorter than its diff:
```python
import functools

import jax
import jax.numpy as jnp
from jax import lax
from jax.experimental import pallas as pl
from jax.experimental.pallas import tpu as pltpu
from jax.sharding import PartitionSpec as P

HEADS = 16
PIECE = 256
HEAD_DIM = 64
PAIR = 2 * HEAD_DIM
SHARDS = 4
CHUNKS = 4
EPS = 1e-05
HIDDEN_PENALTY = 1e33

bf16 = jnp.bfloat16
f32 = jnp.float32

VEC = {
    "ln1_gain": (0, 256),
    "ln1_bias": (256, 256),
    "b_qv": (512, 512),
    "out_bias": (1024, 256),
    "ln2_gain": (1280, 256),
    "ln2_bias": (1536, 256),
    "up_bias": (1792, 1024),
    "down_bias": (2816, 256),
}
VEC_LEN = 3072

any_spec = pl.BlockSpec(memory_space=pltpu.MemorySpace.HBM)


def dot(left, right, left_dim=1, right_dim=0):
    return lax.dot_general(
        left, right, (((left_dim,), (right_dim,)), ((), ())), preferred_element_type=f32
    )


def params(mib):
    return pltpu.CompilerParams(vmem_limit_bytes=int(mib * 2**20))


def cost(flops, moved, transcendentals=0, scale=4):
    return pl.CostEstimate(
        flops=int(scale * flops), bytes_accessed=int(scale * moved), transcendentals=int(scale * transcendentals)
    )


def row_of(vec_ref, name):
    start, size = VEC[name]
    return jnp.concatenate(
        [vec_ref[shard : shard + 1, start : start + size] for shard in range(SHARDS)], axis=1
    )


def whole(shape):
    return pl.BlockSpec(shape, lambda *_: (0,) * len(shape))


def flip(value, axis, size, bit):
    return lax.ppermute(value, axis, [(i, i ^ bit) for i in range(size)])


class Moves:
    def __init__(self, mesh, starts):
        self.reps = mesh.shape["rep"]
        assert mesh.shape["shard"] == SHARDS and self.reps % 4 == 0
        self.shard = lax.axis_index("shard")
        rep = lax.axis_index("rep")
        self.low = rep & 1
        self.mid = (rep >> 1) & 1
        self.index = jnp.concatenate(
            [jnp.stack([self.shard, self.low, self.mid]).astype(jnp.int32), starts]
        )
        self.last = ()

    def wait(self, *values):
        self.index = lax.optimization_barrier((self.index, *values))[0]

    def ran(self, value):
        self.last = (value,)
        return value

    def move(self, value, axis, size, bit):
        return flip(after(value, *self.last), axis, size, bit)

    def core(self, value):
        return self.move(value, "shard", SHARDS, 1)

    def across(self, value):
        return self.move(value, "shard", SHARDS, 2)

    def rep(self, value, bit):
        return self.move(value, "rep", self.reps, bit)

    def half(self, own):
        rows = own.shape[-2] // 2
        return lax.dynamic_slice_in_dim(own, self.low * rows, rows, own.ndim - 2)

    def pick(self, value, which, size):
        return lax.dynamic_slice_in_dim(value, which * size, size, 1)

    def reduce_vec(self, value):
        value = value + self.core(value)
        value = value + self.across(value)
        row = lax.dynamic_slice_in_dim(value, self.shard, 1, 0)
        bit = 1
        while bit < self.reps:
            row = row + self.rep(row, bit)
            bit *= 2
        return row


def after(value, *earlier):
    return lax.optimization_barrier((value, *earlier))[0] if earlier else value


class ShardSum:
    def __init__(self, moves, keep, send):
        self.moves, self.keep = moves, keep
        self.got = moves.core(send)

    def cross(self):
        out = self.keep[1] + self.got[1]
        self.mine = self.keep[0] + self.got[0]
        self.moves.wait(out, self.mine)
        self.got = self.moves.across(out)

    def halves(self):
        moves, mine, got = self.moves, self.mine, self.got
        size = mine.shape[1] // 2
        return [
            moves.pick(mine, which, size) + moves.pick(got, which, size)
            for which in (moves.low, 1 - moves.low)
        ]


class RepSum:
    def __init__(self, moves, sums):
        self.moves = moves
        halves = [s.halves() for s in sums]
        self.mine = jnp.concatenate([h[0] for h in halves])
        self.send(jnp.concatenate([h[1] for h in halves]), 1)
        self.bit = 2

    def send(self, out, bit):
        self.moves.wait(out, self.mine)
        self.got = self.moves.rep(out, bit)

    def split(self):
        moves = self.moves
        size = self.mine.shape[1] // 2
        out, self.mine = [
            moves.pick(self.mine, which, size) + moves.pick(self.got, which, size)
            for which in (1 - moves.mid, moves.mid)
        ]
        self.send(out, 2)

    def add(self):
        self.mine = self.mine + self.got
        self.bit *= 2
        self.got = None
        if self.bit < self.moves.reps:
            self.send(self.mine, self.bit)

    def spread(self):
        while self.got is not None:
            self.add()
        self.send(self.mine, 2)

    def finish(self):
        self.pair = jnp.stack([self.mine, self.got])
        self.send(self.pair, 1)

    def pieces(self):
        self.moves.wait(self.got)
        return (self.pair, self.got)


def piece_copies(index_ref, pieces, target, sems):
    shard, low = index_ref[0], index_ref[1]
    rows = pieces[0].shape[-2]
    if len(pieces) == 4:
        plan = [(piece, shard ^ k, 0, rows) for k, piece in enumerate(pieces)]
    else:
        own, near, far, far_other, far_near, far_other_near = pieces
        half = rows // 2
        plan = (
            (own, shard, 0, rows),
            (near, shard ^ 1, 0, rows),
            (far, shard ^ 2, low * half, half),
            (far_other, shard ^ 2, (1 - low) * half, half),
            (far_near, shard ^ 3, low * half, half),
            (far_other_near, shard ^ 3, (1 - low) * half, half),
        )
    return [
        pltpu.make_async_copy(source, target(to, first, count), sems.at[i])
        for i, (source, to, first, count) in enumerate(plan)
    ]


def norm_parts(value):
    center = value - jnp.mean(value, axis=-1, keepdims=True)
    inverse = lax.rsqrt(jnp.mean(center * center, axis=-1, keepdims=True) + EPS)
    return center * inverse, inverse


def first_norm_body(index_ref, tokens_ref, own_ref, near_ref, far_ref, far_near_ref, normed_ref, vec_ref):
    shard = index_ref[0]

    @pl.when(pl.program_id(0) == 0)
    def _():
        for k, ref in enumerate((own_ref, near_ref, far_ref, far_near_ref)):
            vec_ref[pl.ds(shard ^ k, 1), :] = ref[...].astype(f32)

    hat, _ = norm_parts(tokens_ref[...].astype(f32))
    normed_ref[...] = (hat * row_of(vec_ref, "ln1_gain") + row_of(vec_ref, "ln1_bias")).astype(bf16)


def first_norm(index, tokens, vec_pieces, block=256):
    rows, width = tokens.shape
    row = pl.BlockSpec((block, width), lambda i, idx: (i, 0))
    return pl.pallas_call(
        first_norm_body,
        grid_spec=pltpu.PrefetchScalarGridSpec(
            num_scalar_prefetch=1,
            grid=(rows // block,),
            in_specs=[row] + [whole((1, VEC_LEN))] * 4,
            out_specs=[row, whole((SHARDS, VEC_LEN))],
        ),
        out_shape=[
            jax.ShapeDtypeStruct((rows, width), bf16),
            jax.ShapeDtypeStruct((SHARDS, VEC_LEN), f32),
        ],
        compiler_params=params(16),
        cost_estimate=cost(20 * rows * width, 4 * rows * width),
        name="first_norm",
    )(index, tokens, *vec_pieces)


def joined_body(half, index_ref, *refs):
    pieces, (normed_ref, vec_ref, out_ref, weight_ref, sems) = refs[:-5], refs[-5:]

    @pl.when(pl.program_id(0) == 0)
    def _():
        rows = pieces[0].shape[0]
        copies = piece_copies(
            index_ref,
            pieces,
            lambda to, first, count: weight_ref.at[
                pl.ds(pl.multiple_of(to * rows + first, 128), count), :
            ],
            sems,
        )
        for copy in copies:
            copy.start()
        for copy in copies:
            copy.wait()

    part = weight_ref.shape[1] // 3
    start = VEC["b_qv"][0]
    normed = normed_ref[...]
    for i in range(3):
        cols = slice(i * part, (i + 1) * part)
        value = dot(normed, weight_ref[:, cols])
        if i != 1:
            shard = half if i == 0 else 2 + half
            value = value + vec_ref[shard : shard + 1, start : start + part]
        out_ref[:, cols] = value.astype(bf16)


def joined_product(half, index, pieces, normed, vec, block=256):
    rows, width = normed.shape
    cols = pieces[0].shape[1]
    return pl.pallas_call(
        functools.partial(joined_body, half),
        grid_spec=pltpu.PrefetchScalarGridSpec(
            num_scalar_prefetch=1,
            grid=(rows // block,),
            in_specs=[any_spec] * len(pieces)
            + [pl.BlockSpec((block, width), lambda i, idx: (i, 0)), whole((SHARDS, VEC_LEN))],
            out_specs=[pl.BlockSpec((block, cols), lambda i, idx: (i, 0)), whole((width, cols))],
            scratch_shapes=[pltpu.SemaphoreType.DMA((6,))],
        ),
        out_shape=[
            jax.ShapeDtypeStruct((rows, cols), bf16),
            jax.ShapeDtypeStruct((width, cols), bf16),
        ],
        compiler_params=params(24),
        cost_estimate=cost(2 * rows * width * cols, 2 * (rows * width + rows * cols + 2 * width * cols)),
        name="joined_product",
    )(index, *pieces, normed, vec)


def penalty(start, seq_len):
    key = lax.broadcasted_iota(jnp.int32, (seq_len, seq_len), 0)
    query = lax.broadcasted_iota(jnp.int32, (seq_len, seq_len), 1)
    key_in = (key >= start) & (key < start + PIECE)
    query_in = (query >= start) & (query < start + PIECE)
    seen = (key <= query) | (key_in & query_in)
    return jnp.where(seen, jnp.abs(key - query).astype(f32), HIDDEN_PENALTY)


def slope_of(head):
    return jnp.exp2((jnp.full((1, 1), head, jnp.int32).astype(f32) + 1.0) * (-8.0 / HEADS))


def attend_forward_body(first_head, start_ref, q_ref, k_ref, v_ref, out_ref, total_ref, pen_ref):
    pair = pl.program_id(1)
    seq_len = q_ref.shape[0]

    @pl.when(pair == 0)
    def _():
        pen_ref[...] = penalty(start_ref[3 + pl.program_id(0)], seq_len)

    queries, keys = q_ref[...], k_ref[...]
    values_t = v_ref[...].T
    lane = lax.broadcasted_iota(jnp.int32, (seq_len, PAIR), 1)
    outs = []
    for e in range(2):
        chosen = (lane < HEAD_DIM) if e == 0 else (lane >= HEAD_DIM)
        key_e = jnp.where(chosen, keys * (HEAD_DIM**-0.5), 0).astype(bf16)
        scores = dot(key_e, queries, 1, 1) - slope_of(first_head + 2 * pair + e) * pen_ref[...]
        top = jnp.max(scores, axis=0, keepdims=True)
        weight = jnp.exp(scores - top)
        total = jnp.sum(weight, axis=0, keepdims=True)
        out_t = dot(values_t[e * HEAD_DIM : (e + 1) * HEAD_DIM, :], weight.astype(bf16))
        outs.append(out_t * (1.0 / total))
        total_ref[0, 0, e : e + 1, :] = top + jnp.log(total)
    out_ref[...] = jnp.concatenate(outs, axis=0).T.astype(bf16)


def attend_forward(half, index, joined):
    count = index.shape[0] - 3
    seq_len, width = joined.shape[0] // count, joined.shape[1] // 3
    pairs = width // PAIR

    def cols(first):
        return pl.BlockSpec((seq_len, PAIR), lambda s, h, st: (s, first + h))

    return pl.pallas_call(
        functools.partial(attend_forward_body, half * 2 * pairs),
        grid_spec=pltpu.PrefetchScalarGridSpec(
            num_scalar_prefetch=1,
            grid=(count, pairs),
            in_specs=[cols(0), cols(pairs), cols(2 * pairs)],
            out_specs=[cols(0), pl.BlockSpec((1, 1, 2, seq_len), lambda s, h, st: (s, h, 0, 0))],
            scratch_shapes=[pltpu.VMEM((seq_len, seq_len), f32)],
        ),
        out_shape=[
            jax.ShapeDtypeStruct((count * seq_len, width), bf16),
            jax.ShapeDtypeStruct((count, pairs, 2, seq_len), f32),
        ],
        compiler_params=params(24),
        cost_estimate=cost(
            24 * count * seq_len * seq_len * width, 8 * count * seq_len * width, count * seq_len * seq_len * 2 * pairs
        ),
        name="attend_forward",
    )(index, joined, joined, joined)


def attend_backward_body(
    first_head, start_ref, q_ref, k_ref, v_ref, out_ref, dout_ref, total_ref, dq_ref, dk_ref, dv_ref, pen_ref
):
    pair = pl.program_id(1)
    seq_len = q_ref.shape[0]
    scale = HEAD_DIM**-0.5

    @pl.when(pair == 0)
    def _():
        pen_ref[...] = penalty(start_ref[3 + pl.program_id(0)], seq_len)

    queries, keys, values, d_out = q_ref[...], k_ref[...], v_ref[...], dout_ref[...]
    lane = lax.broadcasted_iota(jnp.int32, (seq_len, PAIR), 1)
    keys_t = keys.T
    both_t = (d_out.astype(f32) * out_ref[...].astype(f32)).T
    d_q, d_k, d_v = [], [], []
    for e in range(2):
        chosen = (lane < HEAD_DIM) if e == 0 else (lane >= HEAD_DIM)
        part = slice(e * HEAD_DIM, (e + 1) * HEAD_DIM)
        key_e = jnp.where(chosen, keys * scale, 0).astype(bf16)
        value_e = jnp.where(chosen, values, 0)
        inner = jnp.sum(both_t[part, :], axis=0, keepdims=True)
        scores = dot(key_e, queries, 1, 1) - slope_of(first_head + 2 * pair + e) * pen_ref[...]
        probs = jnp.exp(scores - total_ref[0, 0, e : e + 1, :])
        d_scores = (probs * (dot(value_e, d_out, 1, 1) - inner)).astype(bf16)
        d_v.append(dot(probs.astype(bf16), d_out))
        d_k.append(dot(d_scores, queries))
        d_q.append(dot(keys_t[part, :], d_scores))
    dq_ref[...] = (jnp.concatenate(d_q, axis=0) * scale).T.astype(bf16)
    dk_ref[...] = (jnp.where(lane < HEAD_DIM, d_k[0], d_k[1]) * scale).astype(bf16)
    dv_ref[...] = jnp.where(lane < HEAD_DIM, d_v[0], d_v[1]).astype(bf16)


def attend_backward(half, index, joined, attended, d_attended, totals):
    count = index.shape[0] - 3
    seq_len, width = joined.shape[0] // count, joined.shape[1] // 3
    pairs = width // PAIR

    def cols(first):
        return pl.BlockSpec((seq_len, PAIR), lambda s, h, st: (s, first + h))

    return pl.pallas_call(
        functools.partial(attend_backward_body, half * 2 * pairs),
        grid_spec=pltpu.PrefetchScalarGridSpec(
            num_scalar_prefetch=1,
            grid=(count, pairs),
            in_specs=[
                cols(0),
                cols(pairs),
                cols(2 * pairs),
                cols(0),
                cols(half * pairs),
                pl.BlockSpec((1, 1, 2, seq_len), lambda s, h, st: (s, h, 0, 0)),
            ],
            out_specs=[cols(0)] * 3,
            scratch_shapes=[pltpu.VMEM((seq_len, seq_len), f32)],
        ),
        out_shape=[jax.ShapeDtypeStruct((count * seq_len, width), bf16)] * 3,
        compiler_params=params(24),
        cost_estimate=cost(
            36 * count * seq_len * seq_len * width, 16 * count * seq_len * width, count * seq_len * seq_len * 2 * pairs
        ),
        name="attend_backward",
    )(index, joined, joined, joined, attended, d_attended, totals)


def middle_body(index_ref, *refs):
    pieces, (a_ref, b_ref, tokens_ref, vec_ref, middle_ref, normed_ref, weight_ref, sems) = refs[:6], refs[6:]

    @pl.when(pl.program_id(0) == 0)
    def _():
        rows = pieces[0].shape[0]
        copies = piece_copies(
            index_ref,
            pieces,
            lambda to, first, count: weight_ref.at[
                pl.ds(pl.multiple_of(to * rows + first, 128), count), :
            ],
            sems,
        )
        for copy in copies:
            copy.start()
        for copy in copies:
            copy.wait()

    part = a_ref.shape[1]
    middle = tokens_ref[...].astype(f32) + row_of(vec_ref, "out_bias")
    middle = middle + dot(a_ref[...], weight_ref[:part, :]) + dot(b_ref[...], weight_ref[part:, :])
    middle_ref[...] = middle
    hat, _ = norm_parts(middle)
    normed_ref[...] = (hat * row_of(vec_ref, "ln2_gain") + row_of(vec_ref, "ln2_bias")).astype(bf16)


def middle_product(index, pieces, attended, tokens, vec, block=256):
    rows, width = tokens.shape
    row = pl.BlockSpec((block, width), lambda i, idx: (i, 0))
    part = pl.BlockSpec((block, attended[0].shape[1]), lambda i, idx: (i, 0))
    return pl.pallas_call(
        middle_body,
        grid_spec=pltpu.PrefetchScalarGridSpec(
            num_scalar_prefetch=1,
            grid=(rows // block,),
            in_specs=[any_spec] * 6 + [part, part, row, whole((SHARDS, VEC_LEN))],
            out_specs=[row, row, whole((width, width))],
            scratch_shapes=[pltpu.SemaphoreType.DMA((6,))],
        ),
        out_shape=[
            jax.ShapeDtypeStruct((rows, width), f32),
            jax.ShapeDtypeStruct((rows, width), bf16),
            jax.ShapeDtypeStruct((width, width), bf16),
        ],
        compiler_params=params(24),
        cost_estimate=cost(2 * rows * width * width, 10 * rows * width + 4 * width * width),
        name="middle_product",
    )(index, *pieces, *attended, tokens, vec)


def gelu_and_slope(pre):
    cube = 0.044715 * pre * pre
    inner = jnp.tanh(0.7978845608028654 * (pre + cube * pre))
    half = 0.5 * (1.0 + inner)
    slope = half + 0.5 * pre * (1.0 - inner * inner) * (0.7978845608028654 * (1.0 + 3.0 * cube))
    return pre * half, slope


def hidden_body(chunk, fresh, index_ref, *refs):
    pieces, refs = refs[:6], refs[6:]
    if not fresh:
        refs = refs[2:]
    normed_hbm, cot_hbm, vec_ref = refs[:3]
    hidden_out, pre_out, keep_ref, send_ref, bias_ref = refs[3:8]
    normed_ref, cot_ref, up_ref, down_ref, hidden_ref, pre_ref, slope_ref, sems, whole_sems = refs[8:]
    step = pl.program_id(0)
    shard = index_ref[0]
    block = 256

    def loads():
        def rows_of(ref, unit):
            rows = pieces[0].shape[1]
            return piece_copies(
                index_ref,
                [piece.at[unit] for piece in pieces],
                lambda to, first, count: ref.at[pl.ds(pl.multiple_of(to * rows + first, 128), count), :],
                sems.at[unit],
            )

        first = [pltpu.make_async_copy(normed_hbm, normed_ref, whole_sems.at[0])] + rows_of(up_ref, 0)
        second = [pltpu.make_async_copy(cot_hbm, cot_ref, whole_sems.at[1])] + rows_of(down_ref, 1)
        return first, second

    def stores():
        cols = pl.ds(chunk * hidden_ref.shape[1], hidden_ref.shape[1])
        return (
            pltpu.make_async_copy(hidden_ref, hidden_out.at[:, cols], whole_sems.at[2]),
            pltpu.make_async_copy(pre_ref, pre_out.at[:, cols], whole_sems.at[3]),
        )

    @pl.when(step == 0)
    def _():
        first, second = loads()
        for copy in first + second:
            copy.start()
        for copy in first:
            copy.wait()

    @pl.when(step == 1)
    def _():
        for copy in loads()[1]:
            copy.wait()

    rows_each = 256
    count = normed_ref.shape[0] // rows_each

    @pl.when(step == 0)
    def _():
        start = VEC["up_bias"][0] + chunk * block
        bias = jnp.concatenate(
            [vec_ref[one : one + 1, start : start + block] for one in range(SHARDS)], axis=1
        )
        for m in range(count):
            rows = slice(m * rows_each, (m + 1) * rows_each)
            value, slope = gelu_and_slope(dot(normed_ref[rows, :], up_ref[...]) + bias)
            value = value.astype(bf16)
            hidden_ref[rows, :] = value
            slope_ref[rows, :] = slope
        stores()[0].start()

    @pl.when(step == 1)
    def _():
        sums = jnp.zeros(bias_ref.shape, f32)
        for m in range(count):
            rows = slice(m * rows_each, (m + 1) * rows_each)
            d_pre = (dot(cot_ref[rows, :], down_ref[...], 1, 1) * slope_ref[rows, :]).astype(bf16)
            pre_ref[rows, :] = d_pre
            sums = sums + jnp.sum(d_pre.astype(f32), axis=0, keepdims=True)
        bias_ref[...] = sums
        stores()[1].start()

    @pl.when(step >= 2)
    def _():
        k = jnp.where(step < 4, 2 * (step - 2) + 1, 2 * (step - 4))
        cols = pl.ds(pl.multiple_of((shard ^ k) * block, block), block)
        left, right = normed_ref[:, cols], hidden_ref[:, cols]
        one = dot(left, pre_ref[...], 0, 0).astype(bf16)
        two = dot(right, cot_ref[...], 0, 0).astype(bf16)

        @pl.when(step < 4)
        def _():
            send_ref[0, 0] = one
            send_ref[0, 1] = two

        @pl.when(step >= 4)
        def _():
            keep_ref[0, 0] = one
            keep_ref[0, 1] = two

    @pl.when(step == 5)
    def _():
        for copy in stores():
            copy.wait()


def hidden_chunk(chunk, index, pieces, carried, normed, cot, vec, hidden_size):
    rows, width = normed.shape
    size = hidden_size // CHUNKS
    fresh = carried is None
    grads = (2, 2, width // SHARDS, size)
    outs = [
        jax.ShapeDtypeStruct((rows, hidden_size), bf16),
        jax.ShapeDtypeStruct((rows, hidden_size), bf16),
        jax.ShapeDtypeStruct(grads, bf16),
        jax.ShapeDtypeStruct(grads, bf16),
        jax.ShapeDtypeStruct((1, size), f32),
    ]
    unit = (1,) + grads[1:]
    return pl.pallas_call(
        functools.partial(hidden_body, chunk, fresh),
        grid_spec=pltpu.PrefetchScalarGridSpec(
            num_scalar_prefetch=1,
            grid=(6,),
            in_specs=[any_spec] * (8 if fresh else 10) + [whole((SHARDS, VEC_LEN))],
            out_specs=[
                any_spec,
                any_spec,
                pl.BlockSpec(unit, lambda i, idx: (jnp.maximum(i - 4, 0), 0, 0, 0)),
                pl.BlockSpec(unit, lambda i, idx: (jnp.clip(i - 2, 0, 1), 0, 0, 0)),
                pl.BlockSpec((1, size), lambda i, idx: (0, 0)),
            ],
            scratch_shapes=[
                pltpu.VMEM((rows, width), bf16),
                pltpu.VMEM((rows, width), bf16),
                pltpu.VMEM((width, size), bf16),
                pltpu.VMEM((size, width), bf16),
                pltpu.VMEM((rows, size), bf16),
                pltpu.VMEM((rows, size), bf16),
                pltpu.VMEM((rows, size), f32),
                pltpu.SemaphoreType.DMA((2, 6)),
                pltpu.SemaphoreType.DMA((4,)),
            ],
        ),
        out_shape=outs,
        input_output_aliases={} if fresh else {7: 0, 8: 1},
        compiler_params=params(48),
        cost_estimate=cost(8 * rows * width * size, 8 * rows * width + 16 * rows * size, rows * size),
        name=f"hidden_chunk{chunk}",
    )(index, *pieces, *(carried or ()), normed, cot, vec)


def norm_back(d_normed, hat, inverse, gain):
    scaled = d_normed * gain
    return inverse * (
        scaled
        - jnp.mean(scaled, axis=-1, keepdims=True)
        - hat * jnp.mean(scaled * hat, axis=-1, keepdims=True)
    )


def column_sum(value):
    return jnp.sum(value, axis=0, keepdims=True)


def chunk_loads(index_ref, pieces, unit, target, sems):
    loads = []
    for chunk in range(CHUNKS):
        group = pieces[6 * chunk : 6 * chunk + 6]
        rows = group[0].shape[1]
        loads.append(
            piece_copies(
                index_ref,
                [piece.at[unit] for piece in group],
                lambda to, first, count, chunk=chunk: target(
                    chunk, pl.multiple_of(to * rows + first, 128), count
                ),
                sems.at[chunk],
            )
        )
    return loads


def block_back_body(index_ref, *refs, blocks):
    pieces, refs = refs[: 6 * CHUNKS], refs[6 * CHUNKS :]
    pre_ref, middle_ref, cot_ref, a_ref, b_ref, weight_ref, vec_ref = refs[:7]
    d_middle_ref, d_attended_ref, keep_ref, send_ref, sums_ref = refs[7:12]
    up_ref, d_one_ref, sems = refs[12:]
    step = pl.program_id(0)
    rows = pre_ref.shape[0]
    size = up_ref.shape[1] // CHUNKS

    def rest(d_normed):
        middle = middle_ref[...]
        cot = cot_ref[...].astype(f32)
        hat, inverse = norm_parts(middle)
        d_middle = cot + norm_back(d_normed, hat, inverse, row_of(vec_ref, "ln2_gain"))
        d_one = d_middle.astype(bf16)
        d_middle_ref[...] = d_middle
        d_one_ref[pl.ds(pl.multiple_of(step * rows, rows), rows), :] = d_one
        sums_ref[0:1, :] += column_sum(d_normed * hat)
        sums_ref[1:2, :] += column_sum(d_normed)
        sums_ref[2:3, :] += column_sum(d_one.astype(f32))
        sums_ref[3:4, :] += column_sum(cot)

    @pl.when(step == 0)
    def _():
        loads = chunk_loads(
            index_ref,
            pieces,
            0,
            lambda chunk, first, count: up_ref.at[pl.ds(first, count), chunk * size : (chunk + 1) * size],
            sems,
        )
        for group in loads:
            for copy in group:
                copy.start()
        sums_ref[...] = jnp.zeros_like(sums_ref)
        d_normed = None
        for chunk, group in enumerate(loads):
            for copy in group:
                copy.wait()
            cols = slice(chunk * size, (chunk + 1) * size)
            term = dot(pre_ref[:, cols], up_ref[:, cols], 1, 1)
            d_normed = term if d_normed is None else d_normed + term
        rest(d_normed)

    @pl.when((step > 0) & (step < blocks))
    def _():
        rest(dot(pre_ref[...], up_ref[...], 1, 1))

    for t, k in enumerate((1, 3, 0, 2)):

        @pl.when(step == blocks + t)
        def _(t=t, k=k):
            block = weight_ref.shape[0] // SHARDS
            part = keep_ref.shape[3]
            d_one = d_one_ref[...]
            d_attended_ref[...] = dot(d_one, weight_ref[t * block : (t + 1) * block, :], 1, 1).astype(bf16)
            shard = index_ref[0] ^ k
            target = send_ref if t < 2 else keep_ref
            cols = pl.ds(pl.multiple_of((shard & 1) * block, block), block)

            def put(ref):
                value = dot(ref[:, cols], d_one, 0, 0).astype(bf16)
                for unit in range(2):
                    target[0, unit] = value[:, unit * part : (unit + 1) * part]

            pl.when(shard < 2)(lambda: put(a_ref))
            pl.when(shard >= 2)(lambda: put(b_ref))


def block_back(index, pieces, d_pre, middle, cot, attended, weight, vec, rows_each=256):
    rows, width = middle.shape
    size = d_pre.shape[1]
    blocks = rows // rows_each
    quarter = width // SHARDS

    def by_rows(cols):
        return pl.BlockSpec((rows_each, cols), lambda i, idx: (jnp.minimum(i, blocks - 1), 0))

    grads = (2, 2, quarter, width // 2)
    unit = (1,) + grads[1:]
    half = whole((rows, attended[0].shape[1]))
    return pl.pallas_call(
        functools.partial(block_back_body, blocks=blocks),
        grid_spec=pltpu.PrefetchScalarGridSpec(
            num_scalar_prefetch=1,
            grid=(blocks + SHARDS,),
            in_specs=[any_spec] * (6 * CHUNKS)
            + [
                by_rows(size),
                by_rows(width),
                by_rows(width),
                half,
                half,
                whole((width, width)),
                whole((SHARDS, VEC_LEN)),
            ],
            out_specs=[
                by_rows(width),
                pl.BlockSpec((rows, quarter), lambda i, idx: (0, jnp.maximum(i - blocks, 0))),
                pl.BlockSpec(unit, lambda i, idx: (jnp.maximum(i - blocks - 2, 0), 0, 0, 0)),
                pl.BlockSpec(unit, lambda i, idx: (jnp.clip(i - blocks, 0, 1), 0, 0, 0)),
                whole((8, width)),
            ],
            scratch_shapes=[
                pltpu.VMEM((width, size), bf16),
                pltpu.VMEM((rows, width), bf16),
                pltpu.SemaphoreType.DMA((CHUNKS, 6)),
            ],
        ),
        out_shape=[
            jax.ShapeDtypeStruct((rows, width), f32),
            jax.ShapeDtypeStruct((rows, width), bf16),
            jax.ShapeDtypeStruct(grads, bf16),
            jax.ShapeDtypeStruct(grads, bf16),
            jax.ShapeDtypeStruct((8, width), f32),
        ],
        compiler_params=params(48),
        cost_estimate=cost(2 * rows * width * (size + 2 * width), 2 * rows * size + 2 * width * size + 16 * rows * width),
        name="block_back",
    )(index, *pieces, d_pre, middle, cot, *attended, weight, vec)


def block_out_body(index_ref, *refs):
    pieces, (hidden_ref, middle_ref, vec_ref, out_ref, down_ref, sems) = refs[: 6 * CHUNKS], refs[6 * CHUNKS :]
    step = pl.program_id(0)
    size = down_ref.shape[0] // CHUNKS

    def rest(value):
        out_ref[...] = (middle_ref[...] + row_of(vec_ref, "down_bias") + value).astype(bf16)

    @pl.when(step == 0)
    def _():
        loads = chunk_loads(
            index_ref,
            pieces,
            1,
            lambda chunk, first, count: down_ref.at[pl.ds(chunk * size + first, count), :],
            sems,
        )
        for group in loads:
            for copy in group:
                copy.start()
        total = None
        for chunk, group in enumerate(loads):
            for copy in group:
                copy.wait()
            cols = slice(chunk * size, (chunk + 1) * size)
            term = dot(hidden_ref[:, cols], down_ref[cols, :])
            total = term if total is None else total + term
        rest(total)

    @pl.when(step > 0)
    def _():
        rest(dot(hidden_ref[...], down_ref[...]))


def block_output(index, pieces, hidden, middle, vec, rows_each=256):
    rows, width = middle.shape
    size = hidden.shape[1]

    def by_rows(cols):
        return pl.BlockSpec((rows_each, cols), lambda i, idx: (i, 0))

    return pl.pallas_call(
        block_out_body,
        grid_spec=pltpu.PrefetchScalarGridSpec(
            num_scalar_prefetch=1,
            grid=(rows // rows_each,),
            in_specs=[any_spec] * (6 * CHUNKS) + [by_rows(size), by_rows(width), whole((SHARDS, VEC_LEN))],
            out_specs=by_rows(width),
            scratch_shapes=[pltpu.VMEM((size, width), bf16), pltpu.SemaphoreType.DMA((CHUNKS, 6))],
        ),
        out_shape=jax.ShapeDtypeStruct((rows, width), bf16),
        compiler_params=params(48),
        cost_estimate=cost(2 * rows * width * size, 2 * rows * size + 2 * width * size + 6 * rows * width),
        name="block_output",
    )(index, *pieces, hidden, middle, vec)


def joined_grad_body(index_ref, normed_ref, dq_ref, dk_ref, dv_ref, keep_ref, send_ref, sums_ref):
    step = pl.program_id(0)
    part = dq_ref.shape[1]

    @pl.when(step == 0)
    def _():
        sums_ref[0:1, :] = column_sum(dq_ref[...].astype(f32))
        sums_ref[1:2, :] = column_sum(dv_ref[...].astype(f32))

    for t, k in enumerate((1, 3, 0, 2)):

        @pl.when(step == t)
        def _(t=t, k=k):
            block = keep_ref.shape[2]
            cols = pl.ds(pl.multiple_of((index_ref[0] ^ k) * block, block), block)
            left = normed_ref[:, cols]
            target = send_ref if t < 2 else keep_ref
            for i, ref in enumerate((dq_ref, dk_ref, dv_ref)):
                target[0, i] = dot(left, ref[...], 0, 0).astype(bf16)


def joined_grad(index, normed, d_q, d_k, d_v):
    rows, width = normed.shape
    part = d_q.shape[1]
    grads = (2, 3, width // SHARDS, part)
    unit = (1,) + grads[1:]
    return pl.pallas_call(
        joined_grad_body,
        grid_spec=pltpu.PrefetchScalarGridSpec(
            num_scalar_prefetch=1,
            grid=(SHARDS,),
            in_specs=[whole((rows, width))] + [whole((rows, part))] * 3,
            out_specs=[
                pl.BlockSpec(unit, lambda i, idx: (jnp.maximum(i - 2, 0), 0, 0, 0)),
                pl.BlockSpec(unit, lambda i, idx: (jnp.minimum(i, 1), 0, 0, 0)),
                whole((2, part)),
            ],
        ),
        out_shape=[
            jax.ShapeDtypeStruct(grads, bf16),
            jax.ShapeDtypeStruct(grads, bf16),
            jax.ShapeDtypeStruct((2, part), f32),
        ],
        compiler_params=params(32),
        cost_estimate=cost(6 * rows * width * part, 2 * rows * width + 6 * rows * part + 6 * width * part),
        name="joined_grad",
    )(index, normed, d_q, d_k, d_v)


def input_grad_body(index_ref, *refs, blocks):
    parts, weights = refs[:6], refs[6:8]
    tokens_ref, d_middle_ref, vec_ref, sums_ref, bqv_a_ref, bqv_b_ref = refs[8:14]
    bias_refs = refs[14 : 14 + CHUNKS]
    out_ref, grads_ref, gain_ref, shift_ref = refs[14 + CHUNKS :]
    step = pl.program_id(0)

    @pl.when(step == 0)
    def _():
        gain_ref[...] = jnp.zeros_like(gain_ref)
        shift_ref[...] = jnp.zeros_like(shift_ref)

    d_normed = None
    for half in range(2):
        for i in range(3):
            ref = parts[3 * half + i]
            part = ref.shape[1]
            term = dot(ref[...], weights[half][:, i * part : (i + 1) * part], 1, 1)
            d_normed = term if d_normed is None else d_normed + term
    hat, inverse = norm_parts(tokens_ref[...].astype(f32))
    out_ref[...] = d_middle_ref[...] + norm_back(d_normed, hat, inverse, row_of(vec_ref, "ln1_gain"))
    gain_ref[...] += column_sum(d_normed * hat)
    shift_ref[...] += column_sum(d_normed)

    @pl.when(step == blocks - 1)
    def _():
        def put(name, shard, value, offset=0):
            first = VEC[name][0] + offset
            grads_ref[shard : shard + 1, first : first + value.shape[1]] = value

        for shard in range(SHARDS):
            cols = slice(shard * 256, (shard + 1) * 256)
            put("ln1_gain", shard, gain_ref[:, cols])
            put("ln1_bias", shard, shift_ref[:, cols])
            put("ln2_gain", shard, sums_ref[0:1, cols])
            put("ln2_bias", shard, sums_ref[1:2, cols])
            put("out_bias", shard, sums_ref[2:3, cols])
            put("down_bias", shard, sums_ref[3:4, cols])
            source = bqv_a_ref if shard % 2 == 0 else bqv_b_ref
            put("b_qv", shard, source[shard // 2 : shard // 2 + 1, :])
            for chunk in range(CHUNKS):
                size = bias_refs[chunk].shape[1] // SHARDS
                put("up_bias", shard, bias_refs[chunk][:, shard * size : (shard + 1) * size], chunk * size)


def input_gradient(index, parts, weights, tokens, d_middle, vec, sums, bqv, biases, rows_each=256):
    rows, width = tokens.shape
    part = parts[0].shape[1]
    blocks = rows // rows_each

    def by_rows(cols):
        return pl.BlockSpec((rows_each, cols), lambda i, idx: (i, 0))

    return pl.pallas_call(
        functools.partial(input_grad_body, blocks=blocks),
        grid_spec=pltpu.PrefetchScalarGridSpec(
            num_scalar_prefetch=1,
            grid=(blocks,),
            in_specs=[by_rows(part)] * 6
            + [whole((width, 3 * part))] * 2
            + [by_rows(width), by_rows(width), whole((SHARDS, VEC_LEN)), whole((8, width))]
            + [whole((2, part))] * 2
            + [whole(bias.shape) for bias in biases],
            out_specs=[by_rows(width), whole((SHARDS, VEC_LEN))],
            scratch_shapes=[pltpu.VMEM((1, width), f32), pltpu.VMEM((1, width), f32)],
        ),
        out_shape=[
            jax.ShapeDtypeStruct((rows, width), f32),
            jax.ShapeDtypeStruct((SHARDS, VEC_LEN), f32),
        ],
        compiler_params=params(40),
        cost_estimate=cost(12 * rows * width * part, 10 * rows * width + 12 * rows * part + 12 * width * part),
        name="input_gradient",
    )(index, *parts, *weights, tokens, d_middle, vec, sums, *bqv, *biases)


def place_body(index_ref, pair_ref, other_ref, *refs, plan, fresh):
    outs = len(refs) - 2 if fresh else (len(refs) - 2) // 2
    out_refs = refs[-2 - outs : -2]
    scratch, sems = refs[-2:]
    low, mid = index_ref[1], index_ref[2]
    rows = pair_ref.shape[2]
    for a, ref in enumerate((pair_ref, other_ref)):
        for b in range(2):
            first = pl.multiple_of((low ^ a) * (2 * rows) + (mid ^ b) * rows, rows)
            for u in range(pair_ref.shape[1]):
                scratch[u, pl.ds(first, rows), :] = ref[b, u].astype(f32)
    copies = []
    for i, (unit, cols, width, out, row, col) in enumerate(plan):
        copies.append(
            pltpu.make_async_copy(
                scratch.at[unit, :, cols : cols + width],
                out_refs[out].at[row : row + 4 * rows, col : col + width],
                sems.at[i],
            )
        )
    for copy in copies:
        copy.start()
    for copy in copies:
        copy.wait()


def place(index, pieces, plan, shapes, carried, name):
    pair, other = pieces
    _, units, rows, width = pair.shape
    fresh = carried is None
    count = len(shapes)
    return pl.pallas_call(
        functools.partial(place_body, plan=plan, fresh=fresh),
        grid_spec=pltpu.PrefetchScalarGridSpec(
            num_scalar_prefetch=1,
            grid=(1,),
            in_specs=[whole(pair.shape), whole(other.shape)] + ([] if fresh else [any_spec] * count),
            out_specs=[any_spec] * count,
            scratch_shapes=[pltpu.VMEM((units, 4 * rows, width), f32), pltpu.SemaphoreType.DMA((len(plan),))],
        ),
        out_shape=[jax.ShapeDtypeStruct(shape, f32) for shape in shapes],
        input_output_aliases={} if fresh else {3 + i: i for i in range(count)},
        compiler_params=params(16),
        cost_estimate=cost(units * 4 * rows * width, units * 4 * rows * width * 6),
        name=name,
    )(index, pair, other, *(carried or ()))


def body(
    mesh,
    tokens,
    piece_start,
    ln1_gain,
    ln1_bias,
    query_key_value_weight,
    b_qv,
    attention_out_weight,
    attention_out_bias,
    ln2_gain,
    ln2_bias,
    up_weight,
    up_bias,
    down_weight,
    down_bias,
    cotangent,
):
    count, seq_len, width = tokens.shape
    rows = count * seq_len
    hidden_size = up_weight.shape[1]
    tokens = tokens.reshape(rows, width)
    cot = cotangent.reshape(rows, width)
    moves = Moves(mesh, piece_start)
    half = width // 2
    size = hidden_size // CHUNKS
    block = size // SHARDS

    own_vec = jnp.concatenate(
        [ln1_gain, ln1_bias, b_qv, attention_out_bias, ln2_gain, ln2_bias, up_bias, down_bias]
    ).reshape(1, VEC_LEN)

    def joined_cols(which):
        return jnp.concatenate(
            [
                query_key_value_weight[:, i * width + which * half : i * width + (which + 1) * half]
                for i in range(3)
            ],
            axis=1,
        )

    def hidden_own(chunk):
        up = jnp.concatenate(
            [
                up_weight[:, s * size + chunk * block : s * size + (chunk + 1) * block]
                for s in range(SHARDS)
            ],
            axis=1,
        )
        return jnp.stack([up, down_weight[chunk * block : (chunk + 1) * block, :]])

    far_vec = moves.across(own_vec)
    near_vec = moves.core(own_vec)
    own_a = joined_cols(0)
    far_a = moves.across(after(own_a, far_vec))
    near_a = moves.core(own_a)
    own_b = joined_cols(1)
    half_b = moves.half(own_b)
    hidden_owns = [hidden_own(chunk) for chunk in range(CHUNKS)]
    hidden_halves = [moves.half(own) for own in hidden_owns]
    out_half = moves.half(attention_out_weight)
    far_near_vec = moves.core(far_vec)
    moves.wait(half_b, out_half, *hidden_halves)
    normed, vec = first_norm(moves.index, tokens, (own_vec, near_vec, far_vec, far_near_vec))
    moves.ran(vec)

    joined, joined_weight, attended, totals = [None] * 2, [None] * 2, [None] * 2, [None] * 2
    hidden_far, hidden_near, hidden_other = [None] * CHUNKS, [None] * CHUNKS, [None] * CHUNKS
    hidden_pieces = [None] * CHUNKS

    def fetch(chunk, earlier):
        hidden_far[chunk] = moves.across(after(hidden_halves[chunk], earlier))
        hidden_near[chunk] = moves.core(after(hidden_owns[chunk], earlier))

    def relay(chunk):
        hidden_other[chunk] = moves.rep(hidden_far[chunk], 1)

    far_b = moves.across(after(half_b, far_a))
    near_b = moves.core(after(own_b, far_a))
    joined[0], joined_weight[0] = joined_product(
        0, moves.index, (own_a, near_a, far_a, moves.core(far_a)), normed, vec
    )
    moves.ran(joined[0])
    moves.wait(far_b, near_b)
    other_b = moves.rep(far_b, 1)
    fetch(0, far_b)
    attended[0], totals[0] = attend_forward(0, moves.index, joined[0])
    moves.ran(totals[0])
    moves.wait(hidden_far[0], hidden_near[0])
    relay(0)
    out_far = moves.across(after(out_half, hidden_far[0]))
    out_near = moves.core(after(attention_out_weight, hidden_far[0]))
    joined[1], joined_weight[1] = joined_product(
        1, moves.index, (own_b, near_b, far_b, other_b, moves.core(far_b), moves.core(other_b)), normed, vec
    )
    moves.ran(joined[1])
    moves.wait(out_far, out_near)
    out_other = moves.rep(out_far, 1)
    fetch(1, out_far)
    attended[1], totals[1] = attend_forward(1, moves.index, joined[1])
    moves.ran(totals[1])
    moves.wait(hidden_far[1], hidden_near[1])
    relay(1)
    fetch(2, hidden_far[1])
    middle, normed_two, out_weight = middle_product(
        moves.index,
        (attention_out_weight, out_near, out_far, out_other, moves.core(out_far), moves.core(out_other)),
        attended,
        tokens,
        vec,
    )
    moves.ran(normed_two)

    carried = None
    shard_sums, up_biases = [], []
    for chunk in range(CHUNKS):
        far, other = hidden_far[chunk], hidden_other[chunk]
        hidden_pieces[chunk] = (
            hidden_owns[chunk],
            hidden_near[chunk],
            far,
            other,
            moves.core(far),
            moves.core(other),
        )
        *carried, keep, send, bias = hidden_chunk(
            chunk, moves.index, hidden_pieces[chunk], carried, normed_two, cot, vec, hidden_size
        )
        moves.ran(bias)
        up_biases.append(bias)
        if chunk + 2 < CHUNKS:
            moves.wait(hidden_far[chunk + 2], hidden_near[chunk + 2])
            relay(chunk + 2)
        if chunk + 3 < CHUNKS:
            fetch(chunk + 3, hidden_far[chunk + 2])
        if chunk > 0:
            shard_sums[chunk - 1].cross()
        shard_sums.append(ShardSum(moves, keep, send))
    all_pieces = [piece for pieces in hidden_pieces for piece in pieces]
    hidden, d_pre = carried
    moves.wait(shard_sums[0].got)
    d_middle, d_attended, keep, send, sums = block_back(
        moves.index, all_pieces, d_pre, middle, cot, attended, out_weight, vec
    )
    moves.ran(sums)
    parts, bqv = [], []

    def backward(which):
        grads = attend_backward(which, moves.index, joined[which], attended[which], d_attended, totals[which])
        parts.extend(grads)
        moves.ran(grads[0])

    def joined_grads(which):
        keep, send, bias = joined_grad(moves.index, normed, *parts[3 * which :])
        bqv.append(bias)
        moves.ran(bias)
        return ShardSum(moves, keep, send)

    shard_sums[3].cross()
    out_sum = ShardSum(moves, keep, send)
    moves.wait(shard_sums[1].got)
    first_sum = RepSum(moves, shard_sums[:2])
    backward(0)
    out_sum.cross()
    a_sum = joined_grads(0)
    first_sum.split()
    moves.wait(shard_sums[2].got)
    second_sum = RepSum(moves, shard_sums[2:3])
    backward(1)
    a_sum.cross()
    first_sum.add()
    b_sum = joined_grads(1)
    moves.wait(shard_sums[3].got)
    third_sum = RepSum(moves, shard_sums[3:4])
    second_sum.split()
    first_sum.spread()
    input_grad, vec_grads = input_gradient(
        moves.index, parts, joined_weight, tokens, d_middle, vec, sums, bqv, up_biases
    )
    moves.ran(vec_grads)
    b_sum.cross()
    first_sum.finish()
    second_sum.add()
    third_sum.split()
    moves.wait(out_sum.got, a_sum.got)
    fourth_sum = RepSum(moves, [out_sum, a_sum])
    block_out = block_output(moves.index, all_pieces, hidden, middle, vec)
    moves.ran(block_out)
    second_sum.spread()
    third_sum.add()
    fourth_sum.split()
    last_sum = RepSum(moves, [b_sum])

    def place_hidden(chunks, pieces, grads, name):
        plan = []
        for i, chunk in enumerate(chunks):
            plan += [(2 * i, s * block, block, 0, 0, s * size + chunk * block) for s in range(SHARDS)]
            plan += [(2 * i + 1, 0, width, 1, chunk * block, 0)]
        shapes = [(width // SHARDS, hidden_size), (size, width)]
        return place(moves.index, pieces, plan, shapes, grads, name)

    grads = place_hidden((0, 1), first_sum.pieces(), None, "place_hidden_first")
    moves.ran(grads[0])
    second_sum.finish()
    third_sum.spread()
    fourth_sum.add()
    last_sum.split()
    vec_sum = moves.reduce_vec(vec_grads).reshape(VEC_LEN)
    grads = place_hidden((2,), second_sum.pieces(), grads, "place_hidden_second")
    moves.ran(grads[0])
    third_sum.finish()
    fourth_sum.spread()
    last_sum.add()
    grad_up, grad_down = place_hidden((3,), third_sum.pieces(), grads, "place_hidden_third")
    moves.ran(grad_up)
    fourth_sum.finish()
    last_sum.spread()
    last_sum.finish()
    third = width // SHARDS
    plan = [(i, 0, half, 0, 0, i * half) for i in range(2)]
    plan += [(2 + i, 0, half, 1, 0, i * width) for i in range(3)]
    shapes = [(third, width), (third, 3 * width)]
    grad_out, grad_joined = place(moves.index, fourth_sum.pieces(), plan, shapes, None, "place_fourth")
    plan = [(i, 0, half, 0, 0, i * width + half) for i in range(3)]
    (grad_joined,) = place(moves.index, last_sum.pieces(), plan, shapes[1:], (grad_joined,), "place_last")

    def vec_part(name):
        first, length = VEC[name]
        return vec_sum[first : first + length]

    return (
        block_out.reshape(count, seq_len, width),
        input_grad.reshape(count, seq_len, width),
        vec_part("ln1_gain"),
        vec_part("ln1_bias"),
        grad_joined,
        vec_part("b_qv"),
        grad_out,
        vec_part("out_bias"),
        vec_part("ln2_gain"),
        vec_part("ln2_bias"),
        grad_up,
        vec_part("up_bias"),
        grad_down,
        vec_part("down_bias"),
    )


def solution(mesh):
    batch = P(("shard", "rep"), None, None)
    vector, matrix = P("shard"), P("shard", None)
    in_specs = (
        batch,
        P(("shard", "rep")),
        vector,
        vector,
        matrix,
        vector,
        matrix,
        vector,
        vector,
        vector,
        matrix,
        vector,
        matrix,
        vector,
        batch,
    )
    out_specs = (
        batch,
        batch,
        vector,
        vector,
        matrix,
        vector,
        matrix,
        vector,
        vector,
        vector,
        matrix,
        vector,
        matrix,
        vector,
    )
    return jax.shard_map(
        functools.partial(body, mesh), mesh=mesh, in_specs=in_specs, out_specs=out_specs, check_vma=False
    )
```

time: 1090 us -> 511 us (0.47)
  blocking collectives: 542 us -> 0 us
  matrix products: 325 us -> 0 us
  Pallas kernels: 0 us -> 219 us
  starting transfers between devices: 1.1 us -> 75.6 us
  waiting for transfers between devices: 97.6 us -> 147 us
  other arithmetic: 66 us -> 29.1 us
  between operations: 19.3 us -> 2.62 us
    psum x1 -> x0, blocking collectives: 488 us -> none  [body(): lax.psum((shard_total[0], shard_total[1], shard_total[2], shard_total[3],...]
    dot_general x36 -> x0, matrix products: 325 us -> none  [the longest x8 87.5 us: contract_rows(): lax.dot_general(left, right, (((0,), (0,)), ((), ())), preferred_element_...]
    pallas_call x0 -> x22, Pallas kernels: none -> 219 us  [the longest x4 68.3 us: hidden_chunk(): pl.pallas_call(functools.partial(hidden_body, chunk, fresh), grid_spec=pl...]
    ppermute x0 -> x80, waiting for transfers between devices: none -> 147 us  [flip(): return lax.ppermute(value, axis, [(i, i ^ bit) for i in range(size)])]
    ppermute x0 -> x80, starting transfers between devices: none -> 75.6 us  [flip(): return lax.ppermute(value, axis, [(i, i ^ bit) for i in range(size)])]
    reduce_scatter x4 -> x0, waiting for transfers between devices: 71.9 us -> none  [the longest x1 71.8 us: body(): lax.psum_scatter(full_total[8].astype(jnp.bfloat16), 'shard', scatter_dim...]
    all_gather x8 -> x0, blocking collectives: 42.2 us -> none  [the longest x1 5.98 us: body(): lax.all_gather(ln2_bias, 'shard', axis=0, tiled=True)]
    convert_element_type x27 -> x0, other arithmetic: 29.2 us -> none  [the longest x2 21.1 us: attend_backward(): grad_scores = (probs * (grad_probs - inner_sum)).astype(jnp.bfloat16)]
  transfers between devices with their start and end apart: 8 -> 80, of which waited for: 3 -> 23; matrix products, arithmetic and copies ran while one was open for 25% -> 7% of each run, Pallas kernels for 0% -> 41%
where the time goes in v1:
time: 511 us; the launch traced here: 503 us
  Pallas kernels  219 us (43%)
  waiting for transfers between devices  147 us (29%)
  starting transfers between devices  75.6 us (15%)
  local copies, waits for them, and re-layouts  29.6 us (6%)
  other arithmetic  29.1 us (6%)
    ppermute x80, waiting for transfers between devices, flip(): return lax.ppermute(value, axis, [(i, i ^ bit) for i in range(size)])  147 us
    ppermute x80, starting transfers between devices, flip(): return lax.ppermute(value, axis, [(i, i ^ bit) for i in range(size)])  75.6 us
    pallas_call x4, Pallas kernels, hidden_chunk(): pl.pallas_call(functools.partial(hidden_body, chunk, fresh), grid_spec=pl...  68.3 us
    pallas_call x2, Pallas kernels, attend_backward(): pl.pallas_call(functools.partial(attend_backward_body, half * 2 * pairs),...  31.5 us
    pallas_call x1, Pallas kernels, block_back(): pl.pallas_call(functools.partial(block_back_body, blocks=blocks), grid_sp...  27.3 us
    pallas_call x2, Pallas kernels, attend_forward(): pl.pallas_call(functools.partial(attend_forward_body, half * 2 * pairs),...  24.1 us
    unnamed x233, local copies, waits for them, and re-layouts  20.4 us
    pallas_call x1, Pallas kernels, block_output(): pl.pallas_call(block_out_body, grid_spec=pltpu.PrefetchScalarGridSpec(num...  15.2 us
  transfers between devices with their start and end apart: 80, of which 23 were waited for; matrix products, arithmetic and copies ran while one was open for 7% of the time, Pallas kernels for 41%

profile of v1, /device:TPU:0, one launch (start us, length us, event | category | flops | bytes accessed | tf_op | source)
XLA Modules:
  0.0 502.8 jit_solution(3438091484382558624)
XLA Ops:
  7.4 3.0 collective-permute-start
  10.4 2.2 fusion.28
  13.3 2.7 fusion.27
  24.1 2.2 first_norm.1
  26.3 13.6 %collective-permute-done.1.refs_2_ = bf16[256,1536]{1,0:T(8,128)(2,1)} collective-permute-done((bf16[256,1536]{1,0:T(8,128)(2,1)S(1)}, bf16[256,1536]{1,0:T(8,128)(2,1)}, u32[]{:S(2)}, u32[]{:S(2)}) %collective-permute-start.1) | collective-permute-done | bytes 786464 | tf_op jit(solution)/shard_map/ppermute | solution.py:65
  40.8 10.6 %collective-permute-done.4.refs_2_ = bf16[128,1536]{1,0:T(8,128)(2,1)S(1)} collective-permute-done((bf16[128,1536]{1,0:T(8,128)(2,1)S(1)}, bf16[128,1536]{1,0:T(8,128)(2,1)S(1)}, u32[]{:S(2)}, u32[]{:S(2)}) %collective-permute-start.4) | collective-permute-done | bytes 393248 | tf_op jit(solution)/shard_map/ppermute | solution.py:65
  51.5 6.0 %joined_product.2 = (bf16[1024,1536]{1,0:T(8,128)(2,1)S(1)}, bf16[1024,1536]{1,0:T(8,128)(2,1)S(1)}) custom-call(s32[5]{0:T(128)S(1)} %pad_add_fusion.index_ref.start_ref, bf16[256,1536]{1,0:T(8,128)(2,1)S(1)} %pad_maximum_fusion.9.refs_0_, bf16[256,1536]{1,0:T(8,128)(2,1)} %collective-permute-done.6.refs_1_, ...), custom_call_target="tpu_custom_call" | custom-call | flops 12884901888 | bytes 46137344 | tf_op jit(solution)/shard_map/joined_product/pallas_call | solution.py:279
  59.7 12.0 %attend_forward.2 = (bf16[1024,512]{1,0:T(8,128)(2,1)S(1)}, f32[2,4,2,512]{3,2,1,0:T(2,128)S(1)}) custom-call(s32[5]{0:T(128)S(1)} %pad_add_fusion.index_ref.start_ref, bf16[1024,1536]{1,0:T(8,128)(2,1)S(1)} %get-tuple-element.221.q_ref.k_ref.v_ref, bf16[1024,1536]{1,0:T(8,128)(2,1)S(1)} %get-tuple-element.221.q_ref.k_ref.v_ref, ...), custom_call_target="tpu_custom_call" | custom-call | flops 25769803776 | bytes 16777216 | tf_op jit(solution)/shard_map/attend_forward/pallas_call | solution.py:345
  74.3 6.9 %collective-permute-done.10.refs_2_ = bf16[128,1024]{1,0:T(8,128)(2,1)S(1)} collective-permute-done((bf16[128,1024]{1,0:T(8,128)(2,1)S(1)}, bf16[128,1024]{1,0:T(8,128)(2,1)S(1)}, u32[]{:S(2)}, u32[]{:S(2)}) %collective-permute-start.10) | collective-permute-done | bytes 262176 | tf_op jit(solution)/shard_map/ppermute | solution.py:65
  81.2 5.5 %joined_product.3 = (bf16[1024,1536]{1,0:T(8,128)(2,1)S(1)}, bf16[1024,1536]{1,0:T(8,128)(2,1)S(1)}) custom-call(s32[5]{0:T(128)S(1)} %pad_add_fusion.index_ref.start_ref, bf16[256,1536]{1,0:T(8,128)(2,1)S(1)} %pad_maximum_fusion.8.refs_0_, bf16[256,1536]{1,0:T(8,128)(2,1)S(1)} %collective-permute-done.5.refs_1_, ...), custom_call_target="tpu_custom_call" | custom-call | flops 12884901888 | bytes 46137344 | tf_op jit(solution)/shard_map/joined_product/pallas_call | solution.py:279
  88.8 12.1 %attend_forward.3 = (bf16[1024,512]{1,0:T(8,128)(2,1)S(1)}, f32[2,4,2,512]{3,2,1,0:T(2,128)S(1)}) custom-call(s32[5]{0:T(128)S(1)} %pad_add_fusion.index_ref.start_ref, bf16[1024,1536]{1,0:T(8,128)(2,1)S(1)} %get-tuple-element.236.q_ref.k_ref.v_ref, bf16[1024,1536]{1,0:T(8,128)(2,1)S(1)} %get-tuple-element.236.q_ref.k_ref.v_ref, ...), custom_call_target="tpu_custom_call" | custom-call | flops 25769803776 | bytes 16777216 | tf_op jit(solution)/shard_map/attend_forward/pallas_call | solution.py:345
  103.0 4.8 middle_product.1
  111.2 4.2 collective-permute-done.19.refs_3_
  118.0 17.0 %hidden_chunk0.1 = (bf16[1024,4096]{1,0:T(8,128)(2,1)}, bf16[1024,4096]{1,0:T(8,128)(2,1)}, bf16[2,2,256,1024]{3,2,1,0:T(8,128)(2,1)}, bf16[2,2,256,1024]{3,2,1,0:T(8,128)(2,1)}, f32[1,1024]{1,0:T(1,128)S(1)}) custom-call(s32[5]{0:T(128)S(1)} %pad_add_fusion.index_ref.start_ref, bf16[2,256,1024]{2,1,0:T(8,128)(2,1)S(1)} %pad_maximum_fusion.1.refs_0_, ...), custom_call_target="tpu_custom_call" | custom-call | flops 34359738368 | bytes 100663296 | tf_op jit(solution)/shard_map/hidden_chunk0/pallas_call | solution.py:601
  138.5 17.2 %hidden_chunk1.1 = (bf16[1024,4096]{1,0:T(8,128)(2,1)}, bf16[1024,4096]{1,0:T(8,128)(2,1)}, bf16[2,2,256,1024]{3,2,1,0:T(8,128)(2,1)}, bf16[2,2,256,1024]{3,2,1,0:T(8,128)(2,1)}, f32[1,1024]{1,0:T(1,128)S(1)}) custom-call(s32[5]{0:T(128)S(1)} %pad_add_fusion.index_ref.start_ref, ...), custom_call_target="tpu_custom_call", output_to_operand_aliasing={{0}: (7, {}), {1}: (8, {})} | custom-call | flops 34359738368 | bytes 100663296 | tf_op jit(solution)/shard_map/hidden_chunk1/pallas_call | solution.py:601
  159.6 17.0 %hidden_chunk2.1 = (bf16[1024,4096]{1,0:T(8,128)(2,1)}, bf16[1024,4096]{1,0:T(8,128)(2,1)}, bf16[2,2,256,1024]{3,2,1,0:T(8,128)(2,1)}, bf16[2,2,256,1024]{3,2,1,0:T(8,128)(2,1)}, f32[1,1024]{1,0:T(1,128)S(1)}) custom-call(s32[5]{0:T(128)S(1)} %pad_add_fusion.index_ref.start_ref, ...), custom_call_target="tpu_custom_call", output_to_operand_aliasing={{0}: (7, {}), {1}: (8, {})} | custom-call | flops 34359738368 | bytes 100663296 | tf_op jit(solution)/shard_map/hidden_chunk2/pallas_call | solution.py:601
  178.0 2.5 slice_add_fusion.2
  181.9 17.1 %hidden_chunk3.1 = (bf16[1024,4096]{1,0:T(8,128)(2,1)}, bf16[1024,4096]{1,0:T(8,128)(2,1)}, bf16[2,2,256,1024]{3,2,1,0:T(8,128)(2,1)}, bf16[2,2,256,1024]{3,2,1,0:T(8,128)(2,1)}, f32[1,1024]{1,0:T(1,128)S(1)}) custom-call(s32[5]{0:T(128)S(1)} %pad_add_fusion.index_ref.start_ref, ...), custom_call_target="tpu_custom_call", output_to_operand_aliasing={{0}: (7, {}), {1}: (8, {})} | custom-call | flops 34359738368 | bytes 100663296 | tf_op jit(solution)/shard_map/hidden_chunk3/pallas_call | solution.py:601
  199.1 4.4 collective-permute-done.36
  203.9 21.5 %collective-permute-done.41 = bf16[2,256,1024]{2,1,0:T(8,128)(2,1)S(1)} collective-permute-done((bf16[2,256,1024]{2,1,0:T(8,128)(2,1)S(1)}, bf16[2,256,1024]{2,1,0:T(8,128)(2,1)S(1)}, u32[]{:S(2)}, u32[]{:S(2)}) %collective-permute-start.41) | collective-permute-done | bytes 1048608 | tf_op jit(solution)/shard_map/ppermute | solution.py:65
  230.7 27.3 %block_back.1 = (f32[1024,1024]{1,0:T(8,128)}, bf16[1024,1024]{1,0:T(8,128)(2,1)}, bf16[2,2,256,512]{3,2,1,0:T(8,128)(2,1)}, bf16[2,2,256,512]{3,2,1,0:T(8,128)(2,1)}, f32[8,1024]{1,0:T(8,128)S(1)}) custom-call(s32[5]{0:T(128)S(1)} %pad_add_fusion.index_ref.start_ref, bf16[2,256,1024]{2,1,0:T(8,128)(2,1)} %copy-done.2, bf16[2,256,1024]{2,1,0:T(8,128)(2,1)} %copy-done.10, ...), custom_call_target="tpu_custom_call" | custom-call | flops 51539607552 | bytes 134217728 | tf_op jit(solution)/shard_map/block_back/pallas_call | solution.py:746
  263.5 15.8 %attend_backward.2 = (bf16[1024,512]{1,0:T(8,128)(2,1)S(1)}, bf16[1024,512]{1,0:T(8,128)(2,1)S(1)}, bf16[1024,512]{1,0:T(8,128)(2,1)S(1)}) custom-call(s32[5]{0:T(128)S(1)} %pad_add_fusion.index_ref.start_ref, bf16[1024,1536]{1,0:T(8,128)(2,1)S(1)} %copy-done.59, bf16[1024,1536]{1,0:T(8,128)(2,1)S(1)} %copy-done.59, bf16[1024,1536]{1,0:T(8,128)(2,1)S(1)} %copy-done.59, ...), custom_call_target="tpu_custom_call" | custom-call | flops 38654705664 | bytes 33554432 | tf_op jit(solution)/shard_map/attend_backward/pallas_call | solution.py:407
  282.4 4.8 joined_grad.2
  295.1 7.4 %collective-permute-done.46 = bf16[4,64,1024]{2,1,0:T(8,128)(2,1)} collective-permute-done((bf16[4,64,1024]{2,1,0:T(8,128)(2,1)}, bf16[4,64,1024]{2,1,0:T(8,128)(2,1)}, u32[]{:S(2)}, u32[]{:S(2)}) %collective-permute-start.46) | collective-permute-done | bytes 524320 | tf_op jit(solution)/shard_map/ppermute | solution.py:65
  305.5 15.8 %attend_backward.3 = (bf16[1024,512]{1,0:T(8,128)(2,1)S(1)}, bf16[1024,512]{1,0:T(8,128)(2,1)S(1)}, bf16[1024,512]{1,0:T(8,128)(2,1)S(1)}) custom-call(s32[5]{0:T(128)S(1)} %pad_add_fusion.index_ref.start_ref, bf16[1024,1536]{1,0:T(8,128)(2,1)S(1)} %copy-done.57, bf16[1024,1536]{1,0:T(8,128)(2,1)S(1)} %copy-done.57, bf16[1024,1536]{1,0:T(8,128)(2,1)S(1)} %copy-done.57, ...), custom_call_target="tpu_custom_call" | custom-call | flops 38654705664 | bytes 33554432 | tf_op jit(solution)/shard_map/attend_backward/pallas_call | solution.py:407
  321.3 2.7 collective-permute-start.49
  325.7 5.1 %joined_grad.3 = (bf16[2,3,256,512]{3,2,1,0:T(8,128)(2,1)S(1)}, bf16[2,3,256,512]{3,2,1,0:T(8,128)(2,1)S(1)}, f32[2,512]{1,0:T(2,128)S(1)}) custom-call(s32[5]{0:T(128)S(1)} %pad_add_fusion.index_ref.start_ref, bf16[1024,1024]{1,0:T(8,128)(2,1)S(1)} %copy-done.9, bf16[1024,512]{1,0:T(8,128)(2,1)S(1)} %get-tuple-element.330.dq_ref.refs_3_, ...), custom_call_target="tpu_custom_call" | custom-call | flops 12884901888 | bytes 33554432 | tf_op jit(solution)/shard_map/joined_grad/pallas_call | solution.py:870
  333.0 13.4 %collective-permute-done.49 = bf16[4,64,1024]{2,1,0:T(8,128)(2,1)S(1)} collective-permute-done((bf16[4,64,1024]{2,1,0:T(8,128)(2,1)S(1)}, bf16[4,64,1024]{2,1,0:T(8,128)(2,1)S(1)}, u32[]{:S(2)}, u32[]{:S(2)}) %collective-permute-start.49) | collective-permute-done | bytes 524320 | tf_op jit(solution)/shard_map/ppermute | solution.py:65
  349.9 12.8 %input_gradient.1 = (f32[1024,1024]{1,0:T(8,128)}, f32[4,3072]{1,0:T(4,128)S(1)}) custom-call(s32[5]{0:T(128)S(1)} %pad_add_fusion.index_ref.start_ref, bf16[1024,512]{1,0:T(8,128)(2,1)S(1)} %copy-done.65, bf16[1024,512]{1,0:T(8,128)(2,1)S(1)} %copy-done.67, bf16[1024,512]{1,0:T(8,128)(2,1)S(1)} %copy-done.69, ...), custom_call_target="tpu_custom_call" | custom-call | flops 25769803776 | bytes 92274688 | tf_op jit(solution)/shard_map/input_gradient/pallas_call | solution.py:946
  362.6 5.0 collective-permute-done.55
  371.7 4.5 collective-permute-done.57
  377.0 8.6 %collective-permute-done.58 = bf16[5,128,512]{2,1,0:T(8,128)(2,1)S(1)} collective-permute-done((bf16[5,128,512]{2,1,0:T(8,128)(2,1)S(1)}, bf16[5,128,512]{2,1,0:T(8,128)(2,1)S(1)}, u32[]{:S(2)}, u32[]{:S(2)}) %collective-permute-start.58) | collective-permute-done | bytes 655392 | tf_op jit(solution)/shard_map/ppermute | solution.py:65
  388.9 15.2 %block_output.1 = bf16[1024,1024]{1,0:T(8,128)(2,1)} custom-call(s32[5]{0:T(128)S(1)} %pad_add_fusion.index_ref.start_ref, bf16[2,256,1024]{2,1,0:T(8,128)(2,1)} %copy-done.2, bf16[2,256,1024]{2,1,0:T(8,128)(2,1)} %copy-done.10, bf16[2,128,1024]{2,1,0:T(8,128)(2,1)S(1)} %copy-done.17, bf16[2,128,1024]{2,1,0:T(8,128)(2,1)S(1)} %copy-done.23, ...), custom_call_target="tpu_custom_call" | custom-call | flops 34359738368 | bytes 92274688 | tf_op jit(solution)/shard_map/block_output/pallas_call | solution.py:828
  405.6 2.3 collective-permute-start.56
  410.0 5.1 %collective-permute-done.56 = bf16[2,64,1024]{2,1,0:T(8,128)(2,1)S(1)} collective-permute-done((bf16[2,64,1024]{2,1,0:T(8,128)(2,1)S(1)}, bf16[2,64,1024]{2,1,0:T(8,128)(2,1)S(1)}, u32[]{:S(2)}, u32[]{:S(2)}) %collective-permute-start.56) | collective-permute-done | bytes 262176 | tf_op jit(solution)/shard_map/ppermute | solution.py:65
  416.0 6.3 %collective-permute-start.66 = (bf16[2,64,1024]{2,1,0:T(8,128)(2,1)}, bf16[2,64,1024]{2,1,0:T(8,128)(2,1)}, u32[]{:S(2)}, u32[]{:S(2)}) collective-permute-start(bf16[2,64,1024]{2,1,0:T(8,128)(2,1)} %add.297), channel_id=1, source_target_pairs={{0,2},{1,3},{2,0},{3,1},{4,6},{5,7},{6,4},{7,5},{8,10},{9,11},{10,... | collective-permute-start | bytes 786440 | tf_op jit(solution)/shard_map/ppermute | solution.py:65
  423.6 2.9 place_hidden_first.1
  428.7 3.9 collective-permute-done.67
  439.5 2.9 collective-permute-done.63
  450.6 7.3 %collective-permute-done.72 = bf16[5,64,512]{2,1,0:T(8,128)(2,1)S(1)} collective-permute-done((bf16[5,64,512]{2,1,0:T(8,128)(2,1)S(1)}, bf16[5,64,512]{2,1,0:T(8,128)(2,1)S(1)}, u32[]{:S(2)}, u32[]{:S(2)}) %collective-permute-start.72) | collective-permute-done | bytes 327712 | tf_op jit(solution)/shard_map/ppermute | solution.py:65
  458.7 3.4 collective-permute-start.76
  462.1 7.9 %collective-permute-done.76 = bf16[3,64,512]{2,1,0:T(8,128)(2,1)S(1)} collective-permute-done((bf16[3,64,512]{2,1,0:T(8,128)(2,1)S(1)}, bf16[3,64,512]{2,1,0:T(8,128)(2,1)S(1)}, u32[]{:S(2)}, u32[]{:S(2)}) %collective-permute-start.76) | collective-permute-done | bytes 196640 | tf_op jit(solution)/shard_map/ppermute | solution.py:65
  472.2 4.2 collective-permute-start.77
  477.7 3.2 collective-permute-done.77
  482.8 3.9 collective-permute-done.65
  488.5 5.6 %collective-permute-done.78.other_ref = bf16[2,5,64,512]{3,2,1,0:T(8,128)(2,1)S(1)} collective-permute-done((bf16[2,5,64,512]{3,2,1,0:T(8,128)(2,1)S(1)}, bf16[2,5,64,512]{3,2,1,0:T(8,128)(2,1)S(1)}, u32[]{:S(2)}, u32[]{:S(2)}) %collective-permute-start.78) | collective-permute-done | bytes 655392 | tf_op jit(solution)/shard_map/ppermute | solution.py:65
  494.1 2.2 place_fourth.1
  496.4 4.3 collective-permute-done.79.other_ref
  (432 shorter events, 114.0 us)
Async XLA Ops:
  7.4 12.9 %collective-permute-start = (bf16[1,3072]{1,0:T(2,128)(2,1)S(1)}, bf16[1,3072]{1,0:T(2,128)(2,1)S(1)}, u32[]{:S(2)}, u32[]{:S(2)}) collective-permute-start(bf16[1,3072]{1,0:T(2,128)(2,1)S(1)} %reshape.80.own_ref), channel_id=1, source_target_pairs={{0,16},{8,24},{16,0},{24,8},{1,17},{9,25},{17,1},{25,9},{2,18},{10... | collective-permute-start | bytes 18440 | tf_op jit(solution)/shard_map/ppermute | solution.py:65
  12.7 38.8 %collective-permute-start.6 = (bf16[256,1536]{1,0:T(8,128)(2,1)S(1)}, bf16[256,1536]{1,0:T(8,128)(2,1)}, u32[]{:S(2)}, u32[]{:S(2)}) collective-permute-start(bf16[256,1536]{1,0:T(8,128)(2,1)S(1)} %pad_maximum_fusion.9.refs_0_), channel_id=1, source_target_pairs={{0,8},{8,0},{16,24},{24,16},{1,9},{9,1},{17,25},{25,17},{2,10},{10... | collective-permute-start | bytes 2359304 | tf_op jit(solution)/shard_map/ppermute | solution.py:65
  20.3 19.7 %collective-permute-start.1 = (bf16[256,1536]{1,0:T(8,128)(2,1)S(1)}, bf16[256,1536]{1,0:T(8,128)(2,1)}, u32[]{:S(2)}, u32[]{:S(2)}) collective-permute-start(bf16[256,1536]{1,0:T(8,128)(2,1)S(1)} %pad_maximum_fusion.9.refs_0_), channel_id=1, source_target_pairs={{0,16},{8,24},{16,0},{24,8},{1,17},{9,25},{17,1},{25,9},{2,18},{10... | collective-permute-start | bytes 2359304 | tf_op jit(solution)/shard_map/ppermute | solution.py:65
  57.6 14.2 %collective-permute-start.8 = (bf16[2,128,1024]{2,1,0:T(8,128)(2,1)S(1)}, bf16[2,128,1024]{2,1,0:T(8,128)(2,1)S(1)}, u32[]{:S(2)}, u32[]{:S(2)}) collective-permute-start(bf16[2,128,1024]{2,1,0:T(8,128)(2,1)S(1)} %copy-done.105), channel_id=1, source_target_pairs={{0,16},{8,24},{16,0},{24,8},{1,17},{9,25},{17,1},{25,9},{2,18},{10... | collective-permute-start | bytes 1572872 | tf_op jit(solution)/shard_map/ppermute | solution.py:65
  58.0 23.2 %collective-permute-start.9 = (bf16[2,256,1024]{2,1,0:T(8,128)(2,1)S(1)}, bf16[2,256,1024]{2,1,0:T(8,128)(2,1)S(1)}, u32[]{:S(2)}, u32[]{:S(2)}) collective-permute-start(bf16[2,256,1024]{2,1,0:T(8,128)(2,1)S(1)} %pad_maximum_fusion.1.refs_0_), channel_id=1, source_target_pairs={{0,8},{8,0},{16,24},{24,16},{1,9},{9,1},{17,25},{25,17},{2,10},{10... | collective-permute-start | bytes 3145736 | tf_op jit(solution)/shard_map/ppermute | solution.py:65
  58.0 14.5 %collective-permute-start.12 = (bf16[128,1536]{1,0:T(8,128)(2,1)S(1)}, bf16[128,1536]{1,0:T(8,128)(2,1)S(1)}, u32[]{:S(2)}, u32[]{:S(2)}) collective-permute-start(bf16[128,1536]{1,0:T(8,128)(2,1)S(1)} %collective-permute-done.4.refs_2_), channel_id=1, source_target_pairs={{0,1},{1,0},{2,3},{3,2},{4,5},{5,4},{6,7},{7,6},{8,9},{9,8},{10,11... | collective-permute-start | bytes 1179656 | tf_op jit(solution)/shard_map/ppermute | solution.py:65
  86.7 16.3 %collective-permute-start.15 = (bf16[2,128,1024]{2,1,0:T(8,128)(2,1)S(1)}, bf16[2,128,1024]{2,1,0:T(8,128)(2,1)S(1)}, u32[]{:S(2)}, u32[]{:S(2)}) collective-permute-start(bf16[2,128,1024]{2,1,0:T(8,128)(2,1)S(1)} %copy-done.104), channel_id=1, source_target_pairs={{0,16},{8,24},{16,0},{24,8},{1,17},{9,25},{17,1},{25,9},{2,18},{10... | collective-permute-start | bytes 1572872 | tf_op jit(solution)/shard_map/ppermute | solution.py:65
  88.3 14.7 %collective-permute-start.16 = (bf16[2,256,1024]{2,1,0:T(8,128)(2,1)S(1)}, bf16[2,256,1024]{2,1,0:T(8,128)(2,1)S(1)}, u32[]{:S(2)}, u32[]{:S(2)}) collective-permute-start(bf16[2,256,1024]{2,1,0:T(8,128)(2,1)S(1)} %pad_maximum_fusion.2.refs_0_.refs_6_), channel_id=1, source_target_pairs={{0,8},{8,0},{16,24},{24,16},{1,9},{9,1},{17,25},{25,17},{2,10},{10... | collective-permute-start | bytes 3145736 | tf_op jit(solution)/shard_map/ppermute | solution.py:65
  88.3 12.9 %collective-permute-start.20 = (bf16[128,1024]{1,0:T(8,128)(2,1)S(1)}, bf16[128,1024]{1,0:T(8,128)(2,1)S(1)}, u32[]{:S(2)}, u32[]{:S(2)}) collective-permute-start(bf16[128,1024]{1,0:T(8,128)(2,1)S(1)} %collective-permute-done.10.refs_2_), channel_id=1, source_target_pairs={{0,1},{1,0},{2,3},{3,2},{4,5},{5,4},{6,7},{7,6},{8,9},{9,8},{10,11... | collective-permute-start | bytes 786440 | tf_op jit(solution)/shard_map/ppermute | solution.py:65
  101.4 14.0 %collective-permute-start.19 = (bf16[2,128,1024]{2,1,0:T(8,128)(2,1)S(1)}, bf16[2,128,1024]{2,1,0:T(8,128)(2,1)S(1)}, u32[]{:S(2)}, u32[]{:S(2)}) collective-permute-start(bf16[2,128,1024]{2,1,0:T(8,128)(2,1)S(1)} %collective-permute-done.8.refs_2_), channel_id=1, source_target_pairs={{0,1},{1,0},{2,3},{3,2},{4,5},{5,4},{6,7},{7,6},{8,9},{9,8},{10,11... | collective-permute-start | bytes 1572872 | tf_op jit(solution)/shard_map/ppermute | solution.py:65
  115.6 20.2 %collective-permute-start.17 = (bf16[2,128,1024]{2,1,0:T(8,128)(2,1)}, bf16[2,128,1024]{2,1,0:T(8,128)(2,1)S(1)}, u32[]{:S(2)}, u32[]{:S(2)}) collective-permute-start(bf16[2,128,1024]{2,1,0:T(8,128)(2,1)} %get-tuple-element.243), channel_id=1, source_target_pairs={{0,16},{8,24},{16,0},{24,8},{1,17},{9,25},{17,1},{25,9},{2,18},{10... | collective-permute-start | bytes 1572872 | tf_op jit(solution)/shard_map/ppermute | solution.py:65
  116.0 19.8 %collective-permute-start.18 = (bf16[2,256,1024]{2,1,0:T(8,128)(2,1)S(1)}, bf16[2,256,1024]{2,1,0:T(8,128)(2,1)S(1)}, u32[]{:S(2)}, u32[]{:S(2)}) collective-permute-start(bf16[2,256,1024]{2,1,0:T(8,128)(2,1)S(1)} %pad_maximum_fusion.3.refs_0_.refs_12_), channel_id=1, source_target_pairs={{0,8},{8,0},{16,24},{24,16},{1,9},{9,1},{17,25},{25,17},{2,10},{10... | collective-permute-start | bytes 3145736 | tf_op jit(solution)/shard_map/ppermute | solution.py:65
  116.3 18.9 %collective-permute-start.28 = (bf16[2,128,1024]{2,1,0:T(8,128)(2,1)S(1)}, bf16[2,128,1024]{2,1,0:T(8,128)(2,1)S(1)}, u32[]{:S(2)}, u32[]{:S(2)}) collective-permute-start(bf16[2,128,1024]{2,1,0:T(8,128)(2,1)S(1)} %collective-permute-done.15.refs_2_.refs_8_), channel_id=1, source_target_pairs={{0,1},{1,0},{2,3},{3,2},{4,5},{5,4},{6,7},{7,6},{8,9},{9,8},{10,11... | collective-permute-start | bytes 1572872 | tf_op jit(solution)/shard_map/ppermute | solution.py:65
  135.8 20.5 %collective-permute-start.25 = (bf16[2,128,1024]{2,1,0:T(8,128)(2,1)S(1)}, bf16[2,128,1024]{2,1,0:T(8,128)(2,1)}, u32[]{:S(2)}, u32[]{:S(2)}) collective-permute-start(bf16[2,128,1024]{2,1,0:T(8,128)(2,1)S(1)} %get-tuple-element.258), channel_id=1, source_target_pairs={{0,16},{8,24},{16,0},{24,8},{1,17},{9,25},{17,1},{25,9},{2,18},{10... | collective-permute-start | bytes 1572872 | tf_op jit(solution)/shard_map/ppermute | solution.py:65
  137.4 19.0 %collective-permute-start.26 = (bf16[2,256,1024]{2,1,0:T(8,128)(2,1)S(1)}, bf16[2,256,1024]{2,1,0:T(8,128)(2,1)S(1)}, u32[]{:S(2)}, u32[]{:S(2)}) collective-permute-start(bf16[2,256,1024]{2,1,0:T(8,128)(2,1)S(1)} %pad_maximum_fusion.4.refs_0_.refs_18_), channel_id=1, source_target_pairs={{0,8},{8,0},{16,24},{24,16},{1,9},{9,1},{17,25},{25,17},{2,10},{10... | collective-permute-start | bytes 3145736 | tf_op jit(solution)/shard_map/ppermute | solution.py:65
  137.4 20.5 %collective-permute-start.27 = (bf16[2,2,256,1024]{3,2,1,0:T(8,128)(2,1)}, bf16[2,2,256,1024]{3,2,1,0:T(8,128)(2,1)S(1)}, u32[]{:S(2)}, u32[]{:S(2)}) collective-permute-start(bf16[2,2,256,1024]{3,2,1,0:T(8,128)(2,1)} %get-tuple-element.264), channel_id=1, source_target_pairs={{0,8},{8,0},{16,24},{24,16},{1,9},{9,1},{17,25},{25,17},{2,10},{10... | collective-permute-start | bytes 6291464 | tf_op jit(solution)/shard_map/ppermute | solution.py:65
  137.9 17.9 %collective-permute-start.32 = (bf16[2,128,1024]{2,1,0:T(8,128)(2,1)S(1)}, bf16[2,128,1024]{2,1,0:T(8,128)(2,1)S(1)}, u32[]{:S(2)}, u32[]{:S(2)}) collective-permute-start(bf16[2,128,1024]{2,1,0:T(8,128)(2,1)S(1)} %collective-permute-done.17.refs_2_.refs_14_), channel_id=1, source_target_pairs={{0,1},{1,0},{2,3},{3,2},{4,5},{5,4},{6,7},{7,6},{8,9},{9,8},{10,11... | collective-permute-start | bytes 1572872 | tf_op jit(solution)/shard_map/ppermute | solution.py:65
  156.3 21.7 %collective-permute-start.31 = (bf16[2,2,256,1024]{3,2,1,0:T(8,128)(2,1)}, bf16[2,2,256,1024]{3,2,1,0:T(8,128)(2,1)}, u32[]{:S(2)}, u32[]{:S(2)}) collective-permute-start(bf16[2,2,256,1024]{3,2,1,0:T(8,128)(2,1)} %get-tuple-element.274), channel_id=1, source_target_pairs={{0,8},{8,0},{16,24},{24,16},{1,9},{9,1},{17,25},{25,17},{2,10},{10... | collective-permute-start | bytes 6291464 | tf_op jit(solution)/shard_map/ppermute | solution.py:65
  156.4 20.4 %collective-permute-start.37 = (bf16[2,128,1024]{2,1,0:T(8,128)(2,1)}, bf16[2,128,1024]{2,1,0:T(8,128)(2,1)}, u32[]{:S(2)}, u32[]{:S(2)}) collective-permute-start(bf16[2,128,1024]{2,1,0:T(8,128)(2,1)} %collective-permute-done.25.refs_2_.refs_20_), channel_id=1, source_target_pairs={{0,1},{1,0},{2,3},{3,2},{4,5},{5,4},{6,7},{7,6},{8,9},{9,8},{10,11... | collective-permute-start | bytes 1572872 | tf_op jit(solution)/shard_map/ppermute | solution.py:65
  177.1 49.8 %collective-permute-start.35 = (bf16[2,2,256,1024]{3,2,1,0:T(8,128)(2,1)}, bf16[2,2,256,1024]{3,2,1,0:T(8,128)(2,1)S(1)}, u32[]{:S(2)}, u32[]{:S(2)}) collective-permute-start(bf16[2,2,256,1024]{3,2,1,0:T(8,128)(2,1)} %get-tuple-element.284), channel_id=1, source_target_pairs={{0,8},{8,0},{16,24},{24,16},{1,9},{9,1},{17,25},{25,17},{2,10},{10... | collective-permute-start | bytes 6291464 | tf_op jit(solution)/shard_map/ppermute | solution.py:65
  177.3 26.2 %collective-permute-start.36 = (bf16[2,256,1024]{2,1,0:T(8,128)(2,1)}, bf16[2,256,1024]{2,1,0:T(8,128)(2,1)S(1)}, u32[]{:S(2)}, u32[]{:S(2)}) collective-permute-start(bf16[2,256,1024]{2,1,0:T(8,128)(2,1)} %get-tuple-element.286), channel_id=1, source_target_pairs={{0,16},{8,24},{16,0},{24,8},{1,17},{9,25},{17,1},{25,9},{2,18},{10... | collective-permute-start | bytes 3145736 | tf_op jit(solution)/shard_map/ppermute | solution.py:65
  180.4 45.0 %collective-permute-start.41 = (bf16[2,256,1024]{2,1,0:T(8,128)(2,1)S(1)}, bf16[2,256,1024]{2,1,0:T(8,128)(2,1)S(1)}, u32[]{:S(2)}, u32[]{:S(2)}) collective-permute-start(bf16[2,256,1024]{2,1,0:T(8,128)(2,1)S(1)} %get-tuple-element.298), channel_id=1, source_target_pairs={{0,16},{8,24},{16,0},{24,8},{1,17},{9,25},{17,1},{25,9},{2,18},{10... | collective-permute-start | bytes 3145736 | tf_op jit(solution)/shard_map/ppermute | solution.py:65
  199.0 60.9 %collective-permute-start.40 = (bf16[2,2,256,1024]{3,2,1,0:T(8,128)(2,1)}, bf16[2,2,256,1024]{3,2,1,0:T(8,128)(2,1)S(1)}, u32[]{:S(2)}, u32[]{:S(2)}) collective-permute-start(bf16[2,2,256,1024]{3,2,1,0:T(8,128)(2,1)} %get-tuple-element.296), channel_id=1, source_target_pairs={{0,8},{8,0},{16,24},{24,16},{1,9},{9,1},{17,25},{25,17},{2,10},{10... | collective-permute-start | bytes 6291464 | tf_op jit(solution)/shard_map/ppermute | solution.py:65
  257.9 21.4 %collective-permute-start.42 = (bf16[2,2,256,512]{3,2,1,0:T(8,128)(2,1)}, bf16[2,2,256,512]{3,2,1,0:T(8,128)(2,1)S(1)}, u32[]{:S(2)}, u32[]{:S(2)}) collective-permute-start(bf16[2,2,256,512]{3,2,1,0:T(8,128)(2,1)} %get-tuple-element.307), channel_id=1, source_target_pairs={{0,8},{8,0},{16,24},{24,16},{1,9},{9,1},{17,25},{25,17},{2,10},{10... | collective-permute-start | bytes 3145736 | tf_op jit(solution)/shard_map/ppermute | solution.py:65
  258.0 29.3 %collective-permute-start.43 = (bf16[4,128,1024]{2,1,0:T(8,128)(2,1)}, bf16[4,128,1024]{2,1,0:T(8,128)(2,1)S(1)}, u32[]{:S(2)}, u32[]{:S(2)}) collective-permute-start(bf16[4,128,1024]{2,1,0:T(8,128)(2,1)} %pad_maximum_fusion.5), channel_id=1, source_target_pairs={{0,1},{1,0},{2,3},{3,2},{4,5},{5,4},{6,7},{7,6},{8,9},{9,8},{10,11... | collective-permute-start | bytes 3145736 | tf_op jit(solution)/shard_map/ppermute | solution.py:65
  259.3 32.2 %collective-permute-start.44 = (bf16[2,256,1024]{2,1,0:T(8,128)(2,1)}, bf16[2,256,1024]{2,1,0:T(8,128)(2,1)}, u32[]{:S(2)}, u32[]{:S(2)}) collective-permute-start(bf16[2,256,1024]{2,1,0:T(8,128)(2,1)} %get-tuple-element.311), channel_id=1, source_target_pairs={{0,16},{8,24},{16,0},{24,8},{1,17},{9,25},{17,1},{25,9},{2,18},{10... | collective-permute-start | bytes 3145736 | tf_op jit(solution)/shard_map/ppermute | solution.py:65
  288.5 14.0 %collective-permute-start.46 = (bf16[4,64,1024]{2,1,0:T(8,128)(2,1)}, bf16[4,64,1024]{2,1,0:T(8,128)(2,1)}, u32[]{:S(2)}, u32[]{:S(2)}) collective-permute-start(bf16[4,64,1024]{2,1,0:T(8,128)(2,1)} %fusion.11), channel_id=1, source_target_pairs={{0,2},{1,3},{2,0},{3,1},{4,6},{5,7},{6,4},{7,5},{8,10},{9,11},{10,... | collective-permute-start | bytes 1572872 | tf_op jit(solution)/shard_map/ppermute | solution.py:65
  290.1 42.4 %collective-permute-start.47 = (bf16[2,256,1024]{2,1,0:T(8,128)(2,1)}, bf16[2,256,1024]{2,1,0:T(8,128)(2,1)S(1)}, u32[]{:S(2)}, u32[]{:S(2)}) collective-permute-start(bf16[2,256,1024]{2,1,0:T(8,128)(2,1)} %get-tuple-element.325), channel_id=1, source_target_pairs={{0,16},{8,24},{16,0},{24,8},{1,17},{9,25},{17,1},{25,9},{2,18},{10... | collective-permute-start | bytes 3145736 | tf_op jit(solution)/shard_map/ppermute | solution.py:65
  291.5 32.6 %collective-permute-start.45 = (bf16[2,3,256,512]{3,2,1,0:T(8,128)(2,1)S(1)}, bf16[2,3,256,512]{3,2,1,0:T(8,128)(2,1)S(1)}, u32[]{:S(2)}, u32[]{:S(2)}) collective-permute-start(bf16[2,3,256,512]{3,2,1,0:T(8,128)(2,1)S(1)} %get-tuple-element.321), channel_id=1, source_target_pairs={{0,8},{8,0},{16,24},{24,16},{1,9},{9,1},{17,25},{25,17},{2,10},{10... | collective-permute-start | bytes 4718600 | tf_op jit(solution)/shard_map/ppermute | solution.py:65
  293.6 30.4 %collective-permute-start.48 = (bf16[2,128,1024]{2,1,0:T(8,128)(2,1)S(1)}, bf16[2,128,1024]{2,1,0:T(8,128)(2,1)S(1)}, u32[]{:S(2)}, u32[]{:S(2)}) collective-permute-start(bf16[2,128,1024]{2,1,0:T(8,128)(2,1)S(1)} %get-tuple-element.328), channel_id=1, source_target_pairs={{0,1},{1,0},{2,3},{3,2},{4,5},{5,4},{6,7},{7,6},{8,9},{9,8},{10,11... | collective-permute-start | bytes 1572872 | tf_op jit(solution)/shard_map/ppermute | solution.py:65
  294.5 37.9 %collective-permute-start.54 = (bf16[2,256,512]{2,1,0:T(8,128)(2,1)S(1)}, bf16[2,256,512]{2,1,0:T(8,128)(2,1)S(1)}, u32[]{:S(2)}, u32[]{:S(2)}) collective-permute-start(bf16[2,256,512]{2,1,0:T(8,128)(2,1)S(1)} %copy-done.106), channel_id=1, source_target_pairs={{0,16},{8,24},{16,0},{24,8},{1,17},{9,25},{17,1},{25,9},{2,18},{10... | collective-permute-start | bytes 1572872 | tf_op jit(solution)/shard_map/ppermute | solution.py:65
  321.3 25.1 %collective-permute-start.49 = (bf16[4,64,1024]{2,1,0:T(8,128)(2,1)S(1)}, bf16[4,64,1024]{2,1,0:T(8,128)(2,1)S(1)}, u32[]{:S(2)}, u32[]{:S(2)}) collective-permute-start(bf16[4,64,1024]{2,1,0:T(8,128)(2,1)S(1)} %fusion.25), channel_id=1, source_target_pairs={{0,4},{1,5},{2,6},{3,7},{4,0},{5,1},{6,2},{7,3},{8,12},{9,13},{10,... | collective-permute-start | bytes 1572872 | tf_op jit(solution)/shard_map/ppermute | solution.py:65
  330.7 19.0 %collective-permute-start.52 = (bf16[2,64,1024]{2,1,0:T(8,128)(2,1)S(1)}, bf16[2,64,1024]{2,1,0:T(8,128)(2,1)S(1)}, u32[]{:S(2)}, u32[]{:S(2)}) collective-permute-start(bf16[2,64,1024]{2,1,0:T(8,128)(2,1)S(1)} %dynamic-slice_add_fusion.3), channel_id=1, source_target_pairs={{0,2},{1,3},{2,0},{3,1},{4,6},{5,7},{6,4},{7,5},{8,10},{9,11},{10,... | collective-permute-start | bytes 786440 | tf_op jit(solution)/shard_map/ppermute | solution.py:65
  346.6 39.9 %collective-permute-start.50 = (bf16[2,3,256,512]{3,2,1,0:T(8,128)(2,1)S(1)}, bf16[2,3,256,512]{3,2,1,0:T(8,128)(2,1)S(1)}, u32[]{:S(2)}, u32[]{:S(2)}) collective-permute-start(bf16[2,3,256,512]{3,2,1,0:T(8,128)(2,1)S(1)} %get-tuple-element.338), channel_id=1, source_target_pairs={{0,8},{8,0},{16,24},{24,16},{1,9},{9,1},{17,25},{25,17},{2,10},{10... | collective-permute-start | bytes 4718600 | tf_op jit(solution)/shard_map/ppermute | solution.py:65
  346.7 24.0 %collective-permute-start.51 = (bf16[4,64,1024]{2,1,0:T(8,128)(2,1)S(1)}, bf16[4,64,1024]{2,1,0:T(8,128)(2,1)S(1)}, u32[]{:S(2)}, u32[]{:S(2)}) collective-permute-start(bf16[4,64,1024]{2,1,0:T(8,128)(2,1)S(1)} %add.285), channel_id=1, source_target_pairs={{0,2},{1,3},{2,0},{3,1},{4,6},{5,7},{6,4},{7,5},{8,10},{9,11},{10,... | collective-permute-start | bytes 1572872 | tf_op jit(solution)/shard_map/ppermute | solution.py:65
  347.4 21.7 %collective-permute-start.53 = (bf16[2,128,1024]{2,1,0:T(8,128)(2,1)S(1)}, bf16[2,128,1024]{2,1,0:T(8,128)(2,1)S(1)}, u32[]{:S(2)}, u32[]{:S(2)}) collective-permute-start(bf16[2,128,1024]{2,1,0:T(8,128)(2,1)S(1)} %get-tuple-element.344), channel_id=1, source_target_pairs={{0,1},{1,0},{2,3},{3,2},{4,5},{5,4},{6,7},{7,6},{8,9},{9,8},{10,11... | collective-permute-start | bytes 1572872 | tf_op jit(solution)/shard_map/ppermute | solution.py:65
  348.3 19.3 %collective-permute-start.55 = (bf16[3,256,512]{2,1,0:T(8,128)(2,1)S(1)}, bf16[3,256,512]{2,1,0:T(8,128)(2,1)S(1)}, u32[]{:S(2)}, u32[]{:S(2)}) collective-permute-start(bf16[3,256,512]{2,1,0:T(8,128)(2,1)S(1)} %get-tuple-element.347), channel_id=1, source_target_pairs={{0,16},{8,24},{16,0},{24,8},{1,17},{9,25},{17,1},{25,9},{2,18},{10... | collective-permute-start | bytes 2359304 | tf_op jit(solution)/shard_map/ppermute | solution.py:65
  367.9 17.7 %collective-permute-start.58 = (bf16[5,128,512]{2,1,0:T(8,128)(2,1)S(1)}, bf16[5,128,512]{2,1,0:T(8,128)(2,1)S(1)}, u32[]{:S(2)}, u32[]{:S(2)}) collective-permute-start(bf16[5,128,512]{2,1,0:T(8,128)(2,1)S(1)} %pad_maximum_fusion.10), channel_id=1, source_target_pairs={{0,1},{1,0},{2,3},{3,2},{4,5},{5,4},{6,7},{7,6},{8,9},{9,8},{10,11... | collective-permute-start | bytes 1966088 | tf_op jit(solution)/shard_map/ppermute | solution.py:65
  370.8 52.8 %collective-permute-start.60 = (bf16[2,4,64,1024]{3,2,1,0:T(8,128)(2,1)S(1)}, bf16[2,4,64,1024]{3,2,1,0:T(8,128)(2,1)S(1)}, u32[]{:S(2)}, u32[]{:S(2)}) collective-permute-start(bf16[2,4,64,1024]{3,2,1,0:T(8,128)(2,1)S(1)} %pad_maximum_fusion.6.pair_ref), channel_id=1, source_target_pairs={{0,1},{1,0},{2,3},{3,2},{4,5},{5,4},{6,7},{7,6},{8,9},{9,8},{10,11... | collective-permute-start | bytes 3145736 | tf_op jit(solution)/shard_map/ppermute | solution.py:65
  386.8 21.1 %collective-permute-start.59 = (bf16[3,256,512]{2,1,0:T(8,128)(2,1)S(1)}, bf16[3,256,512]{2,1,0:T(8,128)(2,1)S(1)}, u32[]{:S(2)}, u32[]{:S(2)}) collective-permute-start(bf16[3,256,512]{2,1,0:T(8,128)(2,1)S(1)} %get-tuple-element.362), channel_id=1, source_target_pairs={{0,16},{8,24},{16,0},{24,8},{1,17},{9,25},{17,1},{25,9},{2,18},{10... | collective-permute-start | bytes 2359304 | tf_op jit(solution)/shard_map/ppermute | solution.py:65
  404.1 18.2 %collective-permute-start.68 = (bf16[5,64,512]{2,1,0:T(8,128)(2,1)}, bf16[5,64,512]{2,1,0:T(8,128)(2,1)}, u32[]{:S(2)}, u32[]{:S(2)}) collective-permute-start(bf16[5,64,512]{2,1,0:T(8,128)(2,1)} %fusion.16), channel_id=1, source_target_pairs={{0,2},{1,3},{2,0},{3,1},{4,6},{5,7},{6,4},{7,5},{8,10},{9,11},{10,... | collective-permute-start | bytes 983048 | tf_op jit(solution)/shard_map/ppermute | solution.py:65
  408.9 26.6 %collective-permute-start.69 = (bf16[3,128,512]{2,1,0:T(8,128)(2,1)}, bf16[3,128,512]{2,1,0:T(8,128)(2,1)}, u32[]{:S(2)}, u32[]{:S(2)}) collective-permute-start(bf16[3,128,512]{2,1,0:T(8,128)(2,1)} %get-tuple-element.378), channel_id=1, source_target_pairs={{0,1},{1,0},{2,3},{3,2},{4,5},{5,4},{6,7},{7,6},{8,9},{9,8},{10,11... | collective-permute-start | bytes 1179656 | tf_op jit(solution)/shard_map/ppermute | solution.py:65
  432.7 14.6 %collective-permute-start.70 = (bf16[2,2,64,1024]{3,2,1,0:T(8,128)(2,1)S(1)}, bf16[2,2,64,1024]{3,2,1,0:T(8,128)(2,1)S(1)}, u32[]{:S(2)}, u32[]{:S(2)}) collective-permute-start(bf16[2,2,64,1024]{3,2,1,0:T(8,128)(2,1)S(1)} %pad_maximum_fusion.12.pair_ref), channel_id=1, source_target_pairs={{0,1},{1,0},{2,3},{3,2},{4,5},{5,4},{6,7},{7,6},{8,9},{9,8},{10,11... | collective-permute-start | bytes 1572872 | tf_op jit(solution)/shard_map/ppermute | solution.py:65
  444.0 13.8 %collective-permute-start.72 = (bf16[5,64,512]{2,1,0:T(8,128)(2,1)S(1)}, bf16[5,64,512]{2,1,0:T(8,128)(2,1)S(1)}, u32[]{:S(2)}, u32[]{:S(2)}) collective-permute-start(bf16[5,64,512]{2,1,0:T(8,128)(2,1)S(1)} %fusion.21), channel_id=1, source_target_pairs={{0,4},{1,5},{2,6},{3,7},{4,0},{5,1},{6,2},{7,3},{8,12},{9,13},{10,... | collective-permute-start | bytes 983048 | tf_op jit(solution)/shard_map/ppermute | solution.py:65
  449.4 20.7 %collective-permute-start.74 = (bf16[2,2,64,1024]{3,2,1,0:T(8,128)(2,1)S(1)}, bf16[2,2,64,1024]{3,2,1,0:T(8,128)(2,1)S(1)}, u32[]{:S(2)}, u32[]{:S(2)}) collective-permute-start(bf16[2,2,64,1024]{3,2,1,0:T(8,128)(2,1)S(1)} %pad_maximum_fusion.13.pair_ref), channel_id=1, source_target_pairs={{0,1},{1,0},{2,3},{3,2},{4,5},{5,4},{6,7},{7,6},{8,9},{9,8},{10,11... | collective-permute-start | bytes 1572872 | tf_op jit(solution)/shard_map/ppermute | solution.py:65
  458.0 18.4 %collective-permute-start.75 = (bf16[5,64,512]{2,1,0:T(8,128)(2,1)S(1)}, bf16[5,64,512]{2,1,0:T(8,128)(2,1)S(1)}, u32[]{:S(2)}, u32[]{:S(2)}) collective-permute-start(bf16[5,64,512]{2,1,0:T(8,128)(2,1)S(1)} %add.314), channel_id=1, source_target_pairs={{0,2},{1,3},{2,0},{3,1},{4,6},{5,7},{6,4},{7,5},{8,10},{9,11},{10,... | collective-permute-start | bytes 983048 | tf_op jit(solution)/shard_map/ppermute | solution.py:65
  476.4 17.7 %collective-permute-start.78 = (bf16[2,5,64,512]{3,2,1,0:T(8,128)(2,1)S(1)}, bf16[2,5,64,512]{3,2,1,0:T(8,128)(2,1)S(1)}, u32[]{:S(2)}, u32[]{:S(2)}) collective-permute-start(bf16[2,5,64,512]{3,2,1,0:T(8,128)(2,1)S(1)} %pad_maximum_fusion.11.pair_ref), channel_id=1, source_target_pairs={{0,1},{1,0},{2,3},{3,2},{4,5},{5,4},{6,7},{7,6},{8,9},{9,8},{10,11... | collective-permute-start | bytes 1966088 | tf_op jit(solution)/shard_map/ppermute | solution.py:65
  480.9 19.8 %collective-permute-start.79 = (bf16[2,3,64,512]{3,2,1,0:T(8,128)(2,1)S(1)}, bf16[2,3,64,512]{3,2,1,0:T(8,128)(2,1)S(1)}, u32[]{:S(2)}, u32[]{:S(2)}) collective-permute-start(bf16[2,3,64,512]{3,2,1,0:T(8,128)(2,1)S(1)} %pad_maximum_fusion.14.pair_ref), channel_id=1, source_target_pairs={{0,1},{1,0},{2,3},{3,2},{4,5},{5,4},{6,7},{7,6},{8,9},{9,8},{10,11... | collective-permute-start | bytes 1179656 | tf_op jit(solution)/shard_map/ppermute | solution.py:65
  (145 other events, 1772.5 us)

commit v2 on v1

--- a/solution.py
+++ b/solution.py
@@ -20,16 +20,17 @@
 f32 = jnp.float32
 
 VEC = {
-    "ln1_gain": (0, 256),
-    "ln1_bias": (256, 256),
-    "b_qv": (512, 512),
-    "out_bias": (1024, 256),
-    "ln2_gain": (1280, 256),
-    "ln2_bias": (1536, 256),
-    "up_bias": (1792, 1024),
-    "down_bias": (2816, 256),
+    "ln1_gain": (0, 1),
+    "ln1_bias": (1, 1),
+    "b_qv": (2, 2),
+    "out_bias": (4, 1),
+    "ln2_gain": (5, 1),
+    "ln2_bias": (6, 1),
+    "up_bias": (7, 4),
+    "down_bias": (11, 1),
 }
-VEC_LEN = 3072
+VEC_ROWS = 16
+LANES = 256
 
 any_spec = pl.BlockSpec(memory_space=pltpu.MemorySpace.HBM)
 
@@ -50,11 +51,13 @@
     )
 
 
+def vec_rows(vec_ref, rows):
+    firsts = [shard * VEC_ROWS + row for shard, row in rows]
+    return jnp.concatenate([vec_ref[first : first + 1, :] for first in firsts], axis=1)
+
+
 def row_of(vec_ref, name):
-    start, size = VEC[name]
-    return jnp.concatenate(
-        [vec_ref[shard : shard + 1, start : start + size] for shard in range(SHARDS)], axis=1
-    )
+    return vec_rows(vec_ref, [(shard, VEC[name][0]) for shard in range(SHARDS)])
 
 
 def whole(shape):
@@ -77,12 +80,21 @@
             [jnp.stack([self.shard, self.low, self.mid]).astype(jnp.int32), starts]
         )
         self.last = ()
+        self.count = 0
+        self.due = []
 
     def wait(self, *values):
-        self.index = lax.optimization_barrier((self.index, *values))[0]
+        self.index = after(self.index, *values, *self.last)
+
+    def by(self, kernels, *values):
+        self.due.append((self.count + kernels, values))
 
     def ran(self, value):
         self.last = (value,)
+        self.count += 1
+        ready = [value for when, values in self.due if when <= self.count for value in values]
+        self.due = [entry for entry in self.due if entry[0] > self.count]
+        self.wait(*ready)
         return value
 
     def move(self, value, axis, size, bit):
@@ -104,34 +116,28 @@
     def pick(self, value, which, size):
         return lax.dynamic_slice_in_dim(value, which * size, size, 1)
 
-    def reduce_vec(self, value):
-        value = value + self.core(value)
-        value = value + self.across(value)
-        row = lax.dynamic_slice_in_dim(value, self.shard, 1, 0)
-        bit = 1
-        while bit < self.reps:
-            row = row + self.rep(row, bit)
-            bit *= 2
-        return row
-
 
 def after(value, *earlier):
     return lax.optimization_barrier((value, *earlier))[0] if earlier else value
 
 
 class ShardSum:
-    def __init__(self, moves, keep, send):
+    def __init__(self, moves, keep, send, kernels=1):
         self.moves, self.keep = moves, keep
         self.got = moves.core(send)
-
-    def cross(self):
+        moves.by(kernels, self.got)
+
+    def cross(self, kernels):
+        self.got = after(self.got, *self.moves.last)
         out = self.keep[1] + self.got[1]
         self.mine = self.keep[0] + self.got[0]
         self.moves.wait(out, self.mine)
         self.got = self.moves.across(out)
+        self.moves.by(kernels, self.got)
 
     def halves(self):
-        moves, mine, got = self.moves, self.mine, self.got
+        moves, mine = self.moves, self.mine
+        got = after(self.got, *moves.last)
         size = mine.shape[1] // 2
         return [
             moves.pick(mine, which, size) + moves.pick(got, which, size)
@@ -140,45 +146,79 @@
 
 
 class RepSum:
-    def __init__(self, moves, sums):
+    def __init__(self, moves, sums, kernels=1):
         self.moves = moves
         halves = [s.halves() for s in sums]
         self.mine = jnp.concatenate([h[0] for h in halves])
-        self.send(jnp.concatenate([h[1] for h in halves]), 1)
         self.bit = 2
-
-    def send(self, out, bit):
+        self.send(jnp.concatenate([h[1] for h in halves]), 1, kernels)
+
+    def send(self, out, bit, kernels):
         self.moves.wait(out, self.mine)
         self.got = self.moves.rep(out, bit)
-
-    def split(self):
+        self.moves.by(kernels, self.got)
+
+    def split(self, kernels=1):
         moves = self.moves
+        got = after(self.got, *moves.last)
         size = self.mine.shape[1] // 2
         out, self.mine = [
-            moves.pick(self.mine, which, size) + moves.pick(self.got, which, size)
+            moves.pick(self.mine, which, size) + moves.pick(got, which, size)
             for which in (1 - moves.mid, moves.mid)
         ]
-        self.send(out, 2)
-
-    def add(self):
-        self.mine = self.mine + self.got
+        self.send(out, 2, kernels)
+
+    def add(self, kernels=1):
+        self.mine = self.mine + after(self.got, *self.moves.last)
         self.bit *= 2
         self.got = None
         if self.bit < self.moves.reps:
-            self.send(self.mine, self.bit)
-
-    def spread(self):
+            self.send(self.mine, self.bit, kernels)
+
+    def spread(self, kernels=1):
         while self.got is not None:
             self.add()
-        self.send(self.mine, 2)
-
-    def finish(self):
-        self.pair = jnp.stack([self.mine, self.got])
-        self.send(self.pair, 1)
+        self.send(self.mine, 2, kernels)
+
+    def finish(self, kernels=1):
+        self.pair = jnp.stack([self.mine, after(self.got, *self.moves.last)])
+        self.send(self.pair, 1, kernels)
 
     def pieces(self):
         self.moves.wait(self.got)
         return (self.pair, self.got)
+
+
+class VecSum:
+    def __init__(self, moves, value):
+        self.moves, self.value = moves, value
+        self.plan = [moves.core, moves.across]
+        bit = 1
+        while bit < moves.reps:
+            self.plan.append(functools.partial(moves.rep, bit=bit))
+            bit *= 2
+        self.at = 0
+        self.send()
+
+    def send(self):
+        self.got = self.plan[self.at](self.value)
+        self.moves.by(1, self.got)
+        self.at += 1
+
+    def step(self):
+        moves = self.moves
+        self.value = self.value + after(self.got, *moves.last)
+        if self.at == 2:
+            self.value = lax.dynamic_slice_in_dim(self.value, moves.shard * VEC_ROWS, VEC_ROWS, 0)
+        moves.wait(self.value)
+        if self.at < len(self.plan):
+            self.send()
+
+    def rest(self):
+        while self.at < len(self.plan):
+            self.step()
+        self.step()
+        return self.value
 
 
 def piece_copies(index_ref, pieces, target, sems):
@@ -215,7 +255,7 @@
     @pl.when(pl.program_id(0) == 0)
     def _():
         for k, ref in enumerate((own_ref, near_ref, far_ref, far_near_ref)):
-            vec_ref[pl.ds(shard ^ k, 1), :] = ref[...].astype(f32)
+            vec_ref[pl.ds(pl.multiple_of((shard ^ k) * VEC_ROWS, VEC_ROWS), VEC_ROWS), :] = ref[...].astype(f32)
 
     hat, _ = norm_parts(tokens_ref[...].astype(f32))
     normed_ref[...] = (hat * row_of(vec_ref, "ln1_gain") + row_of(vec_ref, "ln1_bias")).astype(bf16)
@@ -229,12 +269,12 @@
         grid_spec=pltpu.PrefetchScalarGridSpec(
             num_scalar_prefetch=1,
             grid=(rows // block,),
-            in_specs=[row] + [whole((1, VEC_LEN))] * 4,
-            out_specs=[row, whole((SHARDS, VEC_LEN))],
+            in_specs=[row] + [whole((VEC_ROWS, LANES))] * 4,
+            out_specs=[row, whole((SHARDS * VEC_ROWS, LANES))],
         ),
         out_shape=[
             jax.ShapeDtypeStruct((rows, width), bf16),
-            jax.ShapeDtypeStruct((SHARDS, VEC_LEN), f32),
+            jax.ShapeDtypeStruct((SHARDS * VEC_ROWS, LANES), f32),
         ],
         compiler_params=params(16),
         cost_estimate=cost(20 * rows * width, 4 * rows * width),
@@ -262,14 +302,14 @@
             copy.wait()
 
     part = weight_ref.shape[1] // 3
-    start = VEC["b_qv"][0]
+    first = VEC["b_qv"][0]
     normed = normed_ref[...]
     for i in range(3):
         cols = slice(i * part, (i + 1) * part)
         value = dot(normed, weight_ref[:, cols])
         if i != 1:
             shard = half if i == 0 else 2 + half
-            value = value + vec_ref[shard : shard + 1, start : start + part]
+            value = value + vec_rows(vec_ref, [(shard, first), (shard, first + 1)])
         out_ref[:, cols] = value.astype(bf16)
 
 
@@ -282,7 +322,7 @@
             num_scalar_prefetch=1,
             grid=(rows // block,),
             in_specs=[any_spec] * len(pieces)
-            + [pl.BlockSpec((block, width), lambda i, idx: (i, 0)), whole((SHARDS, VEC_LEN))],
+            + [pl.BlockSpec((block, width), lambda i, idx: (i, 0)), whole((SHARDS * VEC_ROWS, LANES))],
             out_specs=[pl.BlockSpec((block, cols), lambda i, idx: (i, 0)), whole((width, cols))],
             scratch_shapes=[pltpu.SemaphoreType.DMA((6,))],
         ),
@@ -364,69 +404,137 @@
 
 
 def attend_backward_body(
-    first_head, start_ref, q_ref, k_ref, v_ref, out_ref, dout_ref, total_ref, dq_ref, dk_ref, dv_ref, pen_ref
+    first_head,
+    steps,
+    index_ref,
+    q_ref,
+    k_ref,
+    v_ref,
+    out_ref,
+    dout_ref,
+    total_ref,
+    normed_ref,
+    dq_ref,
+    dk_ref,
+    dv_ref,
+    keep_ref,
+    send_ref,
+    sums_ref,
+    pen_ref,
 ):
-    pair = pl.program_id(1)
+    step = pl.program_id(0)
     seq_len = q_ref.shape[0]
     scale = HEAD_DIM**-0.5
-
-    @pl.when(pair == 0)
-    def _():
-        pen_ref[...] = penalty(start_ref[3 + pl.program_id(0)], seq_len)
-
-    queries, keys, values, d_out = q_ref[...], k_ref[...], v_ref[...], dout_ref[...]
-    lane = lax.broadcasted_iota(jnp.int32, (seq_len, PAIR), 1)
-    keys_t = keys.T
-    both_t = (d_out.astype(f32) * out_ref[...].astype(f32)).T
-    d_q, d_k, d_v = [], [], []
-    for e in range(2):
-        chosen = (lane < HEAD_DIM) if e == 0 else (lane >= HEAD_DIM)
-        part = slice(e * HEAD_DIM, (e + 1) * HEAD_DIM)
-        key_e = jnp.where(chosen, keys * scale, 0).astype(bf16)
-        value_e = jnp.where(chosen, values, 0)
-        inner = jnp.sum(both_t[part, :], axis=0, keepdims=True)
-        scores = dot(key_e, queries, 1, 1) - slope_of(first_head + 2 * pair + e) * pen_ref[...]
-        probs = jnp.exp(scores - total_ref[0, 0, e : e + 1, :])
-        d_scores = (probs * (dot(value_e, d_out, 1, 1) - inner)).astype(bf16)
-        d_v.append(dot(probs.astype(bf16), d_out))
-        d_k.append(dot(d_scores, queries))
-        d_q.append(dot(keys_t[part, :], d_scores))
-    dq_ref[...] = (jnp.concatenate(d_q, axis=0) * scale).T.astype(bf16)
-    dk_ref[...] = (jnp.where(lane < HEAD_DIM, d_k[0], d_k[1]) * scale).astype(bf16)
-    dv_ref[...] = jnp.where(lane < HEAD_DIM, d_v[0], d_v[1]).astype(bf16)
-
-
-def attend_backward(half, index, joined, attended, d_attended, totals):
+    pairs = dq_ref.shape[1] // PAIR
+    seq, pair = step // pairs, step % pairs
+
+    @pl.when((step < steps) & (pair == 0))
+    def _():
+        pen_ref[...] = penalty(index_ref[3 + seq], seq_len)
+
+    @pl.when(step < steps)
+    def _():
+        queries, keys, values, d_out = q_ref[...], k_ref[...], v_ref[...], dout_ref[...]
+        lane = lax.broadcasted_iota(jnp.int32, (seq_len, PAIR), 1)
+        keys_t = keys.T
+        both_t = (d_out.astype(f32) * out_ref[...].astype(f32)).T
+        d_q, d_k, d_v = [], [], []
+        for e in range(2):
+            chosen = (lane < HEAD_DIM) if e == 0 else (lane >= HEAD_DIM)
+            part = slice(e * HEAD_DIM, (e + 1) * HEAD_DIM)
+            key_e = jnp.where(chosen, keys * scale, 0).astype(bf16)
+            value_e = jnp.where(chosen, values, 0)
+            inner = jnp.sum(both_t[part, :], axis=0, keepdims=True)
+            scores = dot(key_e, queries, 1, 1) - slope_of(first_head + 2 * pair + e) * pen_ref[...]
+            probs = jnp.exp(scores - total_ref[0, 0, e : e + 1, :])
+            d_scores = (probs * (dot(value_e, d_out, 1, 1) - inner)).astype(bf16)
+            d_v.append(dot(probs.astype(bf16), d_out))
+            d_k.append(dot(d_scores, queries))
+            d_q.append(dot(keys_t[part, :], d_scores))
+        rows = pl.ds(pl.multiple_of(seq * seq_len, seq_len), seq_len)
+        cols = pl.ds(pl.multiple_of(pair * PAIR, PAIR), PAIR)
+        dq_ref[rows, cols] = (jnp.concatenate(d_q, axis=0) * scale).T.astype(bf16)
+        dk_ref[rows, cols] = (jnp.where(lane < HEAD_DIM, d_k[0], d_k[1]) * scale).astype(bf16)
+        dv_ref[rows, cols] = jnp.where(lane < HEAD_DIM, d_v[0], d_v[1]).astype(bf16)
+
+    @pl.when(step == steps)
+    def _():
+        sums_ref[0:1, :] = column_sum(dq_ref[...].astype(f32))
+        sums_ref[1:2, :] = column_sum(dv_ref[...].astype(f32))
+
+    @pl.when(step >= steps)
+    def _():
+        block = keep_ref.shape[2]
+        t = step - steps
+        k = jnp.where(t < 2, 2 * t + 1, 2 * t - 4)
+        left = normed_ref[:, pl.ds(pl.multiple_of((index_ref[0] ^ k) * block, block), block)]
+        for i, ref in enumerate((dq_ref, dk_ref, dv_ref)):
+            value = dot(left, ref[...], 0, 0).astype(bf16)
+
+            @pl.when(t < 2)
+            def _(i=i, value=value):
+                send_ref[0, i] = value
+
+            @pl.when(t >= 2)
+            def _(i=i, value=value):
+                keep_ref[0, i] = value
+
+
+def attend_backward(half, index, joined, attended, d_attended, totals, normed):
     count = index.shape[0] - 3
-    seq_len, width = joined.shape[0] // count, joined.shape[1] // 3
+    rows, width = joined.shape[0], joined.shape[1] // 3
+    seq_len = rows // count
     pairs = width // PAIR
+    steps = count * pairs
+    model = normed.shape[1]
 
     def cols(first):
-        return pl.BlockSpec((seq_len, PAIR), lambda s, h, st: (s, first + h))
-
+        def where(i, idx):
+            at = jnp.minimum(i, steps - 1)
+            return (at // pairs, first + at % pairs)
+
+        return pl.BlockSpec((seq_len, PAIR), where)
+
+    def totals_at(i, idx):
+        at = jnp.minimum(i, steps - 1)
+        return (at // pairs, at % pairs, 0, 0)
+
+    grads = (2, 3, model // SHARDS, width)
+    unit = (1,) + grads[1:]
     return pl.pallas_call(
-        functools.partial(attend_backward_body, half * 2 * pairs),
+        functools.partial(attend_backward_body, half * 2 * pairs, steps),
         grid_spec=pltpu.PrefetchScalarGridSpec(
             num_scalar_prefetch=1,
-            grid=(count, pairs),
+            grid=(steps + SHARDS,),
             in_specs=[
                 cols(0),
                 cols(pairs),
                 cols(2 * pairs),
                 cols(0),
                 cols(half * pairs),
-                pl.BlockSpec((1, 1, 2, seq_len), lambda s, h, st: (s, h, 0, 0)),
+                pl.BlockSpec((1, 1, 2, seq_len), totals_at),
+                whole((rows, model)),
             ],
-            out_specs=[cols(0)] * 3,
+            out_specs=[whole((rows, width))] * 3
+            + [
+                pl.BlockSpec(unit, lambda i, idx: (jnp.clip(i - steps - 2, 0, 1), 0, 0, 0)),
+                pl.BlockSpec(unit, lambda i, idx: (jnp.clip(i - steps, 0, 1), 0, 0, 0)),
+                whole((2, width)),
+            ],
             scratch_shapes=[pltpu.VMEM((seq_len, seq_len), f32)],
         ),
-        out_shape=[jax.ShapeDtypeStruct((count * seq_len, width), bf16)] * 3,
-        compiler_params=params(24),
+        out_shape=[jax.ShapeDtypeStruct((rows, width), bf16)] * 3
+        + [
+            jax.ShapeDtypeStruct(grads, bf16),
+            jax.ShapeDtypeStruct(grads, bf16),
+            jax.ShapeDtypeStruct((2, width), f32),
+        ],
+        compiler_params=params(40),
         cost_estimate=cost(
-            36 * count * seq_len * seq_len * width, 16 * count * seq_len * width, count * seq_len * seq_len * 2 * pairs
+            36 * rows * seq_len * width + 6 * rows * model * width, 16 * rows * width, rows * seq_len * 2 * pairs
         ),
         name="attend_backward",
-    )(index, joined, joined, joined, attended, d_attended, totals)
+    )(index, joined, joined, joined, attended, d_attended, totals, normed)
 
 
 def middle_body(index_ref, *refs):
@@ -465,7 +573,7 @@
         grid_spec=pltpu.PrefetchScalarGridSpec(
             num_scalar_prefetch=1,
             grid=(rows // block,),
-            in_specs=[any_spec] * 6 + [part, part, row, whole((SHARDS, VEC_LEN))],
+            in_specs=[any_spec] * 6 + [part, part, row, whole((SHARDS * VEC_ROWS, LANES))],
             out_specs=[row, row, whole((width, width))],
             scratch_shapes=[pltpu.SemaphoreType.DMA((6,))],
         ),
@@ -538,10 +646,7 @@
 
     @pl.when(step == 0)
     def _():
-        start = VEC["up_bias"][0] + chunk * block
-        bias = jnp.concatenate(
-            [vec_ref[one : one + 1, start : start + block] for one in range(SHARDS)], axis=1
-        )
+        bias = vec_rows(vec_ref, [(one, VEC["up_bias"][0] + chunk) for one in range(SHARDS)])
         for m in range(count):
             rows = slice(m * rows_each, (m + 1) * rows_each)
             value, slope = gelu_and_slope(dot(normed_ref[rows, :], up_ref[...]) + bias)
@@ -603,7 +708,7 @@
         grid_spec=pltpu.PrefetchScalarGridSpec(
             num_scalar_prefetch=1,
             grid=(6,),
-            in_specs=[any_spec] * (8 if fresh else 10) + [whole((SHARDS, VEC_LEN))],
+            in_specs=[any_spec] * (8 if fresh else 10) + [whole((SHARDS * VEC_ROWS, LANES))],
             out_specs=[
                 any_spec,
                 any_spec,
@@ -756,7 +861,7 @@
                 half,
                 half,
                 whole((width, width)),
-                whole((SHARDS, VEC_LEN)),
+                whole((SHARDS * VEC_ROWS, LANES)),
             ],
             out_specs=[
                 by_rows(width),
@@ -830,7 +935,7 @@
         grid_spec=pltpu.PrefetchScalarGridSpec(
             num_scalar_prefetch=1,
             grid=(rows // rows_each,),
-            in_specs=[any_spec] * (6 * CHUNKS) + [by_rows(size), by_rows(width), whole((SHARDS, VEC_LEN))],
+            in_specs=[any_spec] * (6 * CHUNKS) + [by_rows(size), by_rows(width), whole((SHARDS * VEC_ROWS, LANES))],
             out_specs=by_rows(width),
             scratch_shapes=[pltpu.VMEM((size, width), bf16), pltpu.SemaphoreType.DMA((CHUNKS, 6))],
         ),
@@ -839,55 +944,6 @@
         cost_estimate=cost(2 * rows * width * size, 2 * rows * size + 2 * width * size + 6 * rows * width),
         name="block_output",
     )(index, *pieces, hidden, middle, vec)
-
-
-def joined_grad_body(index_ref, normed_ref, dq_ref, dk_ref, dv_ref, keep_ref, send_ref, sums_ref):
-    step = pl.program_id(0)
-    part = dq_ref.shape[1]
-
-    @pl.when(step == 0)
-    def _():
-        sums_ref[0:1, :] = column_sum(dq_ref[...].astype(f32))
-        sums_ref[1:2, :] = column_sum(dv_ref[...].astype(f32))
-
-    for t, k in enumerate((1, 3, 0, 2)):
-
-        @pl.when(step == t)
-        def _(t=t, k=k):
-            block = keep_ref.shape[2]
-            cols = pl.ds(pl.multiple_of((index_ref[0] ^ k) * block, block), block)
-            left = normed_ref[:, cols]
-            target = send_ref if t < 2 else keep_ref
-            for i, ref in enumerate((dq_ref, dk_ref, dv_ref)):
-                target[0, i] = dot(left, ref[...], 0, 0).astype(bf16)
-
-
-def joined_grad(index, normed, d_q, d_k, d_v):
-    rows, width = normed.shape
-    part = d_q.shape[1]
-    grads = (2, 3, width // SHARDS, part)
-    unit = (1,) + grads[1:]
-    return pl.pallas_call(
-        joined_grad_body,
-        grid_spec=pltpu.PrefetchScalarGridSpec(
-            num_scalar_prefetch=1,
-            grid=(SHARDS,),
-            in_specs=[whole((rows, width))] + [whole((rows, part))] * 3,
-            out_specs=[
-                pl.BlockSpec(unit, lambda i, idx: (jnp.maximum(i - 2, 0), 0, 0, 0)),
-                pl.BlockSpec(unit, lambda i, idx: (jnp.minimum(i, 1), 0, 0, 0)),
-                whole((2, part)),
-            ],
-        ),
-        out_shape=[
-            jax.ShapeDtypeStruct(grads, bf16),
-            jax.ShapeDtypeStruct(grads, bf16),
-            jax.ShapeDtypeStruct((2, part), f32),
-        ],
-        compiler_params=params(32),
-        cost_estimate=cost(6 * rows * width * part, 2 * rows * width + 6 * rows * part + 6 * width * part),
-        name="joined_grad",
-    )(index, normed, d_q, d_k, d_v)
 
 
 def input_grad_body(index_ref, *refs, blocks):
@@ -916,9 +972,12 @@
 
     @pl.when(step == blocks - 1)
     def _():
+        grads_ref[...] = jnp.zeros_like(grads_ref)
+
         def put(name, shard, value, offset=0):
-            first = VEC[name][0] + offset
-            grads_ref[shard : shard + 1, first : first + value.shape[1]] = value
+            first = shard * VEC_ROWS + VEC[name][0] + offset
+            for i in range(value.shape[1] // LANES):
+                grads_ref[first + i : first + i + 1, :] = value[:, i * LANES : (i + 1) * LANES]
 
         for shard in range(SHARDS):
             cols = slice(shard * 256, (shard + 1) * 256)
@@ -932,7 +991,7 @@
             put("b_qv", shard, source[shard // 2 : shard // 2 + 1, :])
             for chunk in range(CHUNKS):
                 size = bias_refs[chunk].shape[1] // SHARDS
-                put("up_bias", shard, bias_refs[chunk][:, shard * size : (shard + 1) * size], chunk * size)
+                put("up_bias", shard, bias_refs[chunk][:, shard * size : (shard + 1) * size], chunk)
 
 
 def input_gradient(index, parts, weights, tokens, d_middle, vec, sums, bqv, biases, rows_each=256):
@@ -950,15 +1009,15 @@
             grid=(blocks,),
             in_specs=[by_rows(part)] * 6
             + [whole((width, 3 * part))] * 2
-            + [by_rows(width), by_rows(width), whole((SHARDS, VEC_LEN)), whole((8, width))]
+            + [by_rows(width), by_rows(width), whole((SHARDS * VEC_ROWS, LANES)), whole((8, width))]
             + [whole((2, part))] * 2
             + [whole(bias.shape) for bias in biases],
-            out_specs=[by_rows(width), whole((SHARDS, VEC_LEN))],
+            out_specs=[by_rows(width), whole((SHARDS * VEC_ROWS, LANES))],
             scratch_shapes=[pltpu.VMEM((1, width), f32), pltpu.VMEM((1, width), f32)],
         ),
         out_shape=[
             jax.ShapeDtypeStruct((rows, width), f32),
-            jax.ShapeDtypeStruct((SHARDS, VEC_LEN), f32),
+            jax.ShapeDtypeStruct((SHARDS * VEC_ROWS, LANES), f32),
         ],
         compiler_params=params(40),
         cost_estimate=cost(12 * rows * width * part, 10 * rows * width + 12 * rows * part + 12 * width * part),
@@ -1042,9 +1101,16 @@
     size = hidden_size // CHUNKS
     block = size // SHARDS
 
+    def as_rows(value):
+        return value.reshape(-1, LANES)
+
     own_vec = jnp.concatenate(
-        [ln1_gain, ln1_bias, b_qv, attention_out_bias, ln2_gain, ln2_bias, up_bias, down_bias]
-    ).reshape(1, VEC_LEN)
+        [
+            as_rows(value)
+            for value in (ln1_gain, ln1_bias, b_qv, attention_out_bias, ln2_gain, ln2_bias, up_bias, down_bias)
+        ]
+        + [jnp.zeros((VEC_ROWS - 12, LANES), bf16)]
+    )
 
     def joined_cols(which):
         return jnp.concatenate(
@@ -1068,7 +1134,7 @@
     far_vec = moves.across(own_vec)
     near_vec = moves.core(own_vec)
     own_a = joined_cols(0)
-    far_a = moves.across(after(own_a, far_vec))
+    far_a = moves.across(own_a)
     near_a = moves.core(own_a)
     own_b = joined_cols(1)
     half_b = moves.half(own_b)
@@ -1084,40 +1150,42 @@
     hidden_far, hidden_near, hidden_other = [None] * CHUNKS, [None] * CHUNKS, [None] * CHUNKS
     hidden_pieces = [None] * CHUNKS
 
-    def fetch(chunk, earlier):
-        hidden_far[chunk] = moves.across(after(hidden_halves[chunk], earlier))
-        hidden_near[chunk] = moves.core(after(hidden_owns[chunk], earlier))
-
-    def relay(chunk):
+    def fetch(chunk, kernels):
+        hidden_far[chunk] = moves.across(hidden_halves[chunk])
+        hidden_near[chunk] = moves.core(hidden_owns[chunk])
+        moves.by(kernels, hidden_far[chunk], hidden_near[chunk])
+
+    def relay(chunk, kernels):
         hidden_other[chunk] = moves.rep(hidden_far[chunk], 1)
-
-    far_b = moves.across(after(half_b, far_a))
-    near_b = moves.core(after(own_b, far_a))
+        moves.by(kernels, hidden_other[chunk])
+
+    far_b = moves.across(half_b)
+    near_b = moves.core(own_b)
+    moves.by(1, far_b, near_b)
     joined[0], joined_weight[0] = joined_product(
         0, moves.index, (own_a, near_a, far_a, moves.core(far_a)), normed, vec
     )
     moves.ran(joined[0])
-    moves.wait(far_b, near_b)
     other_b = moves.rep(far_b, 1)
-    fetch(0, far_b)
+    moves.by(1, other_b)
+    fetch(0, 1)
     attended[0], totals[0] = attend_forward(0, moves.index, joined[0])
     moves.ran(totals[0])
-    moves.wait(hidden_far[0], hidden_near[0])
-    relay(0)
-    out_far = moves.across(after(out_half, hidden_far[0]))
-    out_near = moves.core(after(attention_out_weight, hidden_far[0]))
+    relay(0, 2)
+    out_far = moves.across(out_half)
+    out_near = moves.core(attention_out_weight)
+    moves.by(1, out_far, out_near)
     joined[1], joined_weight[1] = joined_product(
         1, moves.index, (own_b, near_b, far_b, other_b, moves.core(far_b), moves.core(other_b)), normed, vec
     )
     moves.ran(joined[1])
-    moves.wait(out_far, out_near)
     out_other = moves.rep(out_far, 1)
-    fetch(1, out_far)
+    moves.by(1, out_other)
+    fetch(1, 1)
     attended[1], totals[1] = attend_forward(1, moves.index, joined[1])
     moves.ran(totals[1])
-    moves.wait(hidden_far[1], hidden_near[1])
-    relay(1)
-    fetch(2, hidden_far[1])
+    relay(1, 2)
+    fetch(2, 2)
     middle, normed_two, out_weight = middle_product(
         moves.index,
         (attention_out_weight, out_near, out_far, out_other, moves.core(out_far), moves.core(out_other)),
@@ -1129,7 +1197,9 @@
 
     carried = None
     shard_sums, up_biases = [], []
-    for chunk in range(CHUNKS):
+
+    def hidden_step(chunk):
+        nonlocal carried
         far, other = hidden_far[chunk], hidden_other[chunk]
         hidden_pieces[chunk] = (
             hidden_owns[chunk],
@@ -1144,17 +1214,21 @@
         )
         moves.ran(bias)
         up_biases.append(bias)
-        if chunk + 2 < CHUNKS:
-            moves.wait(hidden_far[chunk + 2], hidden_near[chunk + 2])
-            relay(chunk + 2)
-        if chunk + 3 < CHUNKS:
-            fetch(chunk + 3, hidden_far[chunk + 2])
-        if chunk > 0:
-            shard_sums[chunk - 1].cross()
         shard_sums.append(ShardSum(moves, keep, send))
+
+    fetch(3, 1)
+    hidden_step(0)
+    relay(2, 1)
+    hidden_step(1)
+    relay(3, 1)
+    shard_sums[0].cross(1)
+    hidden_step(2)
+    shard_sums[1].cross(1)
+    hidden_step(3)
+    shard_sums[2].cross(1)
+    first_sum = RepSum(moves, shard_sums[:2])
     all_pieces = [piece for pieces in hidden_pieces for piece in pieces]
     hidden, d_pre = carried
-    moves.wait(shard_sums[0].got)
     d_middle, d_attended, keep, send, sums = block_back(
         moves.index, all_pieces, d_pre, middle, cot, attended, out_weight, vec
     )
@@ -1162,50 +1236,39 @@
     parts, bqv = [], []
 
     def backward(which):
-        grads = attend_backward(which, moves.index, joined[which], attended[which], d_attended, totals[which])
+        *grads, keep, send, bias = attend_backward(
+            which, moves.index, joined[which], attended[which], d_attended, totals[which], normed
+        )
         parts.extend(grads)
-        moves.ran(grads[0])
-
-    def joined_grads(which):
-        keep, send, bias = joined_grad(moves.index, normed, *parts[3 * which :])
         bqv.append(bias)
         moves.ran(bias)
         return ShardSum(moves, keep, send)
 
-    shard_sums[3].cross()
+    shard_sums[3].cross(1)
     out_sum = ShardSum(moves, keep, send)
-    moves.wait(shard_sums[1].got)
-    first_sum = RepSum(moves, shard_sums[:2])
-    backward(0)
-    out_sum.cross()
-    a_sum = joined_grads(0)
     first_sum.split()
-    moves.wait(shard_sums[2].got)
     second_sum = RepSum(moves, shard_sums[2:3])
-    backward(1)
-    a_sum.cross()
+    a_sum = backward(0)
+    out_sum.cross(1)
     first_sum.add()
-    b_sum = joined_grads(1)
-    moves.wait(shard_sums[3].got)
+    second_sum.split()
     third_sum = RepSum(moves, shard_sums[3:4])
-    second_sum.split()
+    b_sum = backward(1)
+    a_sum.cross(1)
     first_sum.spread()
+    second_sum.add()
+    third_sum.split()
     input_grad, vec_grads = input_gradient(
         moves.index, parts, joined_weight, tokens, d_middle, vec, sums, bqv, up_biases
     )
     moves.ran(vec_grads)
-    b_sum.cross()
+    b_sum.cross(1)
+    fourth_sum = RepSum(moves, [out_sum, a_sum])
     first_sum.finish()
-    second_sum.add()
-    third_sum.split()
-    moves.wait(out_sum.got, a_sum.got)
-    fourth_sum = RepSum(moves, [out_sum, a_sum])
+    second_sum.spread()
+    third_sum.add()
     block_out = block_output(moves.index, all_pieces, hidden, middle, vec)
     moves.ran(block_out)
-    second_sum.spread()
-    third_sum.add()
-    fourth_sum.split()
-    last_sum = RepSum(moves, [b_sum])
 
     def place_hidden(chunks, pieces, grads, name):
         plan = []
@@ -1213,25 +1276,30 @@
             plan += [(2 * i, s * block, block, 0, 0, s * size + chunk * block) for s in range(SHARDS)]
             plan += [(2 * i + 1, 0, width, 1, chunk * block, 0)]
         shapes = [(width // SHARDS, hidden_size), (size, width)]
-        return place(moves.index, pieces, plan, shapes, grads, name)
-
-    grads = place_hidden((0, 1), first_sum.pieces(), None, "place_hidden_first")
-    moves.ran(grads[0])
+        grads = place(moves.index, pieces, plan, shapes, grads, name)
+        moves.ran(grads[0])
+        return grads
+
+    last_sum = RepSum(moves, [b_sum])
+    fourth_sum.split()
     second_sum.finish()
     third_sum.spread()
+    vec_sum = VecSum(moves, vec_grads)
+    grads = place_hidden((0, 1), first_sum.pieces(), None, "place_hidden_first")
+    last_sum.split()
     fourth_sum.add()
-    last_sum.split()
-    vec_sum = moves.reduce_vec(vec_grads).reshape(VEC_LEN)
+    third_sum.finish()
+    vec_sum.step()
     grads = place_hidden((2,), second_sum.pieces(), grads, "place_hidden_second")
-    moves.ran(grads[0])
-    third_sum.finish()
+    last_sum.add()
     fourth_sum.spread()
-    last_sum.add()
+    vec_sum.step()
     grad_up, grad_down = place_hidden((3,), third_sum.pieces(), grads, "place_hidden_third")
-    moves.ran(grad_up)
     fourth_sum.finish()
     last_sum.spread()
+    vec_sum.step()
     last_sum.finish()
+    vec_sum = vec_sum.rest()
     third = width // SHARDS
     plan = [(i, 0, half, 0, 0, i * half) for i in range(2)]
     plan += [(2 + i, 0, half, 1, 0, i * width) for i in range(3)]
@@ -1241,8 +1309,8 @@
     (grad_joined,) = place(moves.index, last_sum.pieces(), plan, shapes[1:], (grad_joined,), "place_last")
 
     def vec_part(name):
-        first, length = VEC[name]
-        return vec_sum[first : first + length]
+        first, count = VEC[name]
+        return vec_sum[first : first + count].reshape(count * LANES)
 
     return (
         block_out.reshape(count, seq_len, width),

time: 511 us -> 434 us (0.85)
  waiting for transfers between devices: 147 us -> 72.9 us
  starting transfers between devices: 75.6 us -> 61.1 us
  other arithmetic: 29.1 us -> 37.1 us
    ppermute x80, waiting for transfers between devices: 147 us -> 72.9 us  [flip(): return lax.ppermute(value, axis, [(i, i ^ bit) for i in range(size)])]
    ppermute x80, starting transfers between devices: 75.6 us -> 61.1 us  [flip(): return lax.ppermute(value, axis, [(i, i ^ bit) for i in range(size)])]
    add x7, other arithmetic: 8.6 us -> 14.3 us  [cross(): self.mine = self.keep[0] + self.got[0]]
    reshape x1 -> x8, local copies, waits for them, and re-layouts: 0.01 us -> 5.33 us  [as_rows(): return value.reshape(-1, LANES)]
    unnamed x233 -> x204, local copies, waits for them, and re-layouts: 20.4 us -> 16.3 us
    pallas_call x4 -> x2, Pallas kernels: 41.4 us -> 44.8 us  [attend_backward(): pl.pallas_call(functools.partial(attend_backward_body, half * 2 * pairs,...]
  transfers between devices with their start and end apart: 80 -> 80, of which waited for: 23 -> 22; matrix products, arithmetic and copies ran while one was open for 7% -> 11% of each run, Pallas kernels for 41% -> 51%
where the time goes in v2:
time: 434 us; the launch traced here: 426 us
  Pallas kernels  223 us (51%)
  waiting for transfers between devices  72.9 us (17%)
  starting transfers between devices  61.1 us (14%)
  other arithmetic  37.1 us (9%)
  local copies, waits for them, and re-layouts  29.5 us (7%)
    ppermute x80, waiting for transfers between devices, flip(): return lax.ppermute(value, axis, [(i, i ^ bit) for i in range(size)])  72.9 us
    pallas_call x4, Pallas kernels, hidden_chunk(): pl.pallas_call(functools.partial(hidden_body, chunk, fresh), grid_spec=pl...  69.2 us
    ppermute x80, starting transfers between devices, flip(): return lax.ppermute(value, axis, [(i, i ^ bit) for i in range(size)])  61.1 us
    pallas_call x2, Pallas kernels, attend_backward(): pl.pallas_call(functools.partial(attend_backward_body, half * 2 * pairs,...  44.8 us
    pallas_call x1, Pallas kernels, block_back(): pl.pallas_call(functools.partial(block_back_body, blocks=blocks), grid_sp...  27.1 us
    pallas_call x2, Pallas kernels, attend_forward(): pl.pallas_call(functools.partial(attend_forward_body, half * 2 * pairs),...  24.1 us
    unnamed x204, local copies, waits for them, and re-layouts  16.3 us
    pallas_call x1, Pallas kernels, block_output(): pl.pallas_call(block_out_body, grid_spec=pltpu.PrefetchScalarGridSpec(num...  15 us
  transfers between devices with their start and end apart: 80, of which 22 were waited for; matrix products, arithmetic and copies ran while one was open for 11% of the time, Pallas kernels for 51%

profile of v2, /device:TPU:0, one launch (start us, length us, event | category | flops | bytes accessed | tf_op | source)
XLA Modules:
  0.0 426.1 jit_solution(15562644321830636184)
XLA Ops:
  6.1 3.0 collective-permute-start.1
  9.1 2.3 fusion.13
  13.8 2.5 slice_bitcast_fusion
  16.3 1.8 maximum_bitcast_fusion.1
  25.1 2.2 first_norm.1
  27.3 5.3 %collective-permute-done.6.refs_2_ = bf16[256,1536]{1,0:T(8,128)(2,1)} collective-permute-done((bf16[256,1536]{1,0:T(8,128)(2,1)}, bf16[256,1536]{1,0:T(8,128)(2,1)}, u32[]{:S(2)}, u32[]{:S(2)}) %collective-permute-start.6) | collective-permute-done | bytes 786464 | tf_op jit(solution)/shard_map/ppermute | solution.py:68
  33.4 1.7 collective-permute-done.7.refs_3_
  35.1 6.2 %joined_product.2 = (bf16[1024,1536]{1,0:T(8,128)(2,1)S(1)}, bf16[1024,1536]{1,0:T(8,128)(2,1)S(1)}) custom-call(s32[5]{0:T(128)S(1)} %pad_add_fusion.index_ref.start_ref, bf16[256,1536]{1,0:T(8,128)(2,1)} %pad_maximum_fusion.9.refs_0_, bf16[256,1536]{1,0:T(8,128)(2,1)} %collective-permute-done.5.refs_1_, bf16[256,1536]{1,0:T(8,128)(2,1)} %collective-permute-done.6.refs_2_, ...), custom_call_target="tpu_custom_call" | custom-call | flops 12884901888 | bytes 46137344 | tf_op jit(solution)/shard_map/joined_product/pallas_call | solution.py:319
  46.4 12.1 %attend_forward.2 = (bf16[1024,512]{1,0:T(8,128)(2,1)S(1)}, f32[2,4,2,512]{3,2,1,0:T(2,128)S(1)}) custom-call(s32[5]{0:T(128)S(1)} %pad_add_fusion.index_ref.start_ref, bf16[1024,1536]{1,0:T(8,128)(2,1)S(1)} %get-tuple-element.255.q_ref.k_ref.v_ref, bf16[1024,1536]{1,0:T(8,128)(2,1)S(1)} %get-tuple-element.255.q_ref.k_ref.v_ref, ...), custom_call_target="tpu_custom_call" | custom-call | flops 25769803776 | bytes 16777216 | tf_op jit(solution)/shard_map/attend_forward/pallas_call | solution.py:385
  61.6 5.5 %joined_product.3 = (bf16[1024,1536]{1,0:T(8,128)(2,1)S(1)}, bf16[1024,1536]{1,0:T(8,128)(2,1)S(1)}) custom-call(s32[5]{0:T(128)S(1)} %pad_add_fusion.index_ref.start_ref, bf16[256,1536]{1,0:T(8,128)(2,1)S(1)} %pad_maximum_fusion.8.refs_0_, bf16[256,1536]{1,0:T(8,128)(2,1)S(1)} %collective-permute-done.4.refs_1_, ...), custom_call_target="tpu_custom_call" | custom-call | flops 12884901888 | bytes 46137344 | tf_op jit(solution)/shard_map/joined_product/pallas_call | solution.py:319
  67.1 1.7 copy-done.42
  71.6 12.1 %attend_forward.3 = (bf16[1024,512]{1,0:T(8,128)(2,1)S(1)}, f32[2,4,2,512]{3,2,1,0:T(2,128)S(1)}) custom-call(s32[5]{0:T(128)S(1)} %pad_add_fusion.index_ref.start_ref, bf16[1024,1536]{1,0:T(8,128)(2,1)S(1)} %get-tuple-element.266.q_ref.k_ref.v_ref, bf16[1024,1536]{1,0:T(8,128)(2,1)S(1)} %get-tuple-element.266.q_ref.k_ref.v_ref, ...), custom_call_target="tpu_custom_call" | custom-call | flops 25769803776 | bytes 16777216 | tf_op jit(solution)/shard_map/attend_forward/pallas_call | solution.py:385
  86.2 4.8 %middle_product.1 = (f32[1024,1024]{1,0:T(8,128)S(1)}, bf16[1024,1024]{1,0:T(8,128)(2,1)S(1)}, bf16[1024,1024]{1,0:T(8,128)(2,1)S(1)}) custom-call(s32[5]{0:T(128)S(1)} %pad_add_fusion.index_ref.start_ref, bf16[256,1024]{1,0:T(8,128)(2,1)S(1)} %copy-done.5, bf16[256,1024]{1,0:T(8,128)(2,1)S(1)} %collective-permute-done.12.refs_1_, ...), custom_call_target="tpu_custom_call" | custom-call | flops 8589934592 | bytes 58720256 | tf_op jit(solution)/shard_map/middle_product/pallas_call | solution.py:571
  98.9 17.0 %hidden_chunk0.1 = (bf16[1024,4096]{1,0:T(8,128)(2,1)}, bf16[1024,4096]{1,0:T(8,128)(2,1)}, bf16[2,2,256,1024]{3,2,1,0:T(8,128)(2,1)}, bf16[2,2,256,1024]{3,2,1,0:T(8,128)(2,1)}, f32[1,1024]{1,0:T(1,128)S(1)}) custom-call(s32[5]{0:T(128)S(1)} %pad_add_fusion.index_ref.start_ref, bf16[2,256,1024]{2,1,0:T(8,128)(2,1)S(1)} %pad_maximum_fusion.1.refs_0_, ...), custom_call_target="tpu_custom_call" | custom-call | flops 34359738368 | bytes 100663296 | tf_op jit(solution)/shard_map/hidden_chunk0/pallas_call | solution.py:706
  118.1 3.6 collective-permute-done.24.refs_2_.refs_20_
  121.7 17.6 %hidden_chunk1.1 = (bf16[1024,4096]{1,0:T(8,128)(2,1)}, bf16[1024,4096]{1,0:T(8,128)(2,1)}, bf16[2,2,256,1024]{3,2,1,0:T(8,128)(2,1)}, bf16[2,2,256,1024]{3,2,1,0:T(8,128)(2,1)}, f32[1,1024]{1,0:T(1,128)S(1)}) custom-call(s32[5]{0:T(128)S(1)} %pad_add_fusion.index_ref.start_ref, ...), custom_call_target="tpu_custom_call", output_to_operand_aliasing={{0}: (7, {}), {1}: (8, {})} | custom-call | flops 34359738368 | bytes 100663296 | tf_op jit(solution)/shard_map/hidden_chunk1/pallas_call | solution.py:706
  140.7 3.1 slice_add_fusion.3
  144.8 17.1 %hidden_chunk2.1 = (bf16[1024,4096]{1,0:T(8,128)(2,1)}, bf16[1024,4096]{1,0:T(8,128)(2,1)}, bf16[2,2,256,1024]{3,2,1,0:T(8,128)(2,1)}, bf16[2,2,256,1024]{3,2,1,0:T(8,128)(2,1)}, f32[1,1024]{1,0:T(1,128)S(1)}) custom-call(s32[5]{0:T(128)S(1)} %pad_add_fusion.index_ref.start_ref, ...), custom_call_target="tpu_custom_call", output_to_operand_aliasing={{0}: (7, {}), {1}: (8, {})} | custom-call | flops 34359738368 | bytes 100663296 | tf_op jit(solution)/shard_map/hidden_chunk2/pallas_call | solution.py:706
  162.6 2.5 slice_add_fusion.2
  166.2 3.9 collective-permute-done.34
  170.2 17.5 %hidden_chunk3.1 = (bf16[1024,4096]{1,0:T(8,128)(2,1)}, bf16[1024,4096]{1,0:T(8,128)(2,1)}, bf16[2,2,256,1024]{3,2,1,0:T(8,128)(2,1)}, bf16[2,2,256,1024]{3,2,1,0:T(8,128)(2,1)}, f32[1,1024]{1,0:T(1,128)S(1)}) custom-call(s32[5]{0:T(128)S(1)} %pad_add_fusion.index_ref.start_ref, ...), custom_call_target="tpu_custom_call", output_to_operand_aliasing={{0}: (7, {}), {1}: (8, {})} | custom-call | flops 34359738368 | bytes 100663296 | tf_op jit(solution)/shard_map/hidden_chunk3/pallas_call | solution.py:706
  189.4 2.5 collective-permute-done.38
  196.4 3.0 slice_add_fusion.1
  200.3 27.1 %block_back.1 = (f32[1024,1024]{1,0:T(8,128)}, bf16[1024,1024]{1,0:T(8,128)(2,1)}, bf16[2,2,256,512]{3,2,1,0:T(8,128)(2,1)}, bf16[2,2,256,512]{3,2,1,0:T(8,128)(2,1)}, f32[8,1024]{1,0:T(8,128)S(1)}) custom-call(s32[5]{0:T(128)S(1)} %pad_add_fusion.index_ref.start_ref, bf16[2,256,1024]{2,1,0:T(8,128)(2,1)} %copy-done.1, bf16[2,256,1024]{2,1,0:T(8,128)(2,1)} %copy-done.8, ...), custom_call_target="tpu_custom_call" | custom-call | flops 51539607552 | bytes 134217728 | tf_op jit(solution)/shard_map/block_back/pallas_call | solution.py:851
  233.9 22.4 %attend_backward.2 = (bf16[1024,512]{1,0:T(8,128)(2,1)S(1)}, bf16[1024,512]{1,0:T(8,128)(2,1)S(1)}, bf16[1024,512]{1,0:T(8,128)(2,1)S(1)}, bf16[2,3,256,512]{3,2...) custom-call(s32[5]{0:T(128)S(1)} %pad_add_fusion.index_ref.start_ref, ...), custom_call_target="tpu_custom_call" | custom-call | flops 51539607552 | bytes 33554432 | tf_op jit(solution)/shard_map/attend_backward/pallas_call | solution.py:504
  258.9 2.6 collective-permute-start.50
  268.2 22.4 %attend_backward.3 = (bf16[1024,512]{1,0:T(8,128)(2,1)S(1)}, bf16[1024,512]{1,0:T(8,128)(2,1)S(1)}, bf16[1024,512]{1,0:T(8,128)(2,1)S(1)}, bf16[2,3,256,512]{3,2...) custom-call(s32[5]{0:T(128)S(1)} %pad_add_fusion.index_ref.start_ref, ...), custom_call_target="tpu_custom_call" | custom-call | flops 51539607552 | bytes 33554432 | tf_op jit(solution)/shard_map/attend_backward/pallas_call | solution.py:504
  296.4 2.1 dynamic-slice_add_fusion
  302.6 13.0 %input_gradient.1 = (f32[1024,1024]{1,0:T(8,128)}, f32[64,256]{1,0:T(8,128)S(1)}) custom-call(s32[5]{0:T(128)S(1)} %pad_add_fusion.index_ref.start_ref, bf16[1024,512]{1,0:T(8,128)(2,1)S(1)} %get-tuple-element.385.refs_0_, bf16[1024,512]{1,0:T(8,128)(2,1)S(1)} %copy-done.50, bf16[1024,512]{1,0:T(8,128)(2,1)S(1)} %copy-done.52, ...), custom_call_target="tpu_custom_call" | custom-call | flops 25769803776 | bytes 92274688 | tf_op jit(solution)/shard_map/input_gradient/pallas_call | solution.py:1005
  320.7 10.2 %collective-permute-done.57 = bf16[2,64,1024]{2,1,0:T(8,128)(2,1)S(1)} collective-permute-done((bf16[2,64,1024]{2,1,0:T(8,128)(2,1)}, bf16[2,64,1024]{2,1,0:T(8,128)(2,1)S(1)}, u32[]{:S(2)}, u32[]{:S(2)}) %collective-permute-start.57) | collective-permute-done | bytes 262176 | tf_op jit(solution)/shard_map/ppermute | solution.py:68
  330.9 2.7 collective-permute-start.63
  337.3 15.0 %block_output.1 = bf16[1024,1024]{1,0:T(8,128)(2,1)} custom-call(s32[5]{0:T(128)S(1)} %pad_add_fusion.index_ref.start_ref, bf16[2,256,1024]{2,1,0:T(8,128)(2,1)} %copy-done.1, bf16[2,256,1024]{2,1,0:T(8,128)(2,1)} %copy-done.8, bf16[2,128,1024]{2,1,0:T(8,128)(2,1)S(1)} %copy-done.14, bf16[2,128,1024]{2,1,0:T(8,128)(2,1)S(1)} %copy-done.16, ...), custom_call_target="tpu_custom_call" | custom-call | flops 34359738368 | bytes 92274688 | tf_op jit(solution)/shard_map/block_output/pallas_call | solution.py:933
  352.9 4.8 %collective-permute-done.60 = bf16[5,128,512]{2,1,0:T(8,128)(2,1)S(1)} collective-permute-done((bf16[5,128,512]{2,1,0:T(8,128)(2,1)S(1)}, bf16[5,128,512]{2,1,0:T(8,128)(2,1)S(1)}, u32[]{:S(2)}, u32[]{:S(2)}) %collective-permute-start.60) | collective-permute-done | bytes 655392 | tf_op jit(solution)/shard_map/ppermute | solution.py:68
  360.9 2.9 place_hidden_first.1
  363.8 2.5 collective-permute-done.66
  366.5 3.2 collective-permute-start.71
  372.6 9.5 %collective-permute-done.67.other_ref = bf16[2,2,64,1024]{3,2,1,0:T(8,128)(2,1)S(1)} collective-permute-done((bf16[2,2,64,1024]{3,2,1,0:T(8,128)(2,1)S(1)}, bf16[2,2,64,1024]{3,2,1,0:T(8,128)(2,1)S(1)}, u32[]{:S(2)}, u32[]{:S(2)}) %collective-permute-start.67) | collective-permute-done | bytes 524320 | tf_op jit(solution)/shard_map/ppermute | solution.py:68
  382.1 2.0 place_hidden_second.1
  387.0 3.1 collective-permute-done.64
  390.2 2.7 collective-permute-start.75
  393.4 2.0 place_hidden_third.1
  397.0 3.3 collective-permute-done.73
  400.7 4.5 %collective-permute-done.74 = f32[16,256]{1,0:T(8,128)S(1)} collective-permute-done((f32[16,256]{1,0:T(8,128)S(1)}, f32[16,256]{1,0:T(8,128)S(1)}, u32[]{:S(2)}, u32[]{:S(2)}) %collective-permute-start.74) | collective-permute-done | bytes 16416 | tf_op jit(solution)/shard_map/ppermute | solution.py:68
  407.1 4.5 %collective-permute-done.77 = bf16[3,64,512]{2,1,0:T(8,128)(2,1)S(1)} collective-permute-done((bf16[3,64,512]{2,1,0:T(8,128)(2,1)S(1)}, bf16[3,64,512]{2,1,0:T(8,128)(2,1)S(1)}, u32[]{:S(2)}, u32[]{:S(2)}) %collective-permute-start.77) | collective-permute-done | bytes 196640 | tf_op jit(solution)/shard_map/ppermute | solution.py:68
  414.4 5.2 %collective-permute-done.78.other_ref = bf16[2,5,64,512]{3,2,1,0:T(8,128)(2,1)S(1)} collective-permute-done((bf16[2,5,64,512]{3,2,1,0:T(8,128)(2,1)S(1)}, bf16[2,5,64,512]{3,2,1,0:T(8,128)(2,1)S(1)}, u32[]{:S(2)}, u32[]{:S(2)}) %collective-permute-start.78) | collective-permute-done | bytes 655392 | tf_op jit(solution)/shard_map/ppermute | solution.py:68
  419.6 2.2 place_fourth.1
  421.8 2.0 collective-permute-done.79.other_ref
  423.8 1.8 place_last.1
  (407 shorter events, 100.9 us)
Async XLA Ops:
  6.1 17.8 %collective-permute-start.1 = (bf16[16,256]{1,0:T(8,128)(2,1)S(1)}, bf16[16,256]{1,0:T(8,128)(2,1)S(1)}, u32[]{:S(2)}, u32[]{:S(2)}) collective-permute-start(bf16[16,256]{1,0:T(8,128)(2,1)S(1)} %concatenate.42.own_ref), channel_id=1, source_target_pairs={{0,16},{8,24},{16,0},{24,8},{1,17},{9,25},{17,1},{25,9},{2,18},{10... | collective-permute-start | bytes 24584 | tf_op jit(solution)/shard_map/ppermute | solution.py:68
  9.1 15.1 %collective-permute-start = (bf16[16,256]{1,0:T(8,128)(2,1)S(1)}, bf16[16,256]{1,0:T(8,128)(2,1)S(1)}, u32[]{:S(2)}, u32[]{:S(2)}) collective-permute-start(bf16[16,256]{1,0:T(8,128)(2,1)S(1)} %concatenate.42.own_ref), channel_id=1, source_target_pairs={{0,8},{8,0},{16,24},{24,16},{1,9},{9,1},{17,25},{25,17},{2,10},{10... | collective-permute-start | bytes 24584 | tf_op jit(solution)/shard_map/ppermute | solution.py:68
  12.3 20.3 %collective-permute-start.6 = (bf16[256,1536]{1,0:T(8,128)(2,1)}, bf16[256,1536]{1,0:T(8,128)(2,1)}, u32[]{:S(2)}, u32[]{:S(2)}) collective-permute-start(bf16[256,1536]{1,0:T(8,128)(2,1)} %pad_maximum_fusion.9.refs_0_), channel_id=1, source_target_pairs={{0,16},{8,24},{16,0},{24,8},{1,17},{9,25},{17,1},{25,9},{2,18},{10... | collective-permute-start | bytes 2359304 | tf_op jit(solution)/shard_map/ppermute | solution.py:68
  12.5 20.8 %collective-permute-start.5 = (bf16[256,1536]{1,0:T(8,128)(2,1)}, bf16[256,1536]{1,0:T(8,128)(2,1)}, u32[]{:S(2)}, u32[]{:S(2)}) collective-permute-start(bf16[256,1536]{1,0:T(8,128)(2,1)} %pad_maximum_fusion.9.refs_0_), channel_id=1, source_target_pairs={{0,8},{8,0},{16,24},{24,16},{1,9},{9,1},{17,25},{25,17},{2,10},{10... | collective-permute-start | bytes 2359304 | tf_op jit(solution)/shard_map/ppermute | solution.py:68
  44.3 14.4 %collective-permute-start.8 = (bf16[128,1536]{1,0:T(8,128)(2,1)S(1)}, bf16[128,1536]{1,0:T(8,128)(2,1)S(1)}, u32[]{:S(2)}, u32[]{:S(2)}) collective-permute-start(bf16[128,1536]{1,0:T(8,128)(2,1)S(1)} %collective-permute-done.3.refs_2_), channel_id=1, source_target_pairs={{0,1},{1,0},{2,3},{3,2},{4,5},{5,4},{6,7},{7,6},{8,9},{9,8},{10,11... | collective-permute-start | bytes 1179656 | tf_op jit(solution)/shard_map/ppermute | solution.py:68
  45.8 15.3 %collective-permute-start.10 = (bf16[2,256,1024]{2,1,0:T(8,128)(2,1)S(1)}, bf16[2,256,1024]{2,1,0:T(8,128)(2,1)S(1)}, u32[]{:S(2)}, u32[]{:S(2)}) collective-permute-start(bf16[2,256,1024]{2,1,0:T(8,128)(2,1)S(1)} %pad_maximum_fusion.1.refs_0_), channel_id=1, source_target_pairs={{0,8},{8,0},{16,24},{24,16},{1,9},{9,1},{17,25},{25,17},{2,10},{10... | collective-permute-start | bytes 3145736 | tf_op jit(solution)/shard_map/ppermute | solution.py:68
  61.1 23.7 %collective-permute-start.15 = (bf16[2,128,1024]{2,1,0:T(8,128)(2,1)S(1)}, bf16[2,128,1024]{2,1,0:T(8,128)(2,1)S(1)}, u32[]{:S(2)}, u32[]{:S(2)}) collective-permute-start(bf16[2,128,1024]{2,1,0:T(8,128)(2,1)S(1)} %collective-permute-done.9.refs_2_), channel_id=1, source_target_pairs={{0,1},{1,0},{2,3},{3,2},{4,5},{5,4},{6,7},{7,6},{8,9},{9,8},{10,11... | collective-permute-start | bytes 1572872 | tf_op jit(solution)/shard_map/ppermute | solution.py:68
  68.8 15.6 %collective-permute-start.16 = (bf16[128,1024]{1,0:T(8,128)(2,1)S(1)}, bf16[128,1024]{1,0:T(8,128)(2,1)S(1)}, u32[]{:S(2)}, u32[]{:S(2)}) collective-permute-start(bf16[128,1024]{1,0:T(8,128)(2,1)S(1)} %collective-permute-done.11.refs_2_), channel_id=1, source_target_pairs={{0,1},{1,0},{2,3},{3,2},{4,5},{5,4},{6,7},{7,6},{8,9},{9,8},{10,11... | collective-permute-start | bytes 786440 | tf_op jit(solution)/shard_map/ppermute | solution.py:68
  95.9 20.6 %collective-permute-start.23 = (bf16[2,256,1024]{2,1,0:T(8,128)(2,1)S(1)}, bf16[2,256,1024]{2,1,0:T(8,128)(2,1)S(1)}, u32[]{:S(2)}, u32[]{:S(2)}) collective-permute-start(bf16[2,256,1024]{2,1,0:T(8,128)(2,1)S(1)} %pad_maximum_fusion.3.refs_0_.refs_12_), channel_id=1, source_target_pairs={{0,8},{8,0},{16,24},{24,16},{1,9},{9,1},{17,25},{25,17},{2,10},{10... | collective-permute-start | bytes 3145736 | tf_op jit(solution)/shard_map/ppermute | solution.py:68
  96.3 19.9 %collective-permute-start.22 = (bf16[2,128,1024]{2,1,0:T(8,128)(2,1)S(1)}, bf16[2,128,1024]{2,1,0:T(8,128)(2,1)S(1)}, u32[]{:S(2)}, u32[]{:S(2)}) collective-permute-start(bf16[2,128,1024]{2,1,0:T(8,128)(2,1)S(1)} %copy-done.94), channel_id=1, source_target_pairs={{0,16},{8,24},{16,0},{24,8},{1,17},{9,25},{17,1},{25,9},{2,18},{10... | collective-permute-start | bytes 1572872 | tf_op jit(solution)/shard_map/ppermute | solution.py:68
  97.1 18.8 %collective-permute-start.21 = (bf16[2,128,1024]{2,1,0:T(8,128)(2,1)S(1)}, bf16[2,128,1024]{2,1,0:T(8,128)(2,1)S(1)}, u32[]{:S(2)}, u32[]{:S(2)}) collective-permute-start(bf16[2,128,1024]{2,1,0:T(8,128)(2,1)S(1)} %collective-permute-done.17.refs_2_.refs_8_), channel_id=1, source_target_pairs={{0,1},{1,0},{2,3},{3,2},{4,5},{5,4},{6,7},{7,6},{8,9},{9,8},{10,11... | collective-permute-start | bytes 1572872 | tf_op jit(solution)/shard_map/ppermute | solution.py:68
  97.6 24.0 %collective-permute-start.25 = (bf16[2,256,1024]{2,1,0:T(8,128)(2,1)S(1)}, bf16[2,256,1024]{2,1,0:T(8,128)(2,1)S(1)}, u32[]{:S(2)}, u32[]{:S(2)}) collective-permute-start(bf16[2,256,1024]{2,1,0:T(8,128)(2,1)S(1)} %pad_maximum_fusion.4.refs_0_.refs_18_), channel_id=1, source_target_pairs={{0,8},{8,0},{16,24},{24,16},{1,9},{9,1},{17,25},{25,17},{2,10},{10... | collective-permute-start | bytes 3145736 | tf_op jit(solution)/shard_map/ppermute | solution.py:68
  97.7 23.9 %collective-permute-start.24 = (bf16[2,128,1024]{2,1,0:T(8,128)(2,1)S(1)}, bf16[2,128,1024]{2,1,0:T(8,128)(2,1)}, u32[]{:S(2)}, u32[]{:S(2)}) collective-permute-start(bf16[2,128,1024]{2,1,0:T(8,128)(2,1)S(1)} %copy-done.93), channel_id=1, source_target_pairs={{0,16},{8,24},{16,0},{24,8},{1,17},{9,25},{17,1},{25,9},{2,18},{10... | collective-permute-start | bytes 1572872 | tf_op jit(solution)/shard_map/ppermute | solution.py:68
  116.5 22.8 %collective-permute-start.29 = (bf16[2,128,1024]{2,1,0:T(8,128)(2,1)S(1)}, bf16[2,128,1024]{2,1,0:T(8,128)(2,1)S(1)}, u32[]{:S(2)}, u32[]{:S(2)}) collective-permute-start(bf16[2,128,1024]{2,1,0:T(8,128)(2,1)S(1)} %collective-permute-done.22.refs_2_.refs_14_), channel_id=1, source_target_pairs={{0,1},{1,0},{2,3},{3,2},{4,5},{5,4},{6,7},{7,6},{8,9},{9,8},{10,11... | collective-permute-start | bytes 1572872 | tf_op jit(solution)/shard_map/ppermute | solution.py:68
  121.6 19.1 %collective-permute-start.28 = (bf16[2,2,256,1024]{3,2,1,0:T(8,128)(2,1)}, bf16[2,2,256,1024]{3,2,1,0:T(8,128)(2,1)}, u32[]{:S(2)}, u32[]{:S(2)}) collective-permute-start(bf16[2,2,256,1024]{3,2,1,0:T(8,128)(2,1)} %get-tuple-element.290), channel_id=1, source_target_pairs={{0,8},{8,0},{16,24},{24,16},{1,9},{9,1},{17,25},{25,17},{2,10},{10... | collective-permute-start | bytes 6291464 | tf_op jit(solution)/shard_map/ppermute | solution.py:68
  140.0 21.9 %collective-permute-start.33 = (bf16[2,128,1024]{2,1,0:T(8,128)(2,1)}, bf16[2,128,1024]{2,1,0:T(8,128)(2,1)}, u32[]{:S(2)}, u32[]{:S(2)}) collective-permute-start(bf16[2,128,1024]{2,1,0:T(8,128)(2,1)} %collective-permute-done.24.refs_2_.refs_20_), channel_id=1, source_target_pairs={{0,1},{1,0},{2,3},{3,2},{4,5},{5,4},{6,7},{7,6},{8,9},{9,8},{10,11... | collective-permute-start | bytes 1572872 | tf_op jit(solution)/shard_map/ppermute | solution.py:68
  140.5 22.0 %collective-permute-start.32 = (bf16[2,2,256,1024]{3,2,1,0:T(8,128)(2,1)}, bf16[2,2,256,1024]{3,2,1,0:T(8,128)(2,1)}, u32[]{:S(2)}, u32[]{:S(2)}) collective-permute-start(bf16[2,2,256,1024]{3,2,1,0:T(8,128)(2,1)} %get-tuple-element.302), channel_id=1, source_target_pairs={{0,8},{8,0},{16,24},{24,16},{1,9},{9,1},{17,25},{25,17},{2,10},{10... | collective-permute-start | bytes 6291464 | tf_op jit(solution)/shard_map/ppermute | solution.py:68
  143.8 26.3 %collective-permute-start.34 = (bf16[2,256,1024]{2,1,0:T(8,128)(2,1)}, bf16[2,256,1024]{2,1,0:T(8,128)(2,1)}, u32[]{:S(2)}, u32[]{:S(2)}) collective-permute-start(bf16[2,256,1024]{2,1,0:T(8,128)(2,1)} %get-tuple-element.304), channel_id=1, source_target_pairs={{0,16},{8,24},{16,0},{24,8},{1,17},{9,25},{17,1},{25,9},{2,18},{10... | collective-permute-start | bytes 3145736 | tf_op jit(solution)/shard_map/ppermute | solution.py:68
  162.5 32.5 %collective-permute-start.37 = (bf16[2,2,256,1024]{3,2,1,0:T(8,128)(2,1)}, bf16[2,2,256,1024]{3,2,1,0:T(8,128)(2,1)S(1)}, u32[]{:S(2)}, u32[]{:S(2)}) collective-permute-start(bf16[2,2,256,1024]{3,2,1,0:T(8,128)(2,1)} %get-tuple-element.315), channel_id=1, source_target_pairs={{0,8},{8,0},{16,24},{24,16},{1,9},{9,1},{17,25},{25,17},{2,10},{10... | collective-permute-start | bytes 6291464 | tf_op jit(solution)/shard_map/ppermute | solution.py:68
  165.0 26.9 %collective-permute-start.38 = (bf16[2,256,1024]{2,1,0:T(8,128)(2,1)S(1)}, bf16[2,256,1024]{2,1,0:T(8,128)(2,1)S(1)}, u32[]{:S(2)}, u32[]{:S(2)}) collective-permute-start(bf16[2,256,1024]{2,1,0:T(8,128)(2,1)S(1)} %get-tuple-element.316), channel_id=1, source_target_pairs={{0,16},{8,24},{16,0},{24,8},{1,17},{9,25},{17,1},{25,9},{2,18},{10... | collective-permute-start | bytes 3145736 | tf_op jit(solution)/shard_map/ppermute | solution.py:68
  187.7 42.7 %collective-permute-start.41 = (bf16[2,2,256,1024]{3,2,1,0:T(8,128)(2,1)}, bf16[2,2,256,1024]{3,2,1,0:T(8,128)(2,1)S(1)}, u32[]{:S(2)}, u32[]{:S(2)}) collective-permute-start(bf16[2,2,256,1024]{3,2,1,0:T(8,128)(2,1)} %get-tuple-element.330), channel_id=1, source_target_pairs={{0,8},{8,0},{16,24},{24,16},{1,9},{9,1},{17,25},{25,17},{2,10},{10... | collective-permute-start | bytes 6291464 | tf_op jit(solution)/shard_map/ppermute | solution.py:68
  193.4 34.1 %collective-permute-start.43 = (bf16[4,128,1024]{2,1,0:T(8,128)(2,1)}, bf16[4,128,1024]{2,1,0:T(8,128)(2,1)S(1)}, u32[]{:S(2)}, u32[]{:S(2)}) collective-permute-start(bf16[4,128,1024]{2,1,0:T(8,128)(2,1)} %pad_maximum_fusion.5), channel_id=1, source_target_pairs={{0,1},{1,0},{2,3},{3,2},{4,5},{5,4},{6,7},{7,6},{8,9},{9,8},{10,11... | collective-permute-start | bytes 3145736 | tf_op jit(solution)/shard_map/ppermute | solution.py:68
  199.4 31.0 %collective-permute-start.42 = (bf16[2,256,1024]{2,1,0:T(8,128)(2,1)}, bf16[2,256,1024]{2,1,0:T(8,128)(2,1)S(1)}, u32[]{:S(2)}, u32[]{:S(2)}) collective-permute-start(bf16[2,256,1024]{2,1,0:T(8,128)(2,1)} %get-tuple-element.331), channel_id=1, source_target_pairs={{0,16},{8,24},{16,0},{24,8},{1,17},{9,25},{17,1},{25,9},{2,18},{10... | collective-permute-start | bytes 3145736 | tf_op jit(solution)/shard_map/ppermute | solution.py:68
  227.5 31.4 %collective-permute-start.45 = (bf16[2,2,256,512]{3,2,1,0:T(8,128)(2,1)}, bf16[2,2,256,512]{3,2,1,0:T(8,128)(2,1)S(1)}, u32[]{:S(2)}, u32[]{:S(2)}) collective-permute-start(bf16[2,2,256,512]{3,2,1,0:T(8,128)(2,1)} %get-tuple-element.347), channel_id=1, source_target_pairs={{0,8},{8,0},{16,24},{24,16},{1,9},{9,1},{17,25},{25,17},{2,10},{10... | collective-permute-start | bytes 3145736 | tf_op jit(solution)/shard_map/ppermute | solution.py:68
  228.8 27.5 %collective-permute-start.46 = (bf16[4,64,1024]{2,1,0:T(8,128)(2,1)}, bf16[4,64,1024]{2,1,0:T(8,128)(2,1)S(1)}, u32[]{:S(2)}, u32[]{:S(2)}) collective-permute-start(bf16[4,64,1024]{2,1,0:T(8,128)(2,1)} %get-tuple-element.348), channel_id=1, source_target_pairs={{0,2},{1,3},{2,0},{3,1},{4,6},{5,7},{6,4},{7,5},{8,10},{9,11},{10,... | collective-permute-start | bytes 1572872 | tf_op jit(solution)/shard_map/ppermute | solution.py:68
  232.2 33.2 %collective-permute-start.44 = (bf16[2,256,1024]{2,1,0:T(8,128)(2,1)}, bf16[2,256,1024]{2,1,0:T(8,128)(2,1)S(1)}, u32[]{:S(2)}, u32[]{:S(2)}) collective-permute-start(bf16[2,256,1024]{2,1,0:T(8,128)(2,1)} %get-tuple-element.345), channel_id=1, source_target_pairs={{0,16},{8,24},{16,0},{24,8},{1,17},{9,25},{17,1},{25,9},{2,18},{10... | collective-permute-start | bytes 3145736 | tf_op jit(solution)/shard_map/ppermute | solution.py:68
  233.3 30.3 %collective-permute-start.47 = (bf16[2,128,1024]{2,1,0:T(8,128)(2,1)S(1)}, bf16[2,128,1024]{2,1,0:T(8,128)(2,1)}, u32[]{:S(2)}, u32[]{:S(2)}) collective-permute-start(bf16[2,128,1024]{2,1,0:T(8,128)(2,1)S(1)} %get-tuple-element.349), channel_id=1, source_target_pairs={{0,1},{1,0},{2,3},{3,2},{4,5},{5,4},{6,7},{7,6},{8,9},{9,8},{10,11... | collective-permute-start | bytes 1572872 | tf_op jit(solution)/shard_map/ppermute | solution.py:68
  258.9 33.8 %collective-permute-start.50 = (bf16[4,64,1024]{2,1,0:T(8,128)(2,1)S(1)}, bf16[4,64,1024]{2,1,0:T(8,128)(2,1)}, u32[]{:S(2)}, u32[]{:S(2)}) collective-permute-start(bf16[4,64,1024]{2,1,0:T(8,128)(2,1)S(1)} %add.277), channel_id=1, source_target_pairs={{0,4},{1,5},{2,6},{3,7},{4,0},{5,1},{6,2},{7,3},{8,12},{9,13},{10,... | collective-permute-start | bytes 1572872 | tf_op jit(solution)/shard_map/ppermute | solution.py:68
  261.5 34.9 %collective-permute-start.48 = (bf16[2,3,256,512]{3,2,1,0:T(8,128)(2,1)S(1)}, bf16[2,3,256,512]{3,2,1,0:T(8,128)(2,1)}, u32[]{:S(2)}, u32[]{:S(2)}) collective-permute-start(bf16[2,3,256,512]{3,2,1,0:T(8,128)(2,1)S(1)} %get-tuple-element.363), channel_id=1, source_target_pairs={{0,8},{8,0},{16,24},{24,16},{1,9},{9,1},{17,25},{25,17},{2,10},{10... | collective-permute-start | bytes 4718600 | tf_op jit(solution)/shard_map/ppermute | solution.py:68
  262.6 35.9 %collective-permute-start.49 = (bf16[2,256,512]{2,1,0:T(8,128)(2,1)}, bf16[2,256,512]{2,1,0:T(8,128)(2,1)}, u32[]{:S(2)}, u32[]{:S(2)}) collective-permute-start(bf16[2,256,512]{2,1,0:T(8,128)(2,1)} %get-tuple-element.364), channel_id=1, source_target_pairs={{0,16},{8,24},{16,0},{24,8},{1,17},{9,25},{17,1},{25,9},{2,18},{10... | collective-permute-start | bytes 1572872 | tf_op jit(solution)/shard_map/ppermute | solution.py:68
  264.8 27.8 %collective-permute-start.51 = (bf16[2,64,1024]{2,1,0:T(8,128)(2,1)S(1)}, bf16[2,64,1024]{2,1,0:T(8,128)(2,1)S(1)}, u32[]{:S(2)}, u32[]{:S(2)}) collective-permute-start(bf16[2,64,1024]{2,1,0:T(8,128)(2,1)S(1)} %get-tuple-element.366), channel_id=1, source_target_pairs={{0,2},{1,3},{2,0},{3,1},{4,6},{5,7},{6,4},{7,5},{8,10},{9,11},{10,... | collective-permute-start | bytes 786440 | tf_op jit(solution)/shard_map/ppermute | solution.py:68
  266.8 29.6 %collective-permute-start.52 = (bf16[2,128,1024]{2,1,0:T(8,128)(2,1)}, bf16[2,128,1024]{2,1,0:T(8,128)(2,1)}, u32[]{:S(2)}, u32[]{:S(2)}) collective-permute-start(bf16[2,128,1024]{2,1,0:T(8,128)(2,1)} %get-tuple-element.367), channel_id=1, source_target_pairs={{0,1},{1,0},{2,3},{3,2},{4,5},{5,4},{6,7},{7,6},{8,9},{9,8},{10,11... | collective-permute-start | bytes 1572872 | tf_op jit(solution)/shard_map/ppermute | solution.py:68
  294.4 21.3 %collective-permute-start.56 = (bf16[2,64,1024]{2,1,0:T(8,128)(2,1)S(1)}, bf16[2,64,1024]{2,1,0:T(8,128)(2,1)}, u32[]{:S(2)}, u32[]{:S(2)}) collective-permute-start(bf16[2,64,1024]{2,1,0:T(8,128)(2,1)S(1)} %add.286), channel_id=1, source_target_pairs={{0,4},{1,5},{2,6},{3,7},{4,0},{5,1},{6,2},{7,3},{8,12},{9,13},{10,... | collective-permute-start | bytes 786440 | tf_op jit(solution)/shard_map/ppermute | solution.py:68
  294.8 24.1 %collective-permute-start.55 = (bf16[4,64,1024]{2,1,0:T(8,128)(2,1)S(1)}, bf16[4,64,1024]{2,1,0:T(8,128)(2,1)S(1)}, u32[]{:S(2)}, u32[]{:S(2)}) collective-permute-start(bf16[4,64,1024]{2,1,0:T(8,128)(2,1)S(1)} %add.285), channel_id=1, source_target_pairs={{0,2},{1,3},{2,0},{3,1},{4,6},{5,7},{6,4},{7,5},{8,10},{9,11},{10,... | collective-permute-start | bytes 1572872 | tf_op jit(solution)/shard_map/ppermute | solution.py:68
  296.3 38.2 %collective-permute-start.53 = (bf16[2,3,256,512]{3,2,1,0:T(8,128)(2,1)S(1)}, bf16[2,3,256,512]{3,2,1,0:T(8,128)(2,1)}, u32[]{:S(2)}, u32[]{:S(2)}) collective-permute-start(bf16[2,3,256,512]{3,2,1,0:T(8,128)(2,1)S(1)} %get-tuple-element.380), channel_id=1, source_target_pairs={{0,8},{8,0},{16,24},{24,16},{1,9},{9,1},{17,25},{25,17},{2,10},{10... | collective-permute-start | bytes 4718600 | tf_op jit(solution)/shard_map/ppermute | solution.py:68
  300.2 33.4 %collective-permute-start.54 = (bf16[3,256,512]{2,1,0:T(8,128)(2,1)S(1)}, bf16[3,256,512]{2,1,0:T(8,128)(2,1)S(1)}, u32[]{:S(2)}, u32[]{:S(2)}) collective-permute-start(bf16[3,256,512]{2,1,0:T(8,128)(2,1)S(1)} %get-tuple-element.381), channel_id=1, source_target_pairs={{0,16},{8,24},{16,0},{24,8},{1,17},{9,25},{17,1},{25,9},{2,18},{10... | collective-permute-start | bytes 2359304 | tf_op jit(solution)/shard_map/ppermute | solution.py:68
  316.7 35.5 %collective-permute-start.62 = (bf16[2,64,1024]{2,1,0:T(8,128)(2,1)S(1)}, bf16[2,64,1024]{2,1,0:T(8,128)(2,1)S(1)}, u32[]{:S(2)}, u32[]{:S(2)}) collective-permute-start(bf16[2,64,1024]{2,1,0:T(8,128)(2,1)S(1)} %add.297), channel_id=1, source_target_pairs={{0,2},{1,3},{2,0},{3,1},{4,6},{5,7},{6,4},{7,5},{8,10},{9,11},{10,... | collective-permute-start | bytes 786440 | tf_op jit(solution)/shard_map/ppermute | solution.py:68
  319.0 42.0 %collective-permute-start.61 = (bf16[2,4,64,1024]{3,2,1,0:T(8,128)(2,1)S(1)}, bf16[2,4,64,1024]{3,2,1,0:T(8,128)(2,1)S(1)}, u32[]{:S(2)}, u32[]{:S(2)}) collective-permute-start(bf16[2,4,64,1024]{3,2,1,0:T(8,128)(2,1)S(1)} %pad_maximum_fusion.6.pair_ref), channel_id=1, source_target_pairs={{0,1},{1,0},{2,3},{3,2},{4,5},{5,4},{6,7},{7,6},{8,9},{9,8},{10,11... | collective-permute-start | bytes 3145736 | tf_op jit(solution)/shard_map/ppermute | solution.py:68
  330.9 21.4 %collective-permute-start.63 = (bf16[2,64,1024]{2,1,0:T(8,128)(2,1)S(1)}, bf16[2,64,1024]{2,1,0:T(8,128)(2,1)S(1)}, u32[]{:S(2)}, u32[]{:S(2)}) collective-permute-start(bf16[2,64,1024]{2,1,0:T(8,128)(2,1)S(1)} %add.298), channel_id=1, source_target_pairs={{0,4},{1,5},{2,6},{3,7},{4,0},{5,1},{6,2},{7,3},{8,12},{9,13},{10,... | collective-permute-start | bytes 786440 | tf_op jit(solution)/shard_map/ppermute | solution.py:68
  333.9 23.9 %collective-permute-start.60 = (bf16[5,128,512]{2,1,0:T(8,128)(2,1)S(1)}, bf16[5,128,512]{2,1,0:T(8,128)(2,1)S(1)}, u32[]{:S(2)}, u32[]{:S(2)}) collective-permute-start(bf16[5,128,512]{2,1,0:T(8,128)(2,1)S(1)} %pad_maximum_fusion.10), channel_id=1, source_target_pairs={{0,1},{1,0},{2,3},{3,2},{4,5},{5,4},{6,7},{7,6},{8,9},{9,8},{10,11... | collective-permute-start | bytes 1966088 | tf_op jit(solution)/shard_map/ppermute | solution.py:68
  336.2 22.3 %collective-permute-start.59 = (bf16[3,256,512]{2,1,0:T(8,128)(2,1)S(1)}, bf16[3,256,512]{2,1,0:T(8,128)(2,1)S(1)}, u32[]{:S(2)}, u32[]{:S(2)}) collective-permute-start(bf16[3,256,512]{2,1,0:T(8,128)(2,1)S(1)} %get-tuple-element.411), channel_id=1, source_target_pairs={{0,16},{8,24},{16,0},{24,8},{1,17},{9,25},{17,1},{25,9},{2,18},{10... | collective-permute-start | bytes 2359304 | tf_op jit(solution)/shard_map/ppermute | solution.py:68
  359.4 22.6 %collective-permute-start.67 = (bf16[2,2,64,1024]{3,2,1,0:T(8,128)(2,1)S(1)}, bf16[2,2,64,1024]{3,2,1,0:T(8,128)(2,1)S(1)}, u32[]{:S(2)}, u32[]{:S(2)}) collective-permute-start(bf16[2,2,64,1024]{3,2,1,0:T(8,128)(2,1)S(1)} %pad_maximum_fusion.12.pair_ref), channel_id=1, source_target_pairs={{0,1},{1,0},{2,3},{3,2},{4,5},{5,4},{6,7},{7,6},{8,9},{9,8},{10,11... | collective-permute-start | bytes 1572872 | tf_op jit(solution)/shard_map/ppermute | solution.py:68
  366.5 17.6 %collective-permute-start.71 = (bf16[5,64,512]{2,1,0:T(8,128)(2,1)S(1)}, bf16[5,64,512]{2,1,0:T(8,128)(2,1)S(1)}, u32[]{:S(2)}, u32[]{:S(2)}) collective-permute-start(bf16[5,64,512]{2,1,0:T(8,128)(2,1)S(1)} %add.308), channel_id=1, source_target_pairs={{0,4},{1,5},{2,6},{3,7},{4,0},{5,1},{6,2},{7,3},{8,12},{9,13},{10,... | collective-permute-start | bytes 983048 | tf_op jit(solution)/shard_map/ppermute | solution.py:68
  369.7 23.7 %collective-permute-start.72 = (bf16[2,2,64,1024]{3,2,1,0:T(8,128)(2,1)S(1)}, bf16[2,2,64,1024]{3,2,1,0:T(8,128)(2,1)S(1)}, u32[]{:S(2)}, u32[]{:S(2)}) collective-permute-start(bf16[2,2,64,1024]{3,2,1,0:T(8,128)(2,1)S(1)} %pad_maximum_fusion.13.pair_ref), channel_id=1, source_target_pairs={{0,1},{1,0},{2,3},{3,2},{4,5},{5,4},{6,7},{7,6},{8,9},{9,8},{10,11... | collective-permute-start | bytes 1572872 | tf_op jit(solution)/shard_map/ppermute | solution.py:68
  370.9 19.2 %collective-permute-start.70 = (bf16[3,64,512]{2,1,0:T(8,128)(2,1)S(1)}, bf16[3,64,512]{2,1,0:T(8,128)(2,1)S(1)}, u32[]{:S(2)}, u32[]{:S(2)}) collective-permute-start(bf16[3,64,512]{2,1,0:T(8,128)(2,1)S(1)} %get-tuple-element.446), channel_id=1, source_target_pairs={{0,2},{1,3},{2,0},{3,1},{4,6},{5,7},{6,4},{7,5},{8,10},{9,11},{10,... | collective-permute-start | bytes 589832 | tf_op jit(solution)/shard_map/ppermute | solution.py:68
  384.2 20.9 %collective-permute-start.76 = (bf16[5,64,512]{2,1,0:T(8,128)(2,1)S(1)}, bf16[5,64,512]{2,1,0:T(8,128)(2,1)S(1)}, u32[]{:S(2)}, u32[]{:S(2)}) collective-permute-start(bf16[5,64,512]{2,1,0:T(8,128)(2,1)S(1)} %add.312), channel_id=1, source_target_pairs={{0,2},{1,3},{2,0},{3,1},{4,6},{5,7},{6,4},{7,5},{8,10},{9,11},{10,... | collective-permute-start | bytes 983048 | tf_op jit(solution)/shard_map/ppermute | solution.py:68
  390.2 15.7 %collective-permute-start.75 = (bf16[3,64,512]{2,1,0:T(8,128)(2,1)S(1)}, bf16[3,64,512]{2,1,0:T(8,128)(2,1)S(1)}, u32[]{:S(2)}, u32[]{:S(2)}) collective-permute-start(bf16[3,64,512]{2,1,0:T(8,128)(2,1)S(1)} %add.311), channel_id=1, source_target_pairs={{0,4},{1,5},{2,6},{3,7},{4,0},{5,1},{6,2},{7,3},{8,12},{9,13},{10,... | collective-permute-start | bytes 589832 | tf_op jit(solution)/shard_map/ppermute | solution.py:68
  405.2 14.4 %collective-permute-start.78 = (bf16[2,5,64,512]{3,2,1,0:T(8,128)(2,1)S(1)}, bf16[2,5,64,512]{3,2,1,0:T(8,128)(2,1)S(1)}, u32[]{:S(2)}, u32[]{:S(2)}) collective-permute-start(bf16[2,5,64,512]{3,2,1,0:T(8,128)(2,1)S(1)} %pad_maximum_fusion.11.pair_ref), channel_id=1, source_target_pairs={{0,1},{1,0},{2,3},{3,2},{4,5},{5,4},{6,7},{7,6},{8,9},{9,8},{10,11... | collective-permute-start | bytes 1966088 | tf_op jit(solution)/shard_map/ppermute | solution.py:68
  (132 other events, 1289.4 us)

commit v3 on v2

--- a/solution.py
+++ b/solution.py
@@ -45,7 +45,7 @@
     return pltpu.CompilerParams(vmem_limit_bytes=int(mib * 2**20))
 
 
-def cost(flops, moved, transcendentals=0, scale=4):
+def cost(flops, moved, transcendentals=0, scale=8):
     return pl.CostEstimate(
         flops=int(scale * flops), bytes_accessed=int(scale * moved), transcendentals=int(scale * transcendentals)
     )
@@ -1104,14 +1104,6 @@
     def as_rows(value):
         return value.reshape(-1, LANES)
 
-    own_vec = jnp.concatenate(
-        [
-            as_rows(value)
-            for value in (ln1_gain, ln1_bias, b_qv, attention_out_bias, ln2_gain, ln2_bias, up_bias, down_bias)
-        ]
-        + [jnp.zeros((VEC_ROWS - 12, LANES), bf16)]
-    )
-
     def joined_cols(which):
         return jnp.concatenate(
             [
@@ -1120,6 +1112,15 @@
             ],
             axis=1,
         )
+
+    own_a = joined_cols(0)
+    own_vec = jnp.concatenate(
+        [
+            as_rows(after(value, own_a))
+            for value in (ln1_gain, ln1_bias, b_qv, attention_out_bias, ln2_gain, ln2_bias, up_bias, down_bias)
+        ]
+        + [jnp.zeros((VEC_ROWS - 12, LANES), bf16)]
+    )
 
     def hidden_own(chunk):
         up = jnp.concatenate(
@@ -1131,11 +1132,10 @@
         )
         return jnp.stack([up, down_weight[chunk * block : (chunk + 1) * block, :]])
 
+    far_a = moves.across(own_a)
+    near_a = moves.core(own_a)
     far_vec = moves.across(own_vec)
     near_vec = moves.core(own_vec)
-    own_a = joined_cols(0)
-    far_a = moves.across(own_a)
-    near_a = moves.core(own_a)
     own_b = joined_cols(1)
     half_b = moves.half(own_b)
     hidden_owns = [hidden_own(chunk) for chunk in range(CHUNKS)]

time: 434 us -> 417 us (0.961)
  other arithmetic: 37.1 us -> 27.1 us
  local copies, waits for them, and re-layouts: 29.5 us -> 22.8 us
    reshape x8, local copies, waits for them, and re-layouts: 5.33 us -> 0.05 us  [as_rows(): return value.reshape(-1, LANES)]
    unnamed x204 -> x220, local copies, waits for them, and re-layouts: 16.3 us -> 14.6 us
  transfers between devices with their start and end apart: 80 -> 80, of which waited for: 22 -> 22; matrix products, arithmetic and copies ran while one was open for 11% -> 8% of each run, Pallas kernels for 51% -> 53%
where the time goes in v3:
time: 417 us; the launch traced here: 410 us
  Pallas kernels  223 us (53%)
  waiting for transfers between devices  74.4 us (18%)
  starting transfers between devices  60.2 us (14%)
  other arithmetic  27.1 us (6%)
  local copies, waits for them, and re-layouts  22.8 us (5%)
    ppermute x80, waiting for transfers between devices, flip(): return lax.ppermute(value, axis, [(i, i ^ bit) for i in range(size)])  74.4 us
    pallas_call x4, Pallas kernels, hidden_chunk(): pl.pallas_call(functools.partial(hidden_body, chunk, fresh), grid_spec=pl...  69.1 us
    ppermute x80, starting transfers between devices, flip(): return lax.ppermute(value, axis, [(i, i ^ bit) for i in range(size)])  60.2 us
    pallas_call x2, Pallas kernels, attend_backward(): pl.pallas_call(functools.partial(attend_backward_body, half * 2 * pairs,...  44.8 us
    pallas_call x1, Pallas kernels, block_back(): pl.pallas_call(functools.partial(block_back_body, blocks=blocks), grid_sp...  27.1 us
    pallas_call x2, Pallas kernels, attend_forward(): pl.pallas_call(functools.partial(attend_forward_body, half * 2 * pairs),...  24.1 us
    pallas_call x1, Pallas kernels, block_output(): pl.pallas_call(block_out_body, grid_spec=pltpu.PrefetchScalarGridSpec(num...  15 us
    unnamed x220, local copies, waits for them, and re-layouts  14.6 us
  transfers between devices with their start and end apart: 80, of which 22 were waited for; matrix products, arithmetic and copies ran while one was open for 8% of the time, Pallas kernels for 53%

profile of v3, /device:TPU:0, one launch (start us, length us, event | category | flops | bytes accessed | tf_op | source)
XLA Modules:
  0.0 409.8 jit_solution(5704270587094361260)
XLA Ops:
  0.7 2.4 fusion.13
  4.4 3.0 collective-permute-start.1
  8.8 2.5 slice_bitcast_fusion
  11.4 1.8 maximum_bitcast_fusion.1
  20.2 2.2 first_norm.1
  22.3 5.3 %collective-permute-done.6.refs_2_ = bf16[256,1536]{1,0:T(8,128)(2,1)} collective-permute-done((bf16[256,1536]{1,0:T(8,128)(2,1)}, bf16[256,1536]{1,0:T(8,128)(2,1)}, u32[]{:S(2)}, u32[]{:S(2)}) %collective-permute-start.6) | collective-permute-done | bytes 786464 | tf_op jit(solution)/shard_map/ppermute | solution.py:68
  30.2 6.2 %joined_product.2 = (bf16[1024,1536]{1,0:T(8,128)(2,1)S(1)}, bf16[1024,1536]{1,0:T(8,128)(2,1)S(1)}) custom-call(s32[5]{0:T(128)S(1)} %pad_add_fusion.index_ref.start_ref, bf16[256,1536]{1,0:T(8,128)(2,1)} %pad_maximum_fusion.9.refs_0_, bf16[256,1536]{1,0:T(8,128)(2,1)} %collective-permute-done.5.refs_1_, bf16[256,1536]{1,0:T(8,128)(2,1)} %collective-permute-done.6.refs_2_, ...), custom_call_target="tpu_custom_call" | custom-call | flops 25769803776 | bytes 92274688 | tf_op jit(solution)/shard_map/joined_product/pallas_call | solution.py:319
  36.4 1.7 copy-done.50
  41.5 12.1 %attend_forward.2 = (bf16[1024,512]{1,0:T(8,128)(2,1)S(1)}, f32[2,4,2,512]{3,2,1,0:T(2,128)S(1)}) custom-call(s32[5]{0:T(128)S(1)} %pad_add_fusion.index_ref.start_ref, bf16[1024,1536]{1,0:T(8,128)(2,1)S(1)} %get-tuple-element.271.q_ref.k_ref.v_ref, bf16[1024,1536]{1,0:T(8,128)(2,1)S(1)} %get-tuple-element.271.q_ref.k_ref.v_ref, ...), custom_call_target="tpu_custom_call" | custom-call | flops 51539607552 | bytes 33554432 | tf_op jit(solution)/shard_map/attend_forward/pallas_call | solution.py:385
  56.8 5.5 %joined_product.3 = (bf16[1024,1536]{1,0:T(8,128)(2,1)S(1)}, bf16[1024,1536]{1,0:T(8,128)(2,1)S(1)}) custom-call(s32[5]{0:T(128)S(1)} %pad_add_fusion.index_ref.start_ref, bf16[256,1536]{1,0:T(8,128)(2,1)S(1)} %pad_maximum_fusion.8.refs_0_, bf16[256,1536]{1,0:T(8,128)(2,1)S(1)} %collective-permute-done.4.refs_1_, ...), custom_call_target="tpu_custom_call" | custom-call | flops 25769803776 | bytes 92274688 | tf_op jit(solution)/shard_map/joined_product/pallas_call | solution.py:319
  62.3 1.7 copy-done.52
  66.7 12.0 %attend_forward.3 = (bf16[1024,512]{1,0:T(8,128)(2,1)S(1)}, f32[2,4,2,512]{3,2,1,0:T(2,128)S(1)}) custom-call(s32[5]{0:T(128)S(1)} %pad_add_fusion.index_ref.start_ref, bf16[1024,1536]{1,0:T(8,128)(2,1)S(1)} %get-tuple-element.282.q_ref.k_ref.v_ref, bf16[1024,1536]{1,0:T(8,128)(2,1)S(1)} %get-tuple-element.282.q_ref.k_ref.v_ref, ...), custom_call_target="tpu_custom_call" | custom-call | flops 51539607552 | bytes 33554432 | tf_op jit(solution)/shard_map/attend_forward/pallas_call | solution.py:385
  81.3 4.8 %middle_product.1 = (f32[1024,1024]{1,0:T(8,128)S(1)}, bf16[1024,1024]{1,0:T(8,128)(2,1)S(1)}, bf16[1024,1024]{1,0:T(8,128)(2,1)S(1)}) custom-call(s32[5]{0:T(128)S(1)} %pad_add_fusion.index_ref.start_ref, bf16[256,1024]{1,0:T(8,128)(2,1)S(1)} %copy-done.5, bf16[256,1024]{1,0:T(8,128)(2,1)S(1)} %collective-permute-done.12.refs_1_, ...), custom_call_target="tpu_custom_call" | custom-call | flops 17179869184 | bytes 117440512 | tf_op jit(solution)/shard_map/middle_product/pallas_call | solution.py:571
  94.0 17.0 %hidden_chunk0.1 = (bf16[1024,4096]{1,0:T(8,128)(2,1)}, bf16[1024,4096]{1,0:T(8,128)(2,1)}, bf16[2,2,256,1024]{3,2,1,0:T(8,128)(2,1)}, bf16[2,2,256,1024]{3,2,1,0:T(8,128)(2,1)}, f32[1,1024]{1,0:T(1,128)S(1)}) custom-call(s32[5]{0:T(128)S(1)} %pad_add_fusion.index_ref.start_ref, bf16[2,256,1024]{2,1,0:T(8,128)(2,1)S(1)} %pad_maximum_fusion.1.refs_0_, ...), custom_call_target="tpu_custom_call" | custom-call | flops 68719476736 | bytes 201326592 | tf_op jit(solution)/shard_map/hidden_chunk0/pallas_call | solution.py:706
  113.1 3.6 collective-permute-done.24.refs_2_.refs_20_
  116.8 17.5 %hidden_chunk1.1 = (bf16[1024,4096]{1,0:T(8,128)(2,1)}, bf16[1024,4096]{1,0:T(8,128)(2,1)}, bf16[2,2,256,1024]{3,2,1,0:T(8,128)(2,1)}, bf16[2,2,256,1024]{3,2,1,0:T(8,128)(2,1)}, f32[1,1024]{1,0:T(1,128)S(1)}) custom-call(s32[5]{0:T(128)S(1)} %pad_add_fusion.index_ref.start_ref, ...), custom_call_target="tpu_custom_call", output_to_operand_aliasing={{0}: (7, {}), {1}: (8, {})} | custom-call | flops 68719476736 | bytes 201326592 | tf_op jit(solution)/shard_map/hidden_chunk1/pallas_call | solution.py:706
  135.8 3.2 slice_add_fusion.3
  139.9 17.0 %hidden_chunk2.1 = (bf16[1024,4096]{1,0:T(8,128)(2,1)}, bf16[1024,4096]{1,0:T(8,128)(2,1)}, bf16[2,2,256,1024]{3,2,1,0:T(8,128)(2,1)}, bf16[2,2,256,1024]{3,2,1,0:T(8,128)(2,1)}, f32[1,1024]{1,0:T(1,128)S(1)}) custom-call(s32[5]{0:T(128)S(1)} %pad_add_fusion.index_ref.start_ref, ...), custom_call_target="tpu_custom_call", output_to_operand_aliasing={{0}: (7, {}), {1}: (8, {})} | custom-call | flops 68719476736 | bytes 201326592 | tf_op jit(solution)/shard_map/hidden_chunk2/pallas_call | solution.py:706
  157.7 2.5 slice_add_fusion.2
  161.3 3.9 collective-permute-done.34
  165.3 17.5 %hidden_chunk3.1 = (bf16[1024,4096]{1,0:T(8,128)(2,1)}, bf16[1024,4096]{1,0:T(8,128)(2,1)}, bf16[2,2,256,1024]{3,2,1,0:T(8,128)(2,1)}, bf16[2,2,256,1024]{3,2,1,0:T(8,128)(2,1)}, f32[1,1024]{1,0:T(1,128)S(1)}) custom-call(s32[5]{0:T(128)S(1)} %pad_add_fusion.index_ref.start_ref, ...), custom_call_target="tpu_custom_call", output_to_operand_aliasing={{0}: (7, {}), {1}: (8, {})} | custom-call | flops 68719476736 | bytes 201326592 | tf_op jit(solution)/shard_map/hidden_chunk3/pallas_call | solution.py:706
  184.4 2.6 collective-permute-done.38
  193.1 27.1 %block_back.1 = (f32[1024,1024]{1,0:T(8,128)}, bf16[1024,1024]{1,0:T(8,128)(2,1)}, bf16[2,2,256,512]{3,2,1,0:T(8,128)(2,1)}, bf16[2,2,256,512]{3,2,1,0:T(8,128)(2,1)}, f32[8,1024]{1,0:T(8,128)S(1)}) custom-call(s32[5]{0:T(128)S(1)} %pad_add_fusion.index_ref.start_ref, bf16[2,256,1024]{2,1,0:T(8,128)(2,1)} %copy-done.1, bf16[2,256,1024]{2,1,0:T(8,128)(2,1)} %copy-done.8, ...), custom_call_target="tpu_custom_call" | custom-call | flops 103079215104 | bytes 268435456 | tf_op jit(solution)/shard_map/block_back/pallas_call | solution.py:851
  221.9 1.6 collective-permute-start.46
  228.4 22.4 %attend_backward.2 = (bf16[1024,512]{1,0:T(8,128)(2,1)S(1)}, bf16[1024,512]{1,0:T(8,128)(2,1)S(1)}, bf16[1024,512]{1,0:T(8,128)(2,1)S(1)}, bf16[2,3,256,512]{3,2...) custom-call(s32[5]{0:T(128)S(1)} %pad_add_fusion.index_ref.start_ref, ...), custom_call_target="tpu_custom_call" | custom-call | flops 103079215104 | bytes 67108864 | tf_op jit(solution)/shard_map/attend_backward/pallas_call | solution.py:504
  251.1 2.7 collective-permute-start.50
  259.7 22.4 %attend_backward.3 = (bf16[1024,512]{1,0:T(8,128)(2,1)S(1)}, bf16[1024,512]{1,0:T(8,128)(2,1)S(1)}, bf16[1024,512]{1,0:T(8,128)(2,1)S(1)}, bf16[2,3,256,512]{3,2...) custom-call(s32[5]{0:T(128)S(1)} %pad_add_fusion.index_ref.start_ref, ...), custom_call_target="tpu_custom_call" | custom-call | flops 103079215104 | bytes 67108864 | tf_op jit(solution)/shard_map/attend_backward/pallas_call | solution.py:504
  285.2 1.7 slice_add_fusion.5
  288.0 13.0 %input_gradient.1 = (f32[1024,1024]{1,0:T(8,128)}, f32[64,256]{1,0:T(8,128)S(1)}) custom-call(s32[5]{0:T(128)S(1)} %pad_add_fusion.index_ref.start_ref, bf16[1024,512]{1,0:T(8,128)(2,1)S(1)} %get-tuple-element.401.refs_0_, bf16[1024,512]{1,0:T(8,128)(2,1)S(1)} %get-tuple-element.402.refs_1_, bf16[1024,512]{1,0:T(8,128)(2,1)S(1)} %get-tuple-element.403.refs_2_, ...), custom_call_target="tpu_custom_call" | custom-call | flops 51539607552 | bytes 184549376 | tf_op jit(solution)/shard_map/input_gradient/pallas_call | solution.py:1005
  305.0 10.1 %collective-permute-done.57 = bf16[2,64,1024]{2,1,0:T(8,128)(2,1)S(1)} collective-permute-done((bf16[2,64,1024]{2,1,0:T(8,128)(2,1)S(1)}, bf16[2,64,1024]{2,1,0:T(8,128)(2,1)S(1)}, u32[]{:S(2)}, u32[]{:S(2)}) %collective-permute-start.57) | collective-permute-done | bytes 262176 | tf_op jit(solution)/shard_map/ppermute | solution.py:68
  315.3 2.1 collective-permute-start.63
  320.6 15.0 %block_output.1 = bf16[1024,1024]{1,0:T(8,128)(2,1)} custom-call(s32[5]{0:T(128)S(1)} %pad_add_fusion.index_ref.start_ref, bf16[2,256,1024]{2,1,0:T(8,128)(2,1)} %copy-done.1, bf16[2,256,1024]{2,1,0:T(8,128)(2,1)} %copy-done.8, bf16[2,128,1024]{2,1,0:T(8,128)(2,1)S(1)} %copy-done.15, bf16[2,128,1024]{2,1,0:T(8,128)(2,1)S(1)} %copy-done.18, ...), custom_call_target="tpu_custom_call" | custom-call | flops 68719476736 | bytes 184549376 | tf_op jit(solution)/shard_map/block_output/pallas_call | solution.py:933
  336.2 5.9 %collective-permute-done.60 = bf16[5,128,512]{2,1,0:T(8,128)(2,1)S(1)} collective-permute-done((bf16[5,128,512]{2,1,0:T(8,128)(2,1)S(1)}, bf16[5,128,512]{2,1,0:T(8,128)(2,1)S(1)}, u32[]{:S(2)}, u32[]{:S(2)}) %collective-permute-start.60) | collective-permute-done | bytes 655392 | tf_op jit(solution)/shard_map/ppermute | solution.py:68
  345.2 2.9 place_hidden_first.1
  348.1 2.6 collective-permute-done.66
  350.8 2.1 collective-permute-start.71
  356.9 9.5 %collective-permute-done.67.other_ref = bf16[2,2,64,1024]{3,2,1,0:T(8,128)(2,1)S(1)} collective-permute-done((bf16[2,2,64,1024]{3,2,1,0:T(8,128)(2,1)S(1)}, bf16[2,2,64,1024]{3,2,1,0:T(8,128)(2,1)S(1)}, u32[]{:S(2)}, u32[]{:S(2)}) %collective-permute-start.67) | collective-permute-done | bytes 524320 | tf_op jit(solution)/shard_map/ppermute | solution.py:68
  366.4 2.0 place_hidden_second.1
  371.2 3.2 collective-permute-done.64
  374.5 2.1 collective-permute-start.75
  377.1 2.0 place_hidden_third.1
  380.8 3.3 collective-permute-done.73
  385.0 3.9 collective-permute-done.74
  390.7 4.6 %collective-permute-done.77 = bf16[3,64,512]{2,1,0:T(8,128)(2,1)S(1)} collective-permute-done((bf16[3,64,512]{2,1,0:T(8,128)(2,1)S(1)}, bf16[3,64,512]{2,1,0:T(8,128)(2,1)S(1)}, u32[]{:S(2)}, u32[]{:S(2)}) %collective-permute-start.77) | collective-permute-done | bytes 196640 | tf_op jit(solution)/shard_map/ppermute | solution.py:68
  398.1 5.2 %collective-permute-done.78.other_ref = bf16[2,5,64,512]{3,2,1,0:T(8,128)(2,1)S(1)} collective-permute-done((bf16[2,5,64,512]{3,2,1,0:T(8,128)(2,1)S(1)}, bf16[2,5,64,512]{3,2,1,0:T(8,128)(2,1)S(1)}, u32[]{:S(2)}, u32[]{:S(2)}) %collective-permute-start.78) | collective-permute-done | bytes 655392 | tf_op jit(solution)/shard_map/ppermute | solution.py:68
  403.3 2.2 place_fourth.1
  405.5 2.0 collective-permute-done.79.other_ref
  407.5 1.8 place_last.1
  (423 shorter events, 87.8 us)
Async XLA Ops:
  4.4 14.6 %collective-permute-start.1 = (bf16[16,256]{1,0:T(8,128)(2,1)S(1)}, bf16[16,256]{1,0:T(8,128)(2,1)S(1)}, u32[]{:S(2)}, u32[]{:S(2)}) collective-permute-start(bf16[16,256]{1,0:T(8,128)(2,1)S(1)} %concatenate.43.own_ref), channel_id=1, source_target_pairs={{0,16},{8,24},{16,0},{24,8},{1,17},{9,25},{17,1},{25,9},{2,18},{10... | collective-permute-start | bytes 24584 | tf_op jit(solution)/shard_map/ppermute | solution.py:68
  7.4 20.3 %collective-permute-start.6 = (bf16[256,1536]{1,0:T(8,128)(2,1)}, bf16[256,1536]{1,0:T(8,128)(2,1)}, u32[]{:S(2)}, u32[]{:S(2)}) collective-permute-start(bf16[256,1536]{1,0:T(8,128)(2,1)} %pad_maximum_fusion.9.refs_0_), channel_id=1, source_target_pairs={{0,16},{8,24},{16,0},{24,8},{1,17},{9,25},{17,1},{25,9},{2,18},{10... | collective-permute-start | bytes 2359304 | tf_op jit(solution)/shard_map/ppermute | solution.py:68
  7.5 21.2 %collective-permute-start.5 = (bf16[256,1536]{1,0:T(8,128)(2,1)}, bf16[256,1536]{1,0:T(8,128)(2,1)}, u32[]{:S(2)}, u32[]{:S(2)}) collective-permute-start(bf16[256,1536]{1,0:T(8,128)(2,1)} %pad_maximum_fusion.9.refs_0_), channel_id=1, source_target_pairs={{0,8},{8,0},{16,24},{24,16},{1,9},{9,1},{17,25},{25,17},{2,10},{10... | collective-permute-start | bytes 2359304 | tf_op jit(solution)/shard_map/ppermute | solution.py:68
  39.5 14.4 %collective-permute-start.8 = (bf16[128,1536]{1,0:T(8,128)(2,1)S(1)}, bf16[128,1536]{1,0:T(8,128)(2,1)S(1)}, u32[]{:S(2)}, u32[]{:S(2)}) collective-permute-start(bf16[128,1536]{1,0:T(8,128)(2,1)S(1)} %collective-permute-done.3.refs_2_), channel_id=1, source_target_pairs={{0,1},{1,0},{2,3},{3,2},{4,5},{5,4},{6,7},{7,6},{8,9},{9,8},{10,11... | collective-permute-start | bytes 1179656 | tf_op jit(solution)/shard_map/ppermute | solution.py:68
  41.0 15.3 %collective-permute-start.10 = (bf16[2,256,1024]{2,1,0:T(8,128)(2,1)S(1)}, bf16[2,256,1024]{2,1,0:T(8,128)(2,1)S(1)}, u32[]{:S(2)}, u32[]{:S(2)}) collective-permute-start(bf16[2,256,1024]{2,1,0:T(8,128)(2,1)S(1)} %pad_maximum_fusion.1.refs_0_), channel_id=1, source_target_pairs={{0,8},{8,0},{16,24},{24,16},{1,9},{9,1},{17,25},{25,17},{2,10},{10... | collective-permute-start | bytes 3145736 | tf_op jit(solution)/shard_map/ppermute | solution.py:68
  56.3 23.6 %collective-permute-start.15 = (bf16[2,128,1024]{2,1,0:T(8,128)(2,1)S(1)}, bf16[2,128,1024]{2,1,0:T(8,128)(2,1)S(1)}, u32[]{:S(2)}, u32[]{:S(2)}) collective-permute-start(bf16[2,128,1024]{2,1,0:T(8,128)(2,1)S(1)} %collective-permute-done.9.refs_2_), channel_id=1, source_target_pairs={{0,1},{1,0},{2,3},{3,2},{4,5},{5,4},{6,7},{7,6},{8,9},{9,8},{10,11... | collective-permute-start | bytes 1572872 | tf_op jit(solution)/shard_map/ppermute | solution.py:68
  64.0 15.6 %collective-permute-start.16 = (bf16[128,1024]{1,0:T(8,128)(2,1)S(1)}, bf16[128,1024]{1,0:T(8,128)(2,1)S(1)}, u32[]{:S(2)}, u32[]{:S(2)}) collective-permute-start(bf16[128,1024]{1,0:T(8,128)(2,1)S(1)} %collective-permute-done.11.refs_2_), channel_id=1, source_target_pairs={{0,1},{1,0},{2,3},{3,2},{4,5},{5,4},{6,7},{7,6},{8,9},{9,8},{10,11... | collective-permute-start | bytes 786440 | tf_op jit(solution)/shard_map/ppermute | solution.py:68
  91.0 20.6 %collective-permute-start.23 = (bf16[2,256,1024]{2,1,0:T(8,128)(2,1)S(1)}, bf16[2,256,1024]{2,1,0:T(8,128)(2,1)S(1)}, u32[]{:S(2)}, u32[]{:S(2)}) collective-permute-start(bf16[2,256,1024]{2,1,0:T(8,128)(2,1)S(1)} %pad_maximum_fusion.3.refs_0_.refs_12_), channel_id=1, source_target_pairs={{0,8},{8,0},{16,24},{24,16},{1,9},{9,1},{17,25},{25,17},{2,10},{10... | collective-permute-start | bytes 3145736 | tf_op jit(solution)/shard_map/ppermute | solution.py:68
  91.3 20.0 %collective-permute-start.22 = (bf16[2,128,1024]{2,1,0:T(8,128)(2,1)S(1)}, bf16[2,128,1024]{2,1,0:T(8,128)(2,1)S(1)}, u32[]{:S(2)}, u32[]{:S(2)}) collective-permute-start(bf16[2,128,1024]{2,1,0:T(8,128)(2,1)S(1)} %copy-done.94), channel_id=1, source_target_pairs={{0,16},{8,24},{16,0},{24,8},{1,17},{9,25},{17,1},{25,9},{2,18},{10... | collective-permute-start | bytes 1572872 | tf_op jit(solution)/shard_map/ppermute | solution.py:68
  92.3 18.7 %collective-permute-start.21 = (bf16[2,128,1024]{2,1,0:T(8,128)(2,1)S(1)}, bf16[2,128,1024]{2,1,0:T(8,128)(2,1)S(1)}, u32[]{:S(2)}, u32[]{:S(2)}) collective-permute-start(bf16[2,128,1024]{2,1,0:T(8,128)(2,1)S(1)} %collective-permute-done.17.refs_2_.refs_8_), channel_id=1, source_target_pairs={{0,1},{1,0},{2,3},{3,2},{4,5},{5,4},{6,7},{7,6},{8,9},{9,8},{10,11... | collective-permute-start | bytes 1572872 | tf_op jit(solution)/shard_map/ppermute | solution.py:68
  92.8 23.9 %collective-permute-start.25 = (bf16[2,256,1024]{2,1,0:T(8,128)(2,1)S(1)}, bf16[2,256,1024]{2,1,0:T(8,128)(2,1)S(1)}, u32[]{:S(2)}, u32[]{:S(2)}) collective-permute-start(bf16[2,256,1024]{2,1,0:T(8,128)(2,1)S(1)} %pad_maximum_fusion.4.refs_0_.refs_18_), channel_id=1, source_target_pairs={{0,8},{8,0},{16,24},{24,16},{1,9},{9,1},{17,25},{25,17},{2,10},{10... | collective-permute-start | bytes 3145736 | tf_op jit(solution)/shard_map/ppermute | solution.py:68
  92.9 23.9 %collective-permute-start.24 = (bf16[2,128,1024]{2,1,0:T(8,128)(2,1)S(1)}, bf16[2,128,1024]{2,1,0:T(8,128)(2,1)}, u32[]{:S(2)}, u32[]{:S(2)}) collective-permute-start(bf16[2,128,1024]{2,1,0:T(8,128)(2,1)S(1)} %copy-done.93), channel_id=1, source_target_pairs={{0,16},{8,24},{16,0},{24,8},{1,17},{9,25},{17,1},{25,9},{2,18},{10... | collective-permute-start | bytes 1572872 | tf_op jit(solution)/shard_map/ppermute | solution.py:68
  111.6 22.8 %collective-permute-start.29 = (bf16[2,128,1024]{2,1,0:T(8,128)(2,1)S(1)}, bf16[2,128,1024]{2,1,0:T(8,128)(2,1)S(1)}, u32[]{:S(2)}, u32[]{:S(2)}) collective-permute-start(bf16[2,128,1024]{2,1,0:T(8,128)(2,1)S(1)} %collective-permute-done.22.refs_2_.refs_14_), channel_id=1, source_target_pairs={{0,1},{1,0},{2,3},{3,2},{4,5},{5,4},{6,7},{7,6},{8,9},{9,8},{10,11... | collective-permute-start | bytes 1572872 | tf_op jit(solution)/shard_map/ppermute | solution.py:68
  116.7 19.1 %collective-permute-start.28 = (bf16[2,2,256,1024]{3,2,1,0:T(8,128)(2,1)}, bf16[2,2,256,1024]{3,2,1,0:T(8,128)(2,1)}, u32[]{:S(2)}, u32[]{:S(2)}) collective-permute-start(bf16[2,2,256,1024]{3,2,1,0:T(8,128)(2,1)} %get-tuple-element.306), channel_id=1, source_target_pairs={{0,8},{8,0},{16,24},{24,16},{1,9},{9,1},{17,25},{25,17},{2,10},{10... | collective-permute-start | bytes 6291464 | tf_op jit(solution)/shard_map/ppermute | solution.py:68
  135.1 21.9 %collective-permute-start.33 = (bf16[2,128,1024]{2,1,0:T(8,128)(2,1)}, bf16[2,128,1024]{2,1,0:T(8,128)(2,1)}, u32[]{:S(2)}, u32[]{:S(2)}) collective-permute-start(bf16[2,128,1024]{2,1,0:T(8,128)(2,1)} %collective-permute-done.24.refs_2_.refs_20_), channel_id=1, source_target_pairs={{0,1},{1,0},{2,3},{3,2},{4,5},{5,4},{6,7},{7,6},{8,9},{9,8},{10,11... | collective-permute-start | bytes 1572872 | tf_op jit(solution)/shard_map/ppermute | solution.py:68
  135.6 22.0 %collective-permute-start.32 = (bf16[2,2,256,1024]{3,2,1,0:T(8,128)(2,1)}, bf16[2,2,256,1024]{3,2,1,0:T(8,128)(2,1)}, u32[]{:S(2)}, u32[]{:S(2)}) collective-permute-start(bf16[2,2,256,1024]{3,2,1,0:T(8,128)(2,1)} %get-tuple-element.318), channel_id=1, source_target_pairs={{0,8},{8,0},{16,24},{24,16},{1,9},{9,1},{17,25},{25,17},{2,10},{10... | collective-permute-start | bytes 6291464 | tf_op jit(solution)/shard_map/ppermute | solution.py:68
  139.0 26.3 %collective-permute-start.34 = (bf16[2,256,1024]{2,1,0:T(8,128)(2,1)}, bf16[2,256,1024]{2,1,0:T(8,128)(2,1)}, u32[]{:S(2)}, u32[]{:S(2)}) collective-permute-start(bf16[2,256,1024]{2,1,0:T(8,128)(2,1)} %get-tuple-element.320), channel_id=1, source_target_pairs={{0,16},{8,24},{16,0},{24,8},{1,17},{9,25},{17,1},{25,9},{2,18},{10... | collective-permute-start | bytes 3145736 | tf_op jit(solution)/shard_map/ppermute | solution.py:68
  157.6 32.5 %collective-permute-start.37 = (bf16[2,2,256,1024]{3,2,1,0:T(8,128)(2,1)}, bf16[2,2,256,1024]{3,2,1,0:T(8,128)(2,1)S(1)}, u32[]{:S(2)}, u32[]{:S(2)}) collective-permute-start(bf16[2,2,256,1024]{3,2,1,0:T(8,128)(2,1)} %get-tuple-element.331), channel_id=1, source_target_pairs={{0,8},{8,0},{16,24},{24,16},{1,9},{9,1},{17,25},{25,17},{2,10},{10... | collective-permute-start | bytes 6291464 | tf_op jit(solution)/shard_map/ppermute | solution.py:68
  160.2 26.9 %collective-permute-start.38 = (bf16[2,256,1024]{2,1,0:T(8,128)(2,1)S(1)}, bf16[2,256,1024]{2,1,0:T(8,128)(2,1)S(1)}, u32[]{:S(2)}, u32[]{:S(2)}) collective-permute-start(bf16[2,256,1024]{2,1,0:T(8,128)(2,1)S(1)} %get-tuple-element.332), channel_id=1, source_target_pairs={{0,16},{8,24},{16,0},{24,8},{1,17},{9,25},{17,1},{25,9},{2,18},{10... | collective-permute-start | bytes 3145736 | tf_op jit(solution)/shard_map/ppermute | solution.py:68
  182.8 40.7 %collective-permute-start.41 = (bf16[2,2,256,1024]{3,2,1,0:T(8,128)(2,1)}, bf16[2,2,256,1024]{3,2,1,0:T(8,128)(2,1)S(1)}, u32[]{:S(2)}, u32[]{:S(2)}) collective-permute-start(bf16[2,2,256,1024]{3,2,1,0:T(8,128)(2,1)} %get-tuple-element.346), channel_id=1, source_target_pairs={{0,8},{8,0},{16,24},{24,16},{1,9},{9,1},{17,25},{25,17},{2,10},{10... | collective-permute-start | bytes 6291464 | tf_op jit(solution)/shard_map/ppermute | solution.py:68
  188.6 31.7 %collective-permute-start.43 = (bf16[4,128,1024]{2,1,0:T(8,128)(2,1)}, bf16[4,128,1024]{2,1,0:T(8,128)(2,1)}, u32[]{:S(2)}, u32[]{:S(2)}) collective-permute-start(bf16[4,128,1024]{2,1,0:T(8,128)(2,1)} %pad_maximum_fusion.5), channel_id=1, source_target_pairs={{0,1},{1,0},{2,3},{3,2},{4,5},{5,4},{6,7},{7,6},{8,9},{9,8},{10,11... | collective-permute-start | bytes 3145736 | tf_op jit(solution)/shard_map/ppermute | solution.py:68
  191.4 32.2 %collective-permute-start.42 = (bf16[2,256,1024]{2,1,0:T(8,128)(2,1)}, bf16[2,256,1024]{2,1,0:T(8,128)(2,1)S(1)}, u32[]{:S(2)}, u32[]{:S(2)}) collective-permute-start(bf16[2,256,1024]{2,1,0:T(8,128)(2,1)} %get-tuple-element.347), channel_id=1, source_target_pairs={{0,16},{8,24},{16,0},{24,8},{1,17},{9,25},{17,1},{25,9},{2,18},{10... | collective-permute-start | bytes 3145736 | tf_op jit(solution)/shard_map/ppermute | solution.py:68
  220.2 30.9 %collective-permute-start.45 = (bf16[2,2,256,512]{3,2,1,0:T(8,128)(2,1)}, bf16[2,2,256,512]{3,2,1,0:T(8,128)(2,1)S(1)}, u32[]{:S(2)}, u32[]{:S(2)}) collective-permute-start(bf16[2,2,256,512]{3,2,1,0:T(8,128)(2,1)} %get-tuple-element.363), channel_id=1, source_target_pairs={{0,8},{8,0},{16,24},{24,16},{1,9},{9,1},{17,25},{25,17},{2,10},{10... | collective-permute-start | bytes 3145736 | tf_op jit(solution)/shard_map/ppermute | solution.py:68
  221.9 29.0 %collective-permute-start.46 = (bf16[4,64,1024]{2,1,0:T(8,128)(2,1)S(1)}, bf16[4,64,1024]{2,1,0:T(8,128)(2,1)S(1)}, u32[]{:S(2)}, u32[]{:S(2)}) collective-permute-start(bf16[4,64,1024]{2,1,0:T(8,128)(2,1)S(1)} %get-tuple-element.364), channel_id=1, source_target_pairs={{0,2},{1,3},{2,0},{3,1},{4,6},{5,7},{6,4},{7,5},{8,10},{9,11},{10,... | collective-permute-start | bytes 1572872 | tf_op jit(solution)/shard_map/ppermute | solution.py:68
  227.0 30.7 %collective-permute-start.44 = (bf16[2,256,1024]{2,1,0:T(8,128)(2,1)S(1)}, bf16[2,256,1024]{2,1,0:T(8,128)(2,1)S(1)}, u32[]{:S(2)}, u32[]{:S(2)}) collective-permute-start(bf16[2,256,1024]{2,1,0:T(8,128)(2,1)S(1)} %get-tuple-element.361), channel_id=1, source_target_pairs={{0,16},{8,24},{16,0},{24,8},{1,17},{9,25},{17,1},{25,9},{2,18},{10... | collective-permute-start | bytes 3145736 | tf_op jit(solution)/shard_map/ppermute | solution.py:68
  227.9 28.1 %collective-permute-start.47 = (bf16[2,128,1024]{2,1,0:T(8,128)(2,1)}, bf16[2,128,1024]{2,1,0:T(8,128)(2,1)}, u32[]{:S(2)}, u32[]{:S(2)}) collective-permute-start(bf16[2,128,1024]{2,1,0:T(8,128)(2,1)} %get-tuple-element.365), channel_id=1, source_target_pairs={{0,1},{1,0},{2,3},{3,2},{4,5},{5,4},{6,7},{7,6},{8,9},{9,8},{10,11... | collective-permute-start | bytes 1572872 | tf_op jit(solution)/shard_map/ppermute | solution.py:68
  251.1 31.2 %collective-permute-start.50 = (bf16[4,64,1024]{2,1,0:T(8,128)(2,1)S(1)}, bf16[4,64,1024]{2,1,0:T(8,128)(2,1)S(1)}, u32[]{:S(2)}, u32[]{:S(2)}) collective-permute-start(bf16[4,64,1024]{2,1,0:T(8,128)(2,1)S(1)} %add.277), channel_id=1, source_target_pairs={{0,4},{1,5},{2,6},{3,7},{4,0},{5,1},{6,2},{7,3},{8,12},{9,13},{10,... | collective-permute-start | bytes 1572872 | tf_op jit(solution)/shard_map/ppermute | solution.py:68
  253.7 31.3 %collective-permute-start.48 = (bf16[2,3,256,512]{3,2,1,0:T(8,128)(2,1)S(1)}, bf16[2,3,256,512]{3,2,1,0:T(8,128)(2,1)}, u32[]{:S(2)}, u32[]{:S(2)}) collective-permute-start(bf16[2,3,256,512]{3,2,1,0:T(8,128)(2,1)S(1)} %get-tuple-element.379), channel_id=1, source_target_pairs={{0,8},{8,0},{16,24},{24,16},{1,9},{9,1},{17,25},{25,17},{2,10},{10... | collective-permute-start | bytes 4718600 | tf_op jit(solution)/shard_map/ppermute | solution.py:68
  254.8 30.4 %collective-permute-start.49 = (bf16[2,256,512]{2,1,0:T(8,128)(2,1)}, bf16[2,256,512]{2,1,0:T(8,128)(2,1)}, u32[]{:S(2)}, u32[]{:S(2)}) collective-permute-start(bf16[2,256,512]{2,1,0:T(8,128)(2,1)} %get-tuple-element.380), channel_id=1, source_target_pairs={{0,16},{8,24},{16,0},{24,8},{1,17},{9,25},{17,1},{25,9},{2,18},{10... | collective-permute-start | bytes 1572872 | tf_op jit(solution)/shard_map/ppermute | solution.py:68
  257.2 24.9 %collective-permute-start.51 = (bf16[2,64,1024]{2,1,0:T(8,128)(2,1)S(1)}, bf16[2,64,1024]{2,1,0:T(8,128)(2,1)S(1)}, u32[]{:S(2)}, u32[]{:S(2)}) collective-permute-start(bf16[2,64,1024]{2,1,0:T(8,128)(2,1)S(1)} %get-tuple-element.382), channel_id=1, source_target_pairs={{0,2},{1,3},{2,0},{3,1},{4,6},{5,7},{6,4},{7,5},{8,10},{9,11},{10,... | collective-permute-start | bytes 786440 | tf_op jit(solution)/shard_map/ppermute | solution.py:68
  258.1 26.9 %collective-permute-start.52 = (bf16[2,128,1024]{2,1,0:T(8,128)(2,1)S(1)}, bf16[2,128,1024]{2,1,0:T(8,128)(2,1)S(1)}, u32[]{:S(2)}, u32[]{:S(2)}) collective-permute-start(bf16[2,128,1024]{2,1,0:T(8,128)(2,1)S(1)} %get-tuple-element.383), channel_id=1, source_target_pairs={{0,1},{1,0},{2,3},{3,2},{4,5},{5,4},{6,7},{7,6},{8,9},{9,8},{10,11... | collective-permute-start | bytes 1572872 | tf_op jit(solution)/shard_map/ppermute | solution.py:68
  282.4 18.6 %collective-permute-start.56 = (bf16[2,64,1024]{2,1,0:T(8,128)(2,1)S(1)}, bf16[2,64,1024]{2,1,0:T(8,128)(2,1)S(1)}, u32[]{:S(2)}, u32[]{:S(2)}) collective-permute-start(bf16[2,64,1024]{2,1,0:T(8,128)(2,1)S(1)} %add.286), channel_id=1, source_target_pairs={{0,4},{1,5},{2,6},{3,7},{4,0},{5,1},{6,2},{7,3},{8,12},{9,13},{10,... | collective-permute-start | bytes 786440 | tf_op jit(solution)/shard_map/ppermute | solution.py:68
  283.4 19.8 %collective-permute-start.55 = (bf16[4,64,1024]{2,1,0:T(8,128)(2,1)S(1)}, bf16[4,64,1024]{2,1,0:T(8,128)(2,1)S(1)}, u32[]{:S(2)}, u32[]{:S(2)}) collective-permute-start(bf16[4,64,1024]{2,1,0:T(8,128)(2,1)S(1)} %add.285), channel_id=1, source_target_pairs={{0,2},{1,3},{2,0},{3,1},{4,6},{5,7},{6,4},{7,5},{8,10},{9,11},{10,... | collective-permute-start | bytes 1572872 | tf_op jit(solution)/shard_map/ppermute | solution.py:68
  285.0 33.3 %collective-permute-start.53 = (bf16[2,3,256,512]{3,2,1,0:T(8,128)(2,1)S(1)}, bf16[2,3,256,512]{3,2,1,0:T(8,128)(2,1)S(1)}, u32[]{:S(2)}, u32[]{:S(2)}) collective-permute-start(bf16[2,3,256,512]{3,2,1,0:T(8,128)(2,1)S(1)} %get-tuple-element.396), channel_id=1, source_target_pairs={{0,8},{8,0},{16,24},{24,16},{1,9},{9,1},{17,25},{25,17},{2,10},{10... | collective-permute-start | bytes 4718600 | tf_op jit(solution)/shard_map/ppermute | solution.py:68
  287.0 30.4 %collective-permute-start.54 = (bf16[3,256,512]{2,1,0:T(8,128)(2,1)S(1)}, bf16[3,256,512]{2,1,0:T(8,128)(2,1)S(1)}, u32[]{:S(2)}, u32[]{:S(2)}) collective-permute-start(bf16[3,256,512]{2,1,0:T(8,128)(2,1)S(1)} %get-tuple-element.397), channel_id=1, source_target_pairs={{0,16},{8,24},{16,0},{24,8},{1,17},{9,25},{17,1},{25,9},{2,18},{10... | collective-permute-start | bytes 2359304 | tf_op jit(solution)/shard_map/ppermute | solution.py:68
  301.1 34.5 %collective-permute-start.62 = (bf16[2,64,1024]{2,1,0:T(8,128)(2,1)S(1)}, bf16[2,64,1024]{2,1,0:T(8,128)(2,1)S(1)}, u32[]{:S(2)}, u32[]{:S(2)}) collective-permute-start(bf16[2,64,1024]{2,1,0:T(8,128)(2,1)S(1)} %add.297), channel_id=1, source_target_pairs={{0,2},{1,3},{2,0},{3,1},{4,6},{5,7},{6,4},{7,5},{8,10},{9,11},{10,... | collective-permute-start | bytes 786440 | tf_op jit(solution)/shard_map/ppermute | solution.py:68
  303.3 41.9 %collective-permute-start.61 = (bf16[2,4,64,1024]{3,2,1,0:T(8,128)(2,1)S(1)}, bf16[2,4,64,1024]{3,2,1,0:T(8,128)(2,1)S(1)}, u32[]{:S(2)}, u32[]{:S(2)}) collective-permute-start(bf16[2,4,64,1024]{3,2,1,0:T(8,128)(2,1)S(1)} %pad_maximum_fusion.6.pair_ref), channel_id=1, source_target_pairs={{0,1},{1,0},{2,3},{3,2},{4,5},{5,4},{6,7},{7,6},{8,9},{9,8},{10,11... | collective-permute-start | bytes 3145736 | tf_op jit(solution)/shard_map/ppermute | solution.py:68
  315.3 20.3 %collective-permute-start.63 = (bf16[2,64,1024]{2,1,0:T(8,128)(2,1)S(1)}, bf16[2,64,1024]{2,1,0:T(8,128)(2,1)S(1)}, u32[]{:S(2)}, u32[]{:S(2)}) collective-permute-start(bf16[2,64,1024]{2,1,0:T(8,128)(2,1)S(1)} %add.298), channel_id=1, source_target_pairs={{0,4},{1,5},{2,6},{3,7},{4,0},{5,1},{6,2},{7,3},{8,12},{9,13},{10,... | collective-permute-start | bytes 786440 | tf_op jit(solution)/shard_map/ppermute | solution.py:68
  317.7 24.4 %collective-permute-start.60 = (bf16[5,128,512]{2,1,0:T(8,128)(2,1)S(1)}, bf16[5,128,512]{2,1,0:T(8,128)(2,1)S(1)}, u32[]{:S(2)}, u32[]{:S(2)}) collective-permute-start(bf16[5,128,512]{2,1,0:T(8,128)(2,1)S(1)} %pad_maximum_fusion.10), channel_id=1, source_target_pairs={{0,1},{1,0},{2,3},{3,2},{4,5},{5,4},{6,7},{7,6},{8,9},{9,8},{10,11... | collective-permute-start | bytes 1966088 | tf_op jit(solution)/shard_map/ppermute | solution.py:68
  318.6 24.2 %collective-permute-start.59 = (bf16[3,256,512]{2,1,0:T(8,128)(2,1)S(1)}, bf16[3,256,512]{2,1,0:T(8,128)(2,1)S(1)}, u32[]{:S(2)}, u32[]{:S(2)}) collective-permute-start(bf16[3,256,512]{2,1,0:T(8,128)(2,1)S(1)} %get-tuple-element.427), channel_id=1, source_target_pairs={{0,16},{8,24},{16,0},{24,8},{1,17},{9,25},{17,1},{25,9},{2,18},{10... | collective-permute-start | bytes 2359304 | tf_op jit(solution)/shard_map/ppermute | solution.py:68
  335.7 15.1 %collective-permute-start.68 = (bf16[2,64,1024]{2,1,0:T(8,128)(2,1)S(1)}, bf16[2,64,1024]{2,1,0:T(8,128)(2,1)S(1)}, u32[]{:S(2)}, u32[]{:S(2)}) collective-permute-start(bf16[2,64,1024]{2,1,0:T(8,128)(2,1)S(1)} %add.304), channel_id=1, source_target_pairs={{0,2},{1,3},{2,0},{3,1},{4,6},{5,7},{6,4},{7,5},{8,10},{9,11},{10,... | collective-permute-start | bytes 786440 | tf_op jit(solution)/shard_map/ppermute | solution.py:68
  343.6 22.7 %collective-permute-start.67 = (bf16[2,2,64,1024]{3,2,1,0:T(8,128)(2,1)S(1)}, bf16[2,2,64,1024]{3,2,1,0:T(8,128)(2,1)S(1)}, u32[]{:S(2)}, u32[]{:S(2)}) collective-permute-start(bf16[2,2,64,1024]{3,2,1,0:T(8,128)(2,1)S(1)} %pad_maximum_fusion.12.pair_ref), channel_id=1, source_target_pairs={{0,1},{1,0},{2,3},{3,2},{4,5},{5,4},{6,7},{7,6},{8,9},{9,8},{10,11... | collective-permute-start | bytes 1572872 | tf_op jit(solution)/shard_map/ppermute | solution.py:68
  350.8 17.6 %collective-permute-start.71 = (bf16[5,64,512]{2,1,0:T(8,128)(2,1)S(1)}, bf16[5,64,512]{2,1,0:T(8,128)(2,1)S(1)}, u32[]{:S(2)}, u32[]{:S(2)}) collective-permute-start(bf16[5,64,512]{2,1,0:T(8,128)(2,1)S(1)} %add.308), channel_id=1, source_target_pairs={{0,4},{1,5},{2,6},{3,7},{4,0},{5,1},{6,2},{7,3},{8,12},{9,13},{10,... | collective-permute-start | bytes 983048 | tf_op jit(solution)/shard_map/ppermute | solution.py:68
  352.9 24.2 %collective-permute-start.72 = (bf16[2,2,64,1024]{3,2,1,0:T(8,128)(2,1)S(1)}, bf16[2,2,64,1024]{3,2,1,0:T(8,128)(2,1)S(1)}, u32[]{:S(2)}, u32[]{:S(2)}) collective-permute-start(bf16[2,2,64,1024]{3,2,1,0:T(8,128)(2,1)S(1)} %pad_maximum_fusion.13.pair_ref), channel_id=1, source_target_pairs={{0,1},{1,0},{2,3},{3,2},{4,5},{5,4},{6,7},{7,6},{8,9},{9,8},{10,11... | collective-permute-start | bytes 1572872 | tf_op jit(solution)/shard_map/ppermute | solution.py:68
  355.2 19.2 %collective-permute-start.70 = (bf16[3,64,512]{2,1,0:T(8,128)(2,1)S(1)}, bf16[3,64,512]{2,1,0:T(8,128)(2,1)S(1)}, u32[]{:S(2)}, u32[]{:S(2)}) collective-permute-start(bf16[3,64,512]{2,1,0:T(8,128)(2,1)S(1)} %get-tuple-element.462), channel_id=1, source_target_pairs={{0,2},{1,3},{2,0},{3,1},{4,6},{5,7},{6,4},{7,5},{8,10},{9,11},{10,... | collective-permute-start | bytes 589832 | tf_op jit(solution)/shard_map/ppermute | solution.py:68
  368.5 20.3 %collective-permute-start.76 = (bf16[5,64,512]{2,1,0:T(8,128)(2,1)S(1)}, bf16[5,64,512]{2,1,0:T(8,128)(2,1)S(1)}, u32[]{:S(2)}, u32[]{:S(2)}) collective-permute-start(bf16[5,64,512]{2,1,0:T(8,128)(2,1)S(1)} %add.312), channel_id=1, source_target_pairs={{0,2},{1,3},{2,0},{3,1},{4,6},{5,7},{6,4},{7,5},{8,10},{9,11},{10,... | collective-permute-start | bytes 983048 | tf_op jit(solution)/shard_map/ppermute | solution.py:68
  374.5 15.0 %collective-permute-start.75 = (bf16[3,64,512]{2,1,0:T(8,128)(2,1)S(1)}, bf16[3,64,512]{2,1,0:T(8,128)(2,1)S(1)}, u32[]{:S(2)}, u32[]{:S(2)}) collective-permute-start(bf16[3,64,512]{2,1,0:T(8,128)(2,1)S(1)} %add.311), channel_id=1, source_target_pairs={{0,4},{1,5},{2,6},{3,7},{4,0},{5,1},{6,2},{7,3},{8,12},{9,13},{10,... | collective-permute-start | bytes 589832 | tf_op jit(solution)/shard_map/ppermute | solution.py:68
  388.9 14.4 %collective-permute-start.78 = (bf16[2,5,64,512]{3,2,1,0:T(8,128)(2,1)S(1)}, bf16[2,5,64,512]{3,2,1,0:T(8,128)(2,1)S(1)}, u32[]{:S(2)}, u32[]{:S(2)}) collective-permute-start(bf16[2,5,64,512]{3,2,1,0:T(8,128)(2,1)S(1)} %pad_maximum_fusion.11.pair_ref), channel_id=1, source_target_pairs={{0,1},{1,0},{2,3},{3,2},{4,5},{5,4},{6,7},{7,6},{8,9},{9,8},{10,11... | collective-permute-start | bytes 1966088 | tf_op jit(solution)/shard_map/ppermute | solution.py:68
  (140 other events, 1274.4 us)

commit v4 on v3

--- a/solution.py
+++ b/solution.py
@@ -323,13 +323,10 @@
             grid=(rows // block,),
             in_specs=[any_spec] * len(pieces)
             + [pl.BlockSpec((block, width), lambda i, idx: (i, 0)), whole((SHARDS * VEC_ROWS, LANES))],
-            out_specs=[pl.BlockSpec((block, cols), lambda i, idx: (i, 0)), whole((width, cols))],
-            scratch_shapes=[pltpu.SemaphoreType.DMA((6,))],
+            out_specs=pl.BlockSpec((block, cols), lambda i, idx: (i, 0)),
+            scratch_shapes=[pltpu.VMEM((width, cols), bf16), pltpu.SemaphoreType.DMA((6,))],
         ),
-        out_shape=[
-            jax.ShapeDtypeStruct((rows, cols), bf16),
-            jax.ShapeDtypeStruct((width, cols), bf16),
-        ],
+        out_shape=jax.ShapeDtypeStruct((rows, cols), bf16),
         compiler_params=params(24),
         cost_estimate=cost(2 * rows * width * cols, 2 * (rows * width + rows * cols + 2 * width * cols)),
         name="joined_product",
@@ -947,14 +944,29 @@
 
 
 def input_grad_body(index_ref, *refs, blocks):
-    parts, weights = refs[:6], refs[6:8]
-    tokens_ref, d_middle_ref, vec_ref, sums_ref, bqv_a_ref, bqv_b_ref = refs[8:14]
-    bias_refs = refs[14 : 14 + CHUNKS]
-    out_ref, grads_ref, gain_ref, shift_ref = refs[14 + CHUNKS :]
+    parts, pieces = refs[:6], (refs[6:10], refs[10:16])
+    tokens_ref, d_middle_ref, vec_ref, sums_ref, bqv_a_ref, bqv_b_ref = refs[16:22]
+    bias_refs = refs[22 : 22 + CHUNKS]
+    out_ref, grads_ref, gain_ref, shift_ref, *weights, sems = refs[22 + CHUNKS :]
     step = pl.program_id(0)
 
     @pl.when(step == 0)
     def _():
+        copies = []
+        for half in range(2):
+            rows = pieces[half][0].shape[0]
+            copies += piece_copies(
+                index_ref,
+                pieces[half],
+                lambda to, first, count, half=half, rows=rows: weights[half].at[
+                    pl.ds(pl.multiple_of(to * rows + first, 128), count), :
+                ],
+                sems.at[half],
+            )
+        for copy in copies:
+            copy.start()
+        for copy in copies:
+            copy.wait()
         gain_ref[...] = jnp.zeros_like(gain_ref)
         shift_ref[...] = jnp.zeros_like(shift_ref)
 
@@ -1008,12 +1020,14 @@
             num_scalar_prefetch=1,
             grid=(blocks,),
             in_specs=[by_rows(part)] * 6
-            + [whole((width, 3 * part))] * 2
+            + [any_spec] * 10
             + [by_rows(width), by_rows(width), whole((SHARDS * VEC_ROWS, LANES)), whole((8, width))]
             + [whole((2, part))] * 2
             + [whole(bias.shape) for bias in biases],
             out_specs=[by_rows(width), whole((SHARDS * VEC_ROWS, LANES))],
-            scratch_shapes=[pltpu.VMEM((1, width), f32), pltpu.VMEM((1, width), f32)],
+            scratch_shapes=[pltpu.VMEM((1, width), f32)] * 2
+            + [pltpu.VMEM((width, 3 * part), bf16)] * 2
+            + [pltpu.SemaphoreType.DMA((2, 6))],
         ),
         out_shape=[
             jax.ShapeDtypeStruct((rows, width), f32),
@@ -1146,7 +1160,7 @@
     normed, vec = first_norm(moves.index, tokens, (own_vec, near_vec, far_vec, far_near_vec))
     moves.ran(vec)
 
-    joined, joined_weight, attended, totals = [None] * 2, [None] * 2, [None] * 2, [None] * 2
+    joined, attended, totals = [None] * 2, [None] * 2, [None] * 2
     hidden_far, hidden_near, hidden_other = [None] * CHUNKS, [None] * CHUNKS, [None] * CHUNKS
     hidden_pieces = [None] * CHUNKS
 
@@ -1162,9 +1176,8 @@
     far_b = moves.across(half_b)
     near_b = moves.core(own_b)
     moves.by(1, far_b, near_b)
-    joined[0], joined_weight[0] = joined_product(
-        0, moves.index, (own_a, near_a, far_a, moves.core(far_a)), normed, vec
-    )
+    joined_pieces = [(own_a, near_a, far_a, moves.core(far_a))]
+    joined[0] = joined_product(0, moves.index, joined_pieces[0], normed, vec)
     moves.ran(joined[0])
     other_b = moves.rep(far_b, 1)
     moves.by(1, other_b)
@@ -1175,9 +1188,8 @@
     out_far = moves.across(out_half)
     out_near = moves.core(attention_out_weight)
     moves.by(1, out_far, out_near)
-    joined[1], joined_weight[1] = joined_product(
-        1, moves.index, (own_b, near_b, far_b, other_b, moves.core(far_b), moves.core(other_b)), normed, vec
-    )
+    joined_pieces.append((own_b, near_b, far_b, other_b, moves.core(far_b), moves.core(other_b)))
+    joined[1] = joined_product(1, moves.index, joined_pieces[1], normed, vec)
     moves.ran(joined[1])
     out_other = moves.rep(out_far, 1)
     moves.by(1, out_other)
@@ -1259,7 +1271,7 @@
     second_sum.add()
     third_sum.split()
     input_grad, vec_grads = input_gradient(
-        moves.index, parts, joined_weight, tokens, d_middle, vec, sums, bqv, up_biases
+        moves.index, parts, joined_pieces[0] + joined_pieces[1], tokens, d_middle, vec, sums, bqv, up_biases
     )
     moves.ran(vec_grads)
     b_sum.cross(1)

time: 417 us -> 416 us (level)
  other arithmetic: 27.1 us -> 19.9 us
    unnamed x220 -> x262, local copies, waits for them, and re-layouts: 14.6 us -> 12.4 us
  transfers between devices with their start and end apart: 80 -> 80, of which waited for: 22 -> 24; matrix products, arithmetic and copies ran while one was open for 8% -> 6% of each run, Pallas kernels for 53% -> 53%
where the time goes in v4:
time: 416 us; the launch traced here: 408 us
  Pallas kernels  224 us (54%)
  waiting for transfers between devices  76.4 us (18%)
  starting transfers between devices  64 us (15%)
  local copies, waits for them, and re-layouts  20.9 us (5%)
  other arithmetic  19.9 us (5%)
    ppermute x80, waiting for transfers between devices, flip(): return lax.ppermute(value, axis, [(i, i ^ bit) for i in range(size)])  76.4 us
    pallas_call x4, Pallas kernels, hidden_chunk(): pl.pallas_call(functools.partial(hidden_body, chunk, fresh), grid_spec=pl...  69 us
    ppermute x80, starting transfers between devices, flip(): return lax.ppermute(value, axis, [(i, i ^ bit) for i in range(size)])  64 us
    pallas_call x2, Pallas kernels, attend_backward(): pl.pallas_call(functools.partial(attend_backward_body, half * 2 * pairs,...  44.8 us
    pallas_call x1, Pallas kernels, block_back(): pl.pallas_call(functools.partial(block_back_body, blocks=blocks), grid_sp...  27.1 us
    pallas_call x2, Pallas kernels, attend_forward(): pl.pallas_call(functools.partial(attend_forward_body, half * 2 * pairs),...  24.1 us
    pallas_call x1, Pallas kernels, block_output(): pl.pallas_call(block_out_body, grid_spec=pltpu.PrefetchScalarGridSpec(num...  15 us
    pallas_call x1, Pallas kernels, input_gradient(): pl.pallas_call(functools.partial(input_grad_body, blocks=blocks), grid_sp...  14 us
  transfers between devices with their start and end apart: 80, of which 24 were waited for; matrix products, arithmetic and copies ran while one was open for 6% of the time, Pallas kernels for 53%

profile of v4, /device:TPU:0, one launch (start us, length us, event | category | flops | bytes accessed | tf_op | source)
XLA Modules:
  0.0 407.8 jit_solution(1386682954880649449)
XLA Ops:
  0.7 2.4 fusion.13
  4.4 3.0 collective-permute-start.1
  9.2 2.5 slice_bitcast_fusion
  19.2 2.2 first_norm.1
  21.4 6.3 %collective-permute-done.6.refs_2_.refs_8_ = bf16[256,1536]{1,0:T(8,128)(2,1)} collective-permute-done((bf16[256,1536]{1,0:T(8,128)(2,1)}, bf16[256,1536]{1,0:T(8,128)(2,1)}, u32[]{:S(2)}, u32[]{:S(2)}) %collective-permute-start.6) | collective-permute-done | bytes 786464 | tf_op jit(solution)/shard_map/ppermute | solution.py:68
  30.2 6.3 %joined_product.2.q_ref.k_ref.v_ref = bf16[1024,1536]{1,0:T(8,128)(2,1)S(1)} custom-call(s32[5]{0:T(128)S(1)} %pad_add_fusion.index_ref.start_ref, bf16[256,1536]{1,0:T(8,128)(2,1)} %pad_maximum_fusion.9.refs_0_.refs_6_, bf16[256,1536]{1,0:T(8,128)(2,1)} %collective-permute-done.5.refs_1_.refs_7_, bf16[256,1536]{1,0:T(8,128)(2,1)} %collective-permute-done.6.refs_2_.refs_8_, ...), custom_call_target="tpu_custom_call" | custom-call | flops 25769803776 | bytes 92274688 | tf_op jit(solution)/shard_map/joined_product/pallas_call | solution.py:319
  36.5 3.0 collective-permute-done.3.refs_2_.refs_12_
  41.6 12.0 %attend_forward.2 = (bf16[1024,512]{1,0:T(8,128)(2,1)S(1)}, f32[2,4,2,512]{3,2,1,0:T(2,128)S(1)}) custom-call(s32[5]{0:T(128)S(1)} %pad_add_fusion.index_ref.start_ref, bf16[1024,1536]{1,0:T(8,128)(2,1)S(1)} %joined_product.2.q_ref.k_ref.v_ref, bf16[1024,1536]{1,0:T(8,128)(2,1)S(1)} %joined_product.2.q_ref.k_ref.v_ref, ...), custom_call_target="tpu_custom_call" | custom-call | flops 51539607552 | bytes 33554432 | tf_op jit(solution)/shard_map/attend_forward/pallas_call | solution.py:382
  57.0 5.5 %joined_product.3.q_ref.k_ref.v_ref = bf16[1024,1536]{1,0:T(8,128)(2,1)S(1)} custom-call(s32[5]{0:T(128)S(1)} %pad_add_fusion.index_ref.start_ref, bf16[256,1536]{1,0:T(8,128)(2,1)S(1)} %pad_maximum_fusion.8.refs_0_.refs_10_, bf16[256,1536]{1,0:T(8,128)(2,1)S(1)} %collective-permute-done.4.refs_1_.refs_11_, ...), custom_call_target="tpu_custom_call" | custom-call | flops 25769803776 | bytes 92274688 | tf_op jit(solution)/shard_map/joined_product/pallas_call | solution.py:319
  65.4 12.0 %attend_forward.3 = (bf16[1024,512]{1,0:T(8,128)(2,1)S(1)}, f32[2,4,2,512]{3,2,1,0:T(2,128)S(1)}) custom-call(s32[5]{0:T(128)S(1)} %pad_add_fusion.index_ref.start_ref, bf16[1024,1536]{1,0:T(8,128)(2,1)S(1)} %joined_product.3.q_ref.k_ref.v_ref, bf16[1024,1536]{1,0:T(8,128)(2,1)S(1)} %joined_product.3.q_ref.k_ref.v_ref, ...), custom_call_target="tpu_custom_call" | custom-call | flops 51539607552 | bytes 33554432 | tf_op jit(solution)/shard_map/attend_forward/pallas_call | solution.py:382
  79.4 4.8 %middle_product.1 = (f32[1024,1024]{1,0:T(8,128)S(1)}, bf16[1024,1024]{1,0:T(8,128)(2,1)S(1)}, bf16[1024,1024]{1,0:T(8,128)(2,1)S(1)}) custom-call(s32[5]{0:T(128)S(1)} %pad_add_fusion.index_ref.start_ref, bf16[256,1024]{1,0:T(8,128)(2,1)S(1)} %copy-done.5, bf16[256,1024]{1,0:T(8,128)(2,1)S(1)} %collective-permute-done.12.refs_1_, ...), custom_call_target="tpu_custom_call" | custom-call | flops 17179869184 | bytes 117440512 | tf_op jit(solution)/shard_map/middle_product/pallas_call | solution.py:568
  93.1 17.0 %hidden_chunk0.1 = (bf16[1024,4096]{1,0:T(8,128)(2,1)}, bf16[1024,4096]{1,0:T(8,128)(2,1)}, bf16[2,2,256,1024]{3,2,1,0:T(8,128)(2,1)}, bf16[2,2,256,1024]{3,2,1,0:T(8,128)(2,1)}, f32[1,1024]{1,0:T(1,128)S(1)}) custom-call(s32[5]{0:T(128)S(1)} %pad_add_fusion.index_ref.start_ref, bf16[2,256,1024]{2,1,0:T(8,128)(2,1)S(1)} %pad_maximum_fusion.1.refs_0_, ...), custom_call_target="tpu_custom_call" | custom-call | flops 68719476736 | bytes 201326592 | tf_op jit(solution)/shard_map/hidden_chunk0/pallas_call | solution.py:703
  111.2 3.6 collective-permute-done.24.refs_2_.refs_20_
  114.9 17.5 %hidden_chunk1.1 = (bf16[1024,4096]{1,0:T(8,128)(2,1)}, bf16[1024,4096]{1,0:T(8,128)(2,1)}, bf16[2,2,256,1024]{3,2,1,0:T(8,128)(2,1)}, bf16[2,2,256,1024]{3,2,1,0:T(8,128)(2,1)}, f32[1,1024]{1,0:T(1,128)S(1)}) custom-call(s32[5]{0:T(128)S(1)} %pad_add_fusion.index_ref.start_ref, ...), custom_call_target="tpu_custom_call", output_to_operand_aliasing={{0}: (7, {}), {1}: (8, {})} | custom-call | flops 68719476736 | bytes 201326592 | tf_op jit(solution)/shard_map/hidden_chunk1/pallas_call | solution.py:703
  134.8 3.2 slice_add_fusion.3
  138.7 17.0 %hidden_chunk2.1 = (bf16[1024,4096]{1,0:T(8,128)(2,1)}, bf16[1024,4096]{1,0:T(8,128)(2,1)}, bf16[2,2,256,1024]{3,2,1,0:T(8,128)(2,1)}, bf16[2,2,256,1024]{3,2,1,0:T(8,128)(2,1)}, f32[1,1024]{1,0:T(1,128)S(1)}) custom-call(s32[5]{0:T(128)S(1)} %pad_add_fusion.index_ref.start_ref, ...), custom_call_target="tpu_custom_call", output_to_operand_aliasing={{0}: (7, {}), {1}: (8, {})} | custom-call | flops 68719476736 | bytes 201326592 | tf_op jit(solution)/shard_map/hidden_chunk2/pallas_call | solution.py:703
  156.4 2.5 slice_add_fusion.2
  160.4 3.8 collective-permute-done.34
  164.3 17.5 %hidden_chunk3.1 = (bf16[1024,4096]{1,0:T(8,128)(2,1)}, bf16[1024,4096]{1,0:T(8,128)(2,1)}, bf16[2,2,256,1024]{3,2,1,0:T(8,128)(2,1)}, bf16[2,2,256,1024]{3,2,1,0:T(8,128)(2,1)}, f32[1,1024]{1,0:T(1,128)S(1)}) custom-call(s32[5]{0:T(128)S(1)} %pad_add_fusion.index_ref.start_ref, ...), custom_call_target="tpu_custom_call", output_to_operand_aliasing={{0}: (7, {}), {1}: (8, {})} | custom-call | flops 68719476736 | bytes 201326592 | tf_op jit(solution)/shard_map/hidden_chunk3/pallas_call | solution.py:703
  182.2 3.9 collective-permute-done.38
  191.0 27.1 %block_back.1 = (f32[1024,1024]{1,0:T(8,128)}, bf16[1024,1024]{1,0:T(8,128)(2,1)}, bf16[2,2,256,512]{3,2,1,0:T(8,128)(2,1)}, bf16[2,2,256,512]{3,2,1,0:T(8,128)(2,1)}, f32[8,1024]{1,0:T(8,128)S(1)}) custom-call(s32[5]{0:T(128)S(1)} %pad_add_fusion.index_ref.start_ref, bf16[2,256,1024]{2,1,0:T(8,128)(2,1)} %copy-done.1, bf16[2,256,1024]{2,1,0:T(8,128)(2,1)} %copy-done.8, ...), custom_call_target="tpu_custom_call" | custom-call | flops 103079215104 | bytes 268435456 | tf_op jit(solution)/shard_map/block_back/pallas_call | solution.py:848
  218.6 1.7 collective-permute-start.46
  223.2 22.4 %attend_backward.2 = (bf16[1024,512]{1,0:T(8,128)(2,1)S(1)}, bf16[1024,512]{1,0:T(8,128)(2,1)S(1)}, bf16[1024,512]{1,0:T(8,128)(2,1)S(1)}, bf16[2,3,256,512]{3,2...) custom-call(s32[5]{0:T(128)S(1)} %pad_add_fusion.index_ref.start_ref, ...), custom_call_target="tpu_custom_call" | custom-call | flops 103079215104 | bytes 67108864 | tf_op jit(solution)/shard_map/attend_backward/pallas_call | solution.py:501
  245.9 2.7 collective-permute-start.50
  253.3 22.4 %attend_backward.3 = (bf16[1024,512]{1,0:T(8,128)(2,1)S(1)}, bf16[1024,512]{1,0:T(8,128)(2,1)S(1)}, bf16[1024,512]{1,0:T(8,128)(2,1)S(1)}, bf16[2,3,256,512]{3,2...) custom-call(s32[5]{0:T(128)S(1)} %pad_add_fusion.index_ref.start_ref, ...), custom_call_target="tpu_custom_call" | custom-call | flops 103079215104 | bytes 67108864 | tf_op jit(solution)/shard_map/attend_backward/pallas_call | solution.py:501
  283.4 14.0 %input_gradient.1 = (f32[1024,1024]{1,0:T(8,128)}, f32[64,256]{1,0:T(8,128)S(1)}) custom-call(s32[5]{0:T(128)S(1)} %pad_add_fusion.index_ref.start_ref, bf16[1024,512]{1,0:T(8,128)(2,1)S(1)} %get-tuple-element.395.refs_0_, bf16[1024,512]{1,0:T(8,128)(2,1)S(1)} %get-tuple-element.396.refs_1_, bf16[1024,512]{1,0:T(8,128)(2,1)S(1)} %copy-done.66, ...), custom_call_target="tpu_custom_call" | custom-call | flops 51539607552 | bytes 184549376 | tf_op jit(solution)/shard_map/input_gradient/pallas_call | solution.py:1017
  300.7 1.6 collective-permute-start.61
  302.5 9.4 %collective-permute-done.57 = bf16[2,64,1024]{2,1,0:T(8,128)(2,1)S(1)} collective-permute-done((bf16[2,64,1024]{2,1,0:T(8,128)(2,1)S(1)}, bf16[2,64,1024]{2,1,0:T(8,128)(2,1)S(1)}, u32[]{:S(2)}, u32[]{:S(2)}) %collective-permute-start.57) | collective-permute-done | bytes 262176 | tf_op jit(solution)/shard_map/ppermute | solution.py:68
  312.0 1.7 collective-permute-start.63
  317.9 15.0 %block_output.1 = bf16[1024,1024]{1,0:T(8,128)(2,1)} custom-call(s32[5]{0:T(128)S(1)} %pad_add_fusion.index_ref.start_ref, bf16[2,256,1024]{2,1,0:T(8,128)(2,1)} %copy-done.1, bf16[2,256,1024]{2,1,0:T(8,128)(2,1)} %copy-done.8, bf16[2,128,1024]{2,1,0:T(8,128)(2,1)S(1)} %copy-done.19, bf16[2,128,1024]{2,1,0:T(8,128)(2,1)S(1)} %copy-done.22, ...), custom_call_target="tpu_custom_call" | custom-call | flops 68719476736 | bytes 184549376 | tf_op jit(solution)/shard_map/block_output/pallas_call | solution.py:930
  334.0 5.8 %collective-permute-done.60 = bf16[5,128,512]{2,1,0:T(8,128)(2,1)S(1)} collective-permute-done((bf16[5,128,512]{2,1,0:T(8,128)(2,1)S(1)}, bf16[5,128,512]{2,1,0:T(8,128)(2,1)S(1)}, u32[]{:S(2)}, u32[]{:S(2)}) %collective-permute-start.60) | collective-permute-done | bytes 655392 | tf_op jit(solution)/shard_map/ppermute | solution.py:68
  341.3 1.6 collective-permute-start.65
  343.5 2.9 place_hidden_first.1
  346.4 2.4 collective-permute-done.66
  348.9 1.7 collective-permute-start.71
  350.6 1.6 collective-permute-start.72
  354.7 10.0 %collective-permute-done.67.other_ref = bf16[2,2,64,1024]{3,2,1,0:T(8,128)(2,1)S(1)} collective-permute-done((bf16[2,2,64,1024]{3,2,1,0:T(8,128)(2,1)S(1)}, bf16[2,2,64,1024]{3,2,1,0:T(8,128)(2,1)S(1)}, u32[]{:S(2)}, u32[]{:S(2)}) %collective-permute-start.67) | collective-permute-done | bytes 524320 | tf_op jit(solution)/shard_map/ppermute | solution.py:68
  364.6 2.0 place_hidden_second.1
  369.1 3.1 collective-permute-done.64
  372.2 1.7 collective-permute-start.75
  375.5 2.0 place_hidden_third.1
  378.6 2.9 collective-permute-done.73
  382.7 3.6 collective-permute-done.74
  389.5 4.2 %collective-permute-done.77 = bf16[3,64,512]{2,1,0:T(8,128)(2,1)S(1)} collective-permute-done((bf16[3,64,512]{2,1,0:T(8,128)(2,1)S(1)}, bf16[3,64,512]{2,1,0:T(8,128)(2,1)S(1)}, u32[]{:S(2)}, u32[]{:S(2)}) %collective-permute-start.77) | collective-permute-done | bytes 196640 | tf_op jit(solution)/shard_map/ppermute | solution.py:68
  395.5 5.7 %collective-permute-done.78.other_ref = bf16[2,5,64,512]{3,2,1,0:T(8,128)(2,1)S(1)} collective-permute-done((bf16[2,5,64,512]{3,2,1,0:T(8,128)(2,1)S(1)}, bf16[2,5,64,512]{3,2,1,0:T(8,128)(2,1)S(1)}, u32[]{:S(2)}, u32[]{:S(2)}) %collective-permute-start.78) | collective-permute-done | bytes 655392 | tf_op jit(solution)/shard_map/ppermute | solution.py:68
  401.3 2.2 place_fourth.1
  403.5 2.0 collective-permute-done.79.other_ref
  405.5 1.8 place_last.1
  (465 shorter events, 83.6 us)
Async XLA Ops:
  7.4 20.3 %collective-permute-start.6 = (bf16[256,1536]{1,0:T(8,128)(2,1)}, bf16[256,1536]{1,0:T(8,128)(2,1)}, u32[]{:S(2)}, u32[]{:S(2)}) collective-permute-start(bf16[256,1536]{1,0:T(8,128)(2,1)} %pad_maximum_fusion.9.refs_0_.refs_6_), channel_id=1, source_target_pairs={{0,16},{8,24},{16,0},{24,8},{1,17},{9,25},{17,1},{25,9},{2,18},{10... | collective-permute-start | bytes 2359304 | tf_op jit(solution)/shard_map/ppermute | solution.py:68
  7.6 21.2 %collective-permute-start.5 = (bf16[256,1536]{1,0:T(8,128)(2,1)}, bf16[256,1536]{1,0:T(8,128)(2,1)}, u32[]{:S(2)}, u32[]{:S(2)}) collective-permute-start(bf16[256,1536]{1,0:T(8,128)(2,1)} %pad_maximum_fusion.9.refs_0_.refs_6_), channel_id=1, source_target_pairs={{0,8},{8,0},{16,24},{24,16},{1,9},{9,1},{17,25},{25,17},{2,10},{10... | collective-permute-start | bytes 2359304 | tf_op jit(solution)/shard_map/ppermute | solution.py:68
  39.5 14.5 %collective-permute-start.8 = (bf16[128,1536]{1,0:T(8,128)(2,1)S(1)}, bf16[128,1536]{1,0:T(8,128)(2,1)S(1)}, u32[]{:S(2)}, u32[]{:S(2)}) collective-permute-start(bf16[128,1536]{1,0:T(8,128)(2,1)S(1)} %collective-permute-done.3.refs_2_.refs_12_), channel_id=1, source_target_pairs={{0,1},{1,0},{2,3},{3,2},{4,5},{5,4},{6,7},{7,6},{8,9},{9,8},{10,11... | collective-permute-start | bytes 1179656 | tf_op jit(solution)/shard_map/ppermute | solution.py:68
  41.1 15.3 %collective-permute-start.10 = (bf16[2,256,1024]{2,1,0:T(8,128)(2,1)S(1)}, bf16[2,256,1024]{2,1,0:T(8,128)(2,1)S(1)}, u32[]{:S(2)}, u32[]{:S(2)}) collective-permute-start(bf16[2,256,1024]{2,1,0:T(8,128)(2,1)S(1)} %pad_maximum_fusion.1.refs_0_), channel_id=1, source_target_pairs={{0,8},{8,0},{16,24},{24,16},{1,9},{9,1},{17,25},{25,17},{2,10},{10... | collective-permute-start | bytes 3145736 | tf_op jit(solution)/shard_map/ppermute | solution.py:68
  41.1 14.3 %collective-permute-start.9 = (bf16[2,128,1024]{2,1,0:T(8,128)(2,1)S(1)}, bf16[2,128,1024]{2,1,0:T(8,128)(2,1)S(1)}, u32[]{:S(2)}, u32[]{:S(2)}) collective-permute-start(bf16[2,128,1024]{2,1,0:T(8,128)(2,1)S(1)} %copy-done.101), channel_id=1, source_target_pairs={{0,16},{8,24},{16,0},{24,8},{1,17},{9,25},{17,1},{25,9},{2,18},{10... | collective-permute-start | bytes 1572872 | tf_op jit(solution)/shard_map/ppermute | solution.py:68
  56.4 21.6 %collective-permute-start.15 = (bf16[2,128,1024]{2,1,0:T(8,128)(2,1)S(1)}, bf16[2,128,1024]{2,1,0:T(8,128)(2,1)S(1)}, u32[]{:S(2)}, u32[]{:S(2)}) collective-permute-start(bf16[2,128,1024]{2,1,0:T(8,128)(2,1)S(1)} %collective-permute-done.9.refs_2_), channel_id=1, source_target_pairs={{0,1},{1,0},{2,3},{3,2},{4,5},{5,4},{6,7},{7,6},{8,9},{9,8},{10,11... | collective-permute-start | bytes 1572872 | tf_op jit(solution)/shard_map/ppermute | solution.py:68
  64.2 14.3 %collective-permute-start.18 = (bf16[2,256,1024]{2,1,0:T(8,128)(2,1)S(1)}, bf16[2,256,1024]{2,1,0:T(8,128)(2,1)S(1)}, u32[]{:S(2)}, u32[]{:S(2)}) collective-permute-start(bf16[2,256,1024]{2,1,0:T(8,128)(2,1)S(1)} %pad_maximum_fusion.2.refs_0_.refs_6_), channel_id=1, source_target_pairs={{0,8},{8,0},{16,24},{24,16},{1,9},{9,1},{17,25},{25,17},{2,10},{10... | collective-permute-start | bytes 3145736 | tf_op jit(solution)/shard_map/ppermute | solution.py:68
  89.1 21.6 %collective-permute-start.23 = (bf16[2,256,1024]{2,1,0:T(8,128)(2,1)S(1)}, bf16[2,256,1024]{2,1,0:T(8,128)(2,1)S(1)}, u32[]{:S(2)}, u32[]{:S(2)}) collective-permute-start(bf16[2,256,1024]{2,1,0:T(8,128)(2,1)S(1)} %pad_maximum_fusion.3.refs_0_.refs_12_), channel_id=1, source_target_pairs={{0,8},{8,0},{16,24},{24,16},{1,9},{9,1},{17,25},{25,17},{2,10},{10... | collective-permute-start | bytes 3145736 | tf_op jit(solution)/shard_map/ppermute | solution.py:68
  89.4 21.0 %collective-permute-start.22 = (bf16[2,128,1024]{2,1,0:T(8,128)(2,1)S(1)}, bf16[2,128,1024]{2,1,0:T(8,128)(2,1)S(1)}, u32[]{:S(2)}, u32[]{:S(2)}) collective-permute-start(bf16[2,128,1024]{2,1,0:T(8,128)(2,1)S(1)} %copy-done.103), channel_id=1, source_target_pairs={{0,16},{8,24},{16,0},{24,8},{1,17},{9,25},{17,1},{25,9},{2,18},{10... | collective-permute-start | bytes 1572872 | tf_op jit(solution)/shard_map/ppermute | solution.py:68
  90.3 19.8 %collective-permute-start.21 = (bf16[2,128,1024]{2,1,0:T(8,128)(2,1)S(1)}, bf16[2,128,1024]{2,1,0:T(8,128)(2,1)S(1)}, u32[]{:S(2)}, u32[]{:S(2)}) collective-permute-start(bf16[2,128,1024]{2,1,0:T(8,128)(2,1)S(1)} %collective-permute-done.17.refs_2_.refs_8_), channel_id=1, source_target_pairs={{0,1},{1,0},{2,3},{3,2},{4,5},{5,4},{6,7},{7,6},{8,9},{9,8},{10,11... | collective-permute-start | bytes 1572872 | tf_op jit(solution)/shard_map/ppermute | solution.py:68
  91.5 23.3 %collective-permute-start.25 = (bf16[2,256,1024]{2,1,0:T(8,128)(2,1)S(1)}, bf16[2,256,1024]{2,1,0:T(8,128)(2,1)S(1)}, u32[]{:S(2)}, u32[]{:S(2)}) collective-permute-start(bf16[2,256,1024]{2,1,0:T(8,128)(2,1)S(1)} %pad_maximum_fusion.4.refs_0_.refs_18_), channel_id=1, source_target_pairs={{0,8},{8,0},{16,24},{24,16},{1,9},{9,1},{17,25},{25,17},{2,10},{10... | collective-permute-start | bytes 3145736 | tf_op jit(solution)/shard_map/ppermute | solution.py:68
  91.6 23.2 %collective-permute-start.24 = (bf16[2,128,1024]{2,1,0:T(8,128)(2,1)S(1)}, bf16[2,128,1024]{2,1,0:T(8,128)(2,1)}, u32[]{:S(2)}, u32[]{:S(2)}) collective-permute-start(bf16[2,128,1024]{2,1,0:T(8,128)(2,1)S(1)} %copy-done.102), channel_id=1, source_target_pairs={{0,16},{8,24},{16,0},{24,8},{1,17},{9,25},{17,1},{25,9},{2,18},{10... | collective-permute-start | bytes 1572872 | tf_op jit(solution)/shard_map/ppermute | solution.py:68
  110.7 21.7 %collective-permute-start.29 = (bf16[2,128,1024]{2,1,0:T(8,128)(2,1)S(1)}, bf16[2,128,1024]{2,1,0:T(8,128)(2,1)S(1)}, u32[]{:S(2)}, u32[]{:S(2)}) collective-permute-start(bf16[2,128,1024]{2,1,0:T(8,128)(2,1)S(1)} %collective-permute-done.22.refs_2_.refs_14_), channel_id=1, source_target_pairs={{0,1},{1,0},{2,3},{3,2},{4,5},{5,4},{6,7},{7,6},{8,9},{9,8},{10,11... | collective-permute-start | bytes 1572872 | tf_op jit(solution)/shard_map/ppermute | solution.py:68
  114.8 20.0 %collective-permute-start.28 = (bf16[2,2,256,1024]{3,2,1,0:T(8,128)(2,1)}, bf16[2,2,256,1024]{3,2,1,0:T(8,128)(2,1)}, u32[]{:S(2)}, u32[]{:S(2)}) collective-permute-start(bf16[2,2,256,1024]{3,2,1,0:T(8,128)(2,1)} %get-tuple-element.300), channel_id=1, source_target_pairs={{0,8},{8,0},{16,24},{24,16},{1,9},{9,1},{17,25},{25,17},{2,10},{10... | collective-permute-start | bytes 6291464 | tf_op jit(solution)/shard_map/ppermute | solution.py:68
  133.1 22.6 %collective-permute-start.33 = (bf16[2,128,1024]{2,1,0:T(8,128)(2,1)}, bf16[2,128,1024]{2,1,0:T(8,128)(2,1)}, u32[]{:S(2)}, u32[]{:S(2)}) collective-permute-start(bf16[2,128,1024]{2,1,0:T(8,128)(2,1)} %collective-permute-done.24.refs_2_.refs_20_), channel_id=1, source_target_pairs={{0,1},{1,0},{2,3},{3,2},{4,5},{5,4},{6,7},{7,6},{8,9},{9,8},{10,11... | collective-permute-start | bytes 1572872 | tf_op jit(solution)/shard_map/ppermute | solution.py:68
  134.6 21.8 %collective-permute-start.32 = (bf16[2,2,256,1024]{3,2,1,0:T(8,128)(2,1)}, bf16[2,2,256,1024]{3,2,1,0:T(8,128)(2,1)}, u32[]{:S(2)}, u32[]{:S(2)}) collective-permute-start(bf16[2,2,256,1024]{3,2,1,0:T(8,128)(2,1)} %get-tuple-element.312), channel_id=1, source_target_pairs={{0,8},{8,0},{16,24},{24,16},{1,9},{9,1},{17,25},{25,17},{2,10},{10... | collective-permute-start | bytes 6291464 | tf_op jit(solution)/shard_map/ppermute | solution.py:68
  138.1 26.2 %collective-permute-start.34 = (bf16[2,256,1024]{2,1,0:T(8,128)(2,1)}, bf16[2,256,1024]{2,1,0:T(8,128)(2,1)S(1)}, u32[]{:S(2)}, u32[]{:S(2)}) collective-permute-start(bf16[2,256,1024]{2,1,0:T(8,128)(2,1)} %get-tuple-element.314), channel_id=1, source_target_pairs={{0,16},{8,24},{16,0},{24,8},{1,17},{9,25},{17,1},{25,9},{2,18},{10... | collective-permute-start | bytes 3145736 | tf_op jit(solution)/shard_map/ppermute | solution.py:68
  156.3 31.8 %collective-permute-start.37 = (bf16[2,2,256,1024]{3,2,1,0:T(8,128)(2,1)}, bf16[2,2,256,1024]{3,2,1,0:T(8,128)(2,1)S(1)}, u32[]{:S(2)}, u32[]{:S(2)}) collective-permute-start(bf16[2,2,256,1024]{3,2,1,0:T(8,128)(2,1)} %get-tuple-element.325), channel_id=1, source_target_pairs={{0,8},{8,0},{16,24},{24,16},{1,9},{9,1},{17,25},{25,17},{2,10},{10... | collective-permute-start | bytes 6291464 | tf_op jit(solution)/shard_map/ppermute | solution.py:68
  158.9 27.2 %collective-permute-start.38 = (bf16[2,256,1024]{2,1,0:T(8,128)(2,1)S(1)}, bf16[2,256,1024]{2,1,0:T(8,128)(2,1)S(1)}, u32[]{:S(2)}, u32[]{:S(2)}) collective-permute-start(bf16[2,256,1024]{2,1,0:T(8,128)(2,1)S(1)} %get-tuple-element.326), channel_id=1, source_target_pairs={{0,16},{8,24},{16,0},{24,8},{1,17},{9,25},{17,1},{25,9},{2,18},{10... | collective-permute-start | bytes 3145736 | tf_op jit(solution)/shard_map/ppermute | solution.py:68
  181.7 38.5 %collective-permute-start.41 = (bf16[2,2,256,1024]{3,2,1,0:T(8,128)(2,1)}, bf16[2,2,256,1024]{3,2,1,0:T(8,128)(2,1)S(1)}, u32[]{:S(2)}, u32[]{:S(2)}) collective-permute-start(bf16[2,2,256,1024]{3,2,1,0:T(8,128)(2,1)} %get-tuple-element.340), channel_id=1, source_target_pairs={{0,8},{8,0},{16,24},{24,16},{1,9},{9,1},{17,25},{25,17},{2,10},{10... | collective-permute-start | bytes 6291464 | tf_op jit(solution)/shard_map/ppermute | solution.py:68
  187.6 30.5 %collective-permute-start.43 = (bf16[4,128,1024]{2,1,0:T(8,128)(2,1)}, bf16[4,128,1024]{2,1,0:T(8,128)(2,1)S(1)}, u32[]{:S(2)}, u32[]{:S(2)}) collective-permute-start(bf16[4,128,1024]{2,1,0:T(8,128)(2,1)} %pad_maximum_fusion.5), channel_id=1, source_target_pairs={{0,1},{1,0},{2,3},{3,2},{4,5},{5,4},{6,7},{7,6},{8,9},{9,8},{10,11... | collective-permute-start | bytes 3145736 | tf_op jit(solution)/shard_map/ppermute | solution.py:68
  189.4 30.8 %collective-permute-start.42 = (bf16[2,256,1024]{2,1,0:T(8,128)(2,1)}, bf16[2,256,1024]{2,1,0:T(8,128)(2,1)S(1)}, u32[]{:S(2)}, u32[]{:S(2)}) collective-permute-start(bf16[2,256,1024]{2,1,0:T(8,128)(2,1)} %get-tuple-element.341), channel_id=1, source_target_pairs={{0,16},{8,24},{16,0},{24,8},{1,17},{9,25},{17,1},{25,9},{2,18},{10... | collective-permute-start | bytes 3145736 | tf_op jit(solution)/shard_map/ppermute | solution.py:68
  218.1 27.8 %collective-permute-start.45 = (bf16[2,2,256,512]{3,2,1,0:T(8,128)(2,1)}, bf16[2,2,256,512]{3,2,1,0:T(8,128)(2,1)S(1)}, u32[]{:S(2)}, u32[]{:S(2)}) collective-permute-start(bf16[2,2,256,512]{3,2,1,0:T(8,128)(2,1)} %get-tuple-element.357), channel_id=1, source_target_pairs={{0,8},{8,0},{16,24},{24,16},{1,9},{9,1},{17,25},{25,17},{2,10},{10... | collective-permute-start | bytes 3145736 | tf_op jit(solution)/shard_map/ppermute | solution.py:68
  218.6 27.1 %collective-permute-start.46 = (bf16[4,64,1024]{2,1,0:T(8,128)(2,1)S(1)}, bf16[4,64,1024]{2,1,0:T(8,128)(2,1)S(1)}, u32[]{:S(2)}, u32[]{:S(2)}) collective-permute-start(bf16[4,64,1024]{2,1,0:T(8,128)(2,1)S(1)} %get-tuple-element.358), channel_id=1, source_target_pairs={{0,2},{1,3},{2,0},{3,1},{4,6},{5,7},{6,4},{7,5},{8,10},{9,11},{10,... | collective-permute-start | bytes 1572872 | tf_op jit(solution)/shard_map/ppermute | solution.py:68
  221.1 31.3 %collective-permute-start.44 = (bf16[2,256,1024]{2,1,0:T(8,128)(2,1)S(1)}, bf16[2,256,1024]{2,1,0:T(8,128)(2,1)S(1)}, u32[]{:S(2)}, u32[]{:S(2)}) collective-permute-start(bf16[2,256,1024]{2,1,0:T(8,128)(2,1)S(1)} %get-tuple-element.355), channel_id=1, source_target_pairs={{0,16},{8,24},{16,0},{24,8},{1,17},{9,25},{17,1},{25,9},{2,18},{10... | collective-permute-start | bytes 3145736 | tf_op jit(solution)/shard_map/ppermute | solution.py:68
  221.9 29.2 %collective-permute-start.47 = (bf16[2,128,1024]{2,1,0:T(8,128)(2,1)S(1)}, bf16[2,128,1024]{2,1,0:T(8,128)(2,1)S(1)}, u32[]{:S(2)}, u32[]{:S(2)}) collective-permute-start(bf16[2,128,1024]{2,1,0:T(8,128)(2,1)S(1)} %get-tuple-element.359), channel_id=1, source_target_pairs={{0,1},{1,0},{2,3},{3,2},{4,5},{5,4},{6,7},{7,6},{8,9},{9,8},{10,11... | collective-permute-start | bytes 1572872 | tf_op jit(solution)/shard_map/ppermute | solution.py:68
  245.9 29.9 %collective-permute-start.50 = (bf16[4,64,1024]{2,1,0:T(8,128)(2,1)S(1)}, bf16[4,64,1024]{2,1,0:T(8,128)(2,1)S(1)}, u32[]{:S(2)}, u32[]{:S(2)}) collective-permute-start(bf16[4,64,1024]{2,1,0:T(8,128)(2,1)S(1)} %add.277), channel_id=1, source_target_pairs={{0,4},{1,5},{2,6},{3,7},{4,0},{5,1},{6,2},{7,3},{8,12},{9,13},{10,... | collective-permute-start | bytes 1572872 | tf_op jit(solution)/shard_map/ppermute | solution.py:68
  248.6 29.9 %collective-permute-start.48 = (bf16[2,3,256,512]{3,2,1,0:T(8,128)(2,1)S(1)}, bf16[2,3,256,512]{3,2,1,0:T(8,128)(2,1)S(1)}, u32[]{:S(2)}, u32[]{:S(2)}) collective-permute-start(bf16[2,3,256,512]{3,2,1,0:T(8,128)(2,1)S(1)} %get-tuple-element.373), channel_id=1, source_target_pairs={{0,8},{8,0},{16,24},{24,16},{1,9},{9,1},{17,25},{25,17},{2,10},{10... | collective-permute-start | bytes 4718600 | tf_op jit(solution)/shard_map/ppermute | solution.py:68
  249.7 29.0 %collective-permute-start.49 = (bf16[2,256,512]{2,1,0:T(8,128)(2,1)}, bf16[2,256,512]{2,1,0:T(8,128)(2,1)S(1)}, u32[]{:S(2)}, u32[]{:S(2)}) collective-permute-start(bf16[2,256,512]{2,1,0:T(8,128)(2,1)} %get-tuple-element.374), channel_id=1, source_target_pairs={{0,16},{8,24},{16,0},{24,8},{1,17},{9,25},{17,1},{25,9},{2,18},{10... | collective-permute-start | bytes 1572872 | tf_op jit(solution)/shard_map/ppermute | solution.py:68
  251.3 24.4 %collective-permute-start.51 = (bf16[2,64,1024]{2,1,0:T(8,128)(2,1)S(1)}, bf16[2,64,1024]{2,1,0:T(8,128)(2,1)S(1)}, u32[]{:S(2)}, u32[]{:S(2)}) collective-permute-start(bf16[2,64,1024]{2,1,0:T(8,128)(2,1)S(1)} %get-tuple-element.376), channel_id=1, source_target_pairs={{0,2},{1,3},{2,0},{3,1},{4,6},{5,7},{6,4},{7,5},{8,10},{9,11},{10,... | collective-permute-start | bytes 786440 | tf_op jit(solution)/shard_map/ppermute | solution.py:68
  252.8 25.7 %collective-permute-start.52 = (bf16[2,128,1024]{2,1,0:T(8,128)(2,1)S(1)}, bf16[2,128,1024]{2,1,0:T(8,128)(2,1)S(1)}, u32[]{:S(2)}, u32[]{:S(2)}) collective-permute-start(bf16[2,128,1024]{2,1,0:T(8,128)(2,1)S(1)} %get-tuple-element.377), channel_id=1, source_target_pairs={{0,1},{1,0},{2,3},{3,2},{4,5},{5,4},{6,7},{7,6},{8,9},{9,8},{10,11... | collective-permute-start | bytes 1572872 | tf_op jit(solution)/shard_map/ppermute | solution.py:68
  276.0 21.4 %collective-permute-start.56 = (bf16[2,64,1024]{2,1,0:T(8,128)(2,1)S(1)}, bf16[2,64,1024]{2,1,0:T(8,128)(2,1)S(1)}, u32[]{:S(2)}, u32[]{:S(2)}) collective-permute-start(bf16[2,64,1024]{2,1,0:T(8,128)(2,1)S(1)} %add.286), channel_id=1, source_target_pairs={{0,4},{1,5},{2,6},{3,7},{4,0},{5,1},{6,2},{7,3},{8,12},{9,13},{10,... | collective-permute-start | bytes 786440 | tf_op jit(solution)/shard_map/ppermute | solution.py:68
  277.4 22.2 %collective-permute-start.55 = (bf16[4,64,1024]{2,1,0:T(8,128)(2,1)S(1)}, bf16[4,64,1024]{2,1,0:T(8,128)(2,1)}, u32[]{:S(2)}, u32[]{:S(2)}) collective-permute-start(bf16[4,64,1024]{2,1,0:T(8,128)(2,1)S(1)} %add.285), channel_id=1, source_target_pairs={{0,2},{1,3},{2,0},{3,1},{4,6},{5,7},{6,4},{7,5},{8,10},{9,11},{10,... | collective-permute-start | bytes 1572872 | tf_op jit(solution)/shard_map/ppermute | solution.py:68
  278.5 37.1 %collective-permute-start.53 = (bf16[2,3,256,512]{3,2,1,0:T(8,128)(2,1)S(1)}, bf16[2,3,256,512]{3,2,1,0:T(8,128)(2,1)S(1)}, u32[]{:S(2)}, u32[]{:S(2)}) collective-permute-start(bf16[2,3,256,512]{3,2,1,0:T(8,128)(2,1)S(1)} %get-tuple-element.390), channel_id=1, source_target_pairs={{0,8},{8,0},{16,24},{24,16},{1,9},{9,1},{17,25},{25,17},{2,10},{10... | collective-permute-start | bytes 4718600 | tf_op jit(solution)/shard_map/ppermute | solution.py:68
  279.0 34.7 %collective-permute-start.54 = (bf16[3,256,512]{2,1,0:T(8,128)(2,1)S(1)}, bf16[3,256,512]{2,1,0:T(8,128)(2,1)S(1)}, u32[]{:S(2)}, u32[]{:S(2)}) collective-permute-start(bf16[3,256,512]{2,1,0:T(8,128)(2,1)S(1)} %get-tuple-element.391), channel_id=1, source_target_pairs={{0,16},{8,24},{16,0},{24,8},{1,17},{9,25},{17,1},{25,9},{2,18},{10... | collective-permute-start | bytes 2359304 | tf_op jit(solution)/shard_map/ppermute | solution.py:68
  297.5 35.4 %collective-permute-start.62 = (bf16[2,64,1024]{2,1,0:T(8,128)(2,1)S(1)}, bf16[2,64,1024]{2,1,0:T(8,128)(2,1)S(1)}, u32[]{:S(2)}, u32[]{:S(2)}) collective-permute-start(bf16[2,64,1024]{2,1,0:T(8,128)(2,1)S(1)} %add.297), channel_id=1, source_target_pairs={{0,2},{1,3},{2,0},{3,1},{4,6},{5,7},{6,4},{7,5},{8,10},{9,11},{10,... | collective-permute-start | bytes 786440 | tf_op jit(solution)/shard_map/ppermute | solution.py:68
  300.7 42.8 %collective-permute-start.61 = (bf16[2,4,64,1024]{3,2,1,0:T(8,128)(2,1)S(1)}, bf16[2,4,64,1024]{3,2,1,0:T(8,128)(2,1)S(1)}, u32[]{:S(2)}, u32[]{:S(2)}) collective-permute-start(bf16[2,4,64,1024]{3,2,1,0:T(8,128)(2,1)S(1)} %pad_maximum_fusion.6.pair_ref), channel_id=1, source_target_pairs={{0,1},{1,0},{2,3},{3,2},{4,5},{5,4},{6,7},{7,6},{8,9},{9,8},{10,11... | collective-permute-start | bytes 3145736 | tf_op jit(solution)/shard_map/ppermute | solution.py:68
  312.0 20.9 %collective-permute-start.63 = (bf16[2,64,1024]{2,1,0:T(8,128)(2,1)S(1)}, bf16[2,64,1024]{2,1,0:T(8,128)(2,1)S(1)}, u32[]{:S(2)}, u32[]{:S(2)}) collective-permute-start(bf16[2,64,1024]{2,1,0:T(8,128)(2,1)S(1)} %add.298), channel_id=1, source_target_pairs={{0,4},{1,5},{2,6},{3,7},{4,0},{5,1},{6,2},{7,3},{8,12},{9,13},{10,... | collective-permute-start | bytes 786440 | tf_op jit(solution)/shard_map/ppermute | solution.py:68
  314.0 25.9 %collective-permute-start.60 = (bf16[5,128,512]{2,1,0:T(8,128)(2,1)S(1)}, bf16[5,128,512]{2,1,0:T(8,128)(2,1)S(1)}, u32[]{:S(2)}, u32[]{:S(2)}) collective-permute-start(bf16[5,128,512]{2,1,0:T(8,128)(2,1)S(1)} %pad_maximum_fusion.10), channel_id=1, source_target_pairs={{0,1},{1,0},{2,3},{3,2},{4,5},{5,4},{6,7},{7,6},{8,9},{9,8},{10,11... | collective-permute-start | bytes 1966088 | tf_op jit(solution)/shard_map/ppermute | solution.py:68
  315.9 25.2 %collective-permute-start.59 = (bf16[3,256,512]{2,1,0:T(8,128)(2,1)S(1)}, bf16[3,256,512]{2,1,0:T(8,128)(2,1)S(1)}, u32[]{:S(2)}, u32[]{:S(2)}) collective-permute-start(bf16[3,256,512]{2,1,0:T(8,128)(2,1)S(1)} %get-tuple-element.419), channel_id=1, source_target_pairs={{0,16},{8,24},{16,0},{24,8},{1,17},{9,25},{17,1},{25,9},{2,18},{10... | collective-permute-start | bytes 2359304 | tf_op jit(solution)/shard_map/ppermute | solution.py:68
  333.0 15.9 %collective-permute-start.68 = (bf16[2,64,1024]{2,1,0:T(8,128)(2,1)S(1)}, bf16[2,64,1024]{2,1,0:T(8,128)(2,1)S(1)}, u32[]{:S(2)}, u32[]{:S(2)}) collective-permute-start(bf16[2,64,1024]{2,1,0:T(8,128)(2,1)S(1)} %add.304), channel_id=1, source_target_pairs={{0,2},{1,3},{2,0},{3,1},{4,6},{5,7},{6,4},{7,5},{8,10},{9,11},{10,... | collective-permute-start | bytes 786440 | tf_op jit(solution)/shard_map/ppermute | solution.py:68
  343.0 21.7 %collective-permute-start.67 = (bf16[2,2,64,1024]{3,2,1,0:T(8,128)(2,1)S(1)}, bf16[2,2,64,1024]{3,2,1,0:T(8,128)(2,1)S(1)}, u32[]{:S(2)}, u32[]{:S(2)}) collective-permute-start(bf16[2,2,64,1024]{3,2,1,0:T(8,128)(2,1)S(1)} %pad_maximum_fusion.12.pair_ref), channel_id=1, source_target_pairs={{0,1},{1,0},{2,3},{3,2},{4,5},{5,4},{6,7},{7,6},{8,9},{9,8},{10,11... | collective-permute-start | bytes 1572872 | tf_op jit(solution)/shard_map/ppermute | solution.py:68
  348.9 17.8 %collective-permute-start.71 = (bf16[5,64,512]{2,1,0:T(8,128)(2,1)S(1)}, bf16[5,64,512]{2,1,0:T(8,128)(2,1)S(1)}, u32[]{:S(2)}, u32[]{:S(2)}) collective-permute-start(bf16[5,64,512]{2,1,0:T(8,128)(2,1)S(1)} %add.308), channel_id=1, source_target_pairs={{0,4},{1,5},{2,6},{3,7},{4,0},{5,1},{6,2},{7,3},{8,12},{9,13},{10,... | collective-permute-start | bytes 983048 | tf_op jit(solution)/shard_map/ppermute | solution.py:68
  350.6 24.9 %collective-permute-start.72 = (bf16[2,2,64,1024]{3,2,1,0:T(8,128)(2,1)S(1)}, bf16[2,2,64,1024]{3,2,1,0:T(8,128)(2,1)S(1)}, u32[]{:S(2)}, u32[]{:S(2)}) collective-permute-start(bf16[2,2,64,1024]{3,2,1,0:T(8,128)(2,1)S(1)} %pad_maximum_fusion.13.pair_ref), channel_id=1, source_target_pairs={{0,1},{1,0},{2,3},{3,2},{4,5},{5,4},{6,7},{7,6},{8,9},{9,8},{10,11... | collective-permute-start | bytes 1572872 | tf_op jit(solution)/shard_map/ppermute | solution.py:68
  353.5 18.7 %collective-permute-start.70 = (bf16[3,64,512]{2,1,0:T(8,128)(2,1)S(1)}, bf16[3,64,512]{2,1,0:T(8,128)(2,1)S(1)}, u32[]{:S(2)}, u32[]{:S(2)}) collective-permute-start(bf16[3,64,512]{2,1,0:T(8,128)(2,1)S(1)} %get-tuple-element.454), channel_id=1, source_target_pairs={{0,2},{1,3},{2,0},{3,1},{4,6},{5,7},{6,4},{7,5},{8,10},{9,11},{10,... | collective-permute-start | bytes 589832 | tf_op jit(solution)/shard_map/ppermute | solution.py:68
  366.8 19.5 %collective-permute-start.76 = (bf16[5,64,512]{2,1,0:T(8,128)(2,1)S(1)}, bf16[5,64,512]{2,1,0:T(8,128)(2,1)S(1)}, u32[]{:S(2)}, u32[]{:S(2)}) collective-permute-start(bf16[5,64,512]{2,1,0:T(8,128)(2,1)S(1)} %add.312), channel_id=1, source_target_pairs={{0,2},{1,3},{2,0},{3,1},{4,6},{5,7},{6,4},{7,5},{8,10},{9,11},{10,... | collective-permute-start | bytes 983048 | tf_op jit(solution)/shard_map/ppermute | solution.py:68
  372.2 15.6 %collective-permute-start.75 = (bf16[3,64,512]{2,1,0:T(8,128)(2,1)S(1)}, bf16[3,64,512]{2,1,0:T(8,128)(2,1)S(1)}, u32[]{:S(2)}, u32[]{:S(2)}) collective-permute-start(bf16[3,64,512]{2,1,0:T(8,128)(2,1)S(1)} %add.311), channel_id=1, source_target_pairs={{0,4},{1,5},{2,6},{3,7},{4,0},{5,1},{6,2},{7,3},{8,12},{9,13},{10,... | collective-permute-start | bytes 589832 | tf_op jit(solution)/shard_map/ppermute | solution.py:68
  386.4 14.9 %collective-permute-start.78 = (bf16[2,5,64,512]{3,2,1,0:T(8,128)(2,1)S(1)}, bf16[2,5,64,512]{3,2,1,0:T(8,128)(2,1)S(1)}, u32[]{:S(2)}, u32[]{:S(2)}) collective-permute-start(bf16[2,5,64,512]{3,2,1,0:T(8,128)(2,1)S(1)} %pad_maximum_fusion.11.pair_ref), channel_id=1, source_target_pairs={{0,1},{1,0},{2,3},{3,2},{4,5},{5,4},{6,7},{7,6},{8,9},{9,8},{10,11... | collective-permute-start | bytes 1966088 | tf_op jit(solution)/shard_map/ppermute | solution.py:68
  (161 other events, 1331.2 us)

commit v5 on v4

--- a/solution.py
+++ b/solution.py
@@ -1278,7 +1278,6 @@
     fourth_sum = RepSum(moves, [out_sum, a_sum])
     first_sum.finish()
     second_sum.spread()
-    third_sum.add()
     block_out = block_output(moves.index, all_pieces, hidden, middle, vec)
     moves.ran(block_out)
 
@@ -1295,20 +1294,21 @@
     last_sum = RepSum(moves, [b_sum])
     fourth_sum.split()
     second_sum.finish()
-    third_sum.spread()
+    third_sum.add()
     vec_sum = VecSum(moves, vec_grads)
     grads = place_hidden((0, 1), first_sum.pieces(), None, "place_hidden_first")
     last_sum.split()
     fourth_sum.add()
-    third_sum.finish()
+    third_sum.spread()
     vec_sum.step()
     grads = place_hidden((2,), second_sum.pieces(), grads, "place_hidden_second")
     last_sum.add()
     fourth_sum.spread()
+    third_sum.finish()
     vec_sum.step()
-    grad_up, grad_down = place_hidden((3,), third_sum.pieces(), grads, "place_hidden_third")
     fourth_sum.finish()
     last_sum.spread()
+    grad_up, grad_down = place_hidden((3,), third_sum.pieces(), grads, "place_hidden_third")
     vec_sum.step()
     last_sum.finish()
     vec_sum = vec_sum.rest()

time: 416 us -> 431 us (1.036)
  waiting for transfers between devices: 76.4 us -> 96.4 us
    ppermute x80, waiting for transfers between devices: 76.4 us -> 96.4 us  [flip(): return lax.ppermute(value, axis, [(i, i ^ bit) for i in range(size)])]
    unnamed x262 -> x250, local copies, waits for them, and re-layouts: 12.4 us -> 8.85 us
  transfers between devices with their start and end apart: 80 -> 80, of which waited for: 24 -> 26; matrix products, arithmetic and copies ran while one was open for 6% -> 6% of each run, Pallas kernels for 53% -> 51%
where the time goes in v5:
time: 431 us; the launch traced here: 423 us
  Pallas kernels  224 us (52%)
  waiting for transfers between devices  96.4 us (22%)
  starting transfers between devices  64.2 us (15%)
  other arithmetic  18.7 us (4%)
  local copies, waits for them, and re-layouts  17.3 us (4%)
    ppermute x80, waiting for transfers between devices, flip(): return lax.ppermute(value, axis, [(i, i ^ bit) for i in range(size)])  96.4 us
    pallas_call x4, Pallas kernels, hidden_chunk(): pl.pallas_call(functools.partial(hidden_body, chunk, fresh), grid_spec=pl...  69 us
    ppermute x80, starting transfers between devices, flip(): return lax.ppermute(value, axis, [(i, i ^ bit) for i in range(size)])  64.2 us
    pallas_call x2, Pallas kernels, attend_backward(): pl.pallas_call(functools.partial(attend_backward_body, half * 2 * pairs,...  44.8 us
    pallas_call x1, Pallas kernels, block_back(): pl.pallas_call(functools.partial(block_back_body, blocks=blocks), grid_sp...  27.1 us
    pallas_call x2, Pallas kernels, attend_forward(): pl.pallas_call(functools.partial(attend_forward_body, half * 2 * pairs),...  24.1 us
    pallas_call x1, Pallas kernels, block_output(): pl.pallas_call(block_out_body, grid_spec=pltpu.PrefetchScalarGridSpec(num...  15 us
    pallas_call x1, Pallas kernels, input_gradient(): pl.pallas_call(functools.partial(input_grad_body, blocks=blocks), grid_sp...  14 us
  transfers between devices with their start and end apart: 80, of which 26 were waited for; matrix products, arithmetic and copies ran while one was open for 6% of the time, Pallas kernels for 51%

profile of v5, /device:TPU:0, one launch (start us, length us, event | category | flops | bytes accessed | tf_op | source)
XLA Modules:
  0.0 423.4 jit_solution(18227469594470745683)
XLA Ops:
  0.7 2.4 fusion.13
  4.4 3.0 collective-permute-start.1
  9.2 2.5 slice_bitcast_fusion
  19.2 2.2 first_norm.1
  21.4 6.3 %collective-permute-done.6.refs_2_.refs_8_ = bf16[256,1536]{1,0:T(8,128)(2,1)} collective-permute-done((bf16[256,1536]{1,0:T(8,128)(2,1)}, bf16[256,1536]{1,0:T(8,128)(2,1)}, u32[]{:S(2)}, u32[]{:S(2)}) %collective-permute-start.6) | collective-permute-done | bytes 786464 | tf_op jit(solution)/shard_map/ppermute | solution.py:68
  30.2 6.3 %joined_product.2.q_ref.k_ref.v_ref = bf16[1024,1536]{1,0:T(8,128)(2,1)S(1)} custom-call(s32[5]{0:T(128)S(1)} %pad_add_fusion.index_ref.start_ref, bf16[256,1536]{1,0:T(8,128)(2,1)} %pad_maximum_fusion.9.refs_0_.refs_6_, bf16[256,1536]{1,0:T(8,128)(2,1)} %collective-permute-done.5.refs_1_.refs_7_, bf16[256,1536]{1,0:T(8,128)(2,1)} %collective-permute-done.6.refs_2_.refs_8_, ...), custom_call_target="tpu_custom_call" | custom-call | flops 25769803776 | bytes 92274688 | tf_op jit(solution)/shard_map/joined_product/pallas_call | solution.py:319
  36.5 3.0 collective-permute-done.3.refs_2_.refs_12_
  41.6 12.1 %attend_forward.2 = (bf16[1024,512]{1,0:T(8,128)(2,1)S(1)}, f32[2,4,2,512]{3,2,1,0:T(2,128)S(1)}) custom-call(s32[5]{0:T(128)S(1)} %pad_add_fusion.index_ref.start_ref, bf16[1024,1536]{1,0:T(8,128)(2,1)S(1)} %joined_product.2.q_ref.k_ref.v_ref, bf16[1024,1536]{1,0:T(8,128)(2,1)S(1)} %joined_product.2.q_ref.k_ref.v_ref, ...), custom_call_target="tpu_custom_call" | custom-call | flops 51539607552 | bytes 33554432 | tf_op jit(solution)/shard_map/attend_forward/pallas_call | solution.py:382
  56.9 5.5 %joined_product.3.q_ref.k_ref.v_ref = bf16[1024,1536]{1,0:T(8,128)(2,1)S(1)} custom-call(s32[5]{0:T(128)S(1)} %pad_add_fusion.index_ref.start_ref, bf16[256,1536]{1,0:T(8,128)(2,1)S(1)} %pad_maximum_fusion.8.refs_0_.refs_10_, bf16[256,1536]{1,0:T(8,128)(2,1)S(1)} %collective-permute-done.4.refs_1_.refs_11_, ...), custom_call_target="tpu_custom_call" | custom-call | flops 25769803776 | bytes 92274688 | tf_op jit(solution)/shard_map/joined_product/pallas_call | solution.py:319
  65.3 12.0 %attend_forward.3 = (bf16[1024,512]{1,0:T(8,128)(2,1)S(1)}, f32[2,4,2,512]{3,2,1,0:T(2,128)S(1)}) custom-call(s32[5]{0:T(128)S(1)} %pad_add_fusion.index_ref.start_ref, bf16[1024,1536]{1,0:T(8,128)(2,1)S(1)} %joined_product.3.q_ref.k_ref.v_ref, bf16[1024,1536]{1,0:T(8,128)(2,1)S(1)} %joined_product.3.q_ref.k_ref.v_ref, ...), custom_call_target="tpu_custom_call" | custom-call | flops 51539607552 | bytes 33554432 | tf_op jit(solution)/shard_map/attend_forward/pallas_call | solution.py:382
  79.4 4.8 %middle_product.1 = (f32[1024,1024]{1,0:T(8,128)S(1)}, bf16[1024,1024]{1,0:T(8,128)(2,1)S(1)}, bf16[1024,1024]{1,0:T(8,128)(2,1)S(1)}) custom-call(s32[5]{0:T(128)S(1)} %pad_add_fusion.index_ref.start_ref, bf16[256,1024]{1,0:T(8,128)(2,1)S(1)} %copy-done.5, bf16[256,1024]{1,0:T(8,128)(2,1)S(1)} %collective-permute-done.12.refs_1_, ...), custom_call_target="tpu_custom_call" | custom-call | flops 17179869184 | bytes 117440512 | tf_op jit(solution)/shard_map/middle_product/pallas_call | solution.py:568
  93.0 17.0 %hidden_chunk0.1 = (bf16[1024,4096]{1,0:T(8,128)(2,1)}, bf16[1024,4096]{1,0:T(8,128)(2,1)}, bf16[2,2,256,1024]{3,2,1,0:T(8,128)(2,1)}, bf16[2,2,256,1024]{3,2,1,0:T(8,128)(2,1)}, f32[1,1024]{1,0:T(1,128)S(1)}) custom-call(s32[5]{0:T(128)S(1)} %pad_add_fusion.index_ref.start_ref, bf16[2,256,1024]{2,1,0:T(8,128)(2,1)S(1)} %pad_maximum_fusion.1.refs_0_, ...), custom_call_target="tpu_custom_call" | custom-call | flops 68719476736 | bytes 201326592 | tf_op jit(solution)/shard_map/hidden_chunk0/pallas_call | solution.py:703
  111.2 3.6 collective-permute-done.24.refs_2_.refs_20_
  114.9 17.5 %hidden_chunk1.1 = (bf16[1024,4096]{1,0:T(8,128)(2,1)}, bf16[1024,4096]{1,0:T(8,128)(2,1)}, bf16[2,2,256,1024]{3,2,1,0:T(8,128)(2,1)}, bf16[2,2,256,1024]{3,2,1,0:T(8,128)(2,1)}, f32[1,1024]{1,0:T(1,128)S(1)}) custom-call(s32[5]{0:T(128)S(1)} %pad_add_fusion.index_ref.start_ref, ...), custom_call_target="tpu_custom_call", output_to_operand_aliasing={{0}: (7, {}), {1}: (8, {})} | custom-call | flops 68719476736 | bytes 201326592 | tf_op jit(solution)/shard_map/hidden_chunk1/pallas_call | solution.py:703
  134.8 3.2 slice_add_fusion.3
  138.6 17.1 %hidden_chunk2.1 = (bf16[1024,4096]{1,0:T(8,128)(2,1)}, bf16[1024,4096]{1,0:T(8,128)(2,1)}, bf16[2,2,256,1024]{3,2,1,0:T(8,128)(2,1)}, bf16[2,2,256,1024]{3,2,1,0:T(8,128)(2,1)}, f32[1,1024]{1,0:T(1,128)S(1)}) custom-call(s32[5]{0:T(128)S(1)} %pad_add_fusion.index_ref.start_ref, ...), custom_call_target="tpu_custom_call", output_to_operand_aliasing={{0}: (7, {}), {1}: (8, {})} | custom-call | flops 68719476736 | bytes 201326592 | tf_op jit(solution)/shard_map/hidden_chunk2/pallas_call | solution.py:703
  156.4 2.5 slice_add_fusion.2
  160.4 3.8 collective-permute-done.34
  164.2 17.5 %hidden_chunk3.1 = (bf16[1024,4096]{1,0:T(8,128)(2,1)}, bf16[1024,4096]{1,0:T(8,128)(2,1)}, bf16[2,2,256,1024]{3,2,1,0:T(8,128)(2,1)}, bf16[2,2,256,1024]{3,2,1,0:T(8,128)(2,1)}, f32[1,1024]{1,0:T(1,128)S(1)}) custom-call(s32[5]{0:T(128)S(1)} %pad_add_fusion.index_ref.start_ref, ...), custom_call_target="tpu_custom_call", output_to_operand_aliasing={{0}: (7, {}), {1}: (8, {})} | custom-call | flops 68719476736 | bytes 201326592 | tf_op jit(solution)/shard_map/hidden_chunk3/pallas_call | solution.py:703
  182.2 3.9 collective-permute-done.38
  190.9 27.1 %block_back.1 = (f32[1024,1024]{1,0:T(8,128)}, bf16[1024,1024]{1,0:T(8,128)(2,1)}, bf16[2,2,256,512]{3,2,1,0:T(8,128)(2,1)}, bf16[2,2,256,512]{3,2,1,0:T(8,128)(2,1)}, f32[8,1024]{1,0:T(8,128)S(1)}) custom-call(s32[5]{0:T(128)S(1)} %pad_add_fusion.index_ref.start_ref, bf16[2,256,1024]{2,1,0:T(8,128)(2,1)} %copy-done.1, bf16[2,256,1024]{2,1,0:T(8,128)(2,1)} %copy-done.8, ...), custom_call_target="tpu_custom_call" | custom-call | flops 103079215104 | bytes 268435456 | tf_op jit(solution)/shard_map/block_back/pallas_call | solution.py:848
  223.0 22.4 %attend_backward.2 = (bf16[1024,512]{1,0:T(8,128)(2,1)S(1)}, bf16[1024,512]{1,0:T(8,128)(2,1)S(1)}, bf16[1024,512]{1,0:T(8,128)(2,1)S(1)}, bf16[2,3,256,512]{3,2...) custom-call(s32[5]{0:T(128)S(1)} %pad_add_fusion.index_ref.start_ref, ...), custom_call_target="tpu_custom_call" | custom-call | flops 103079215104 | bytes 67108864 | tf_op jit(solution)/shard_map/attend_backward/pallas_call | solution.py:501
  245.7 2.7 collective-permute-start.50
  253.1 22.4 %attend_backward.3 = (bf16[1024,512]{1,0:T(8,128)(2,1)S(1)}, bf16[1024,512]{1,0:T(8,128)(2,1)S(1)}, bf16[1024,512]{1,0:T(8,128)(2,1)S(1)}, bf16[2,3,256,512]{3,2...) custom-call(s32[5]{0:T(128)S(1)} %pad_add_fusion.index_ref.start_ref, ...), custom_call_target="tpu_custom_call" | custom-call | flops 103079215104 | bytes 67108864 | tf_op jit(solution)/shard_map/attend_backward/pallas_call | solution.py:501
  279.9 14.0 %input_gradient.1 = (f32[1024,1024]{1,0:T(8,128)}, f32[64,256]{1,0:T(8,128)S(1)}) custom-call(s32[5]{0:T(128)S(1)} %pad_add_fusion.index_ref.start_ref, bf16[1024,512]{1,0:T(8,128)(2,1)S(1)} %get-tuple-element.395.refs_0_, bf16[1024,512]{1,0:T(8,128)(2,1)S(1)} %get-tuple-element.396.refs_1_, bf16[1024,512]{1,0:T(8,128)(2,1)S(1)} %get-tuple-element.397.refs_2_, ...), custom_call_target="tpu_custom_call" | custom-call | flops 51539607552 | bytes 184549376 | tf_op jit(solution)/shard_map/input_gradient/pallas_call | solution.py:1017
  300.2 8.2 %collective-permute-done.57 = bf16[2,64,1024]{2,1,0:T(8,128)(2,1)S(1)} collective-permute-done((bf16[2,64,1024]{2,1,0:T(8,128)(2,1)S(1)}, bf16[2,64,1024]{2,1,0:T(8,128)(2,1)S(1)}, u32[]{:S(2)}, u32[]{:S(2)}) %collective-permute-start.57) | collective-permute-done | bytes 262176 | tf_op jit(solution)/shard_map/ppermute | solution.py:68
  310.7 15.0 %block_output.1 = bf16[1024,1024]{1,0:T(8,128)(2,1)} custom-call(s32[5]{0:T(128)S(1)} %pad_add_fusion.index_ref.start_ref, bf16[2,256,1024]{2,1,0:T(8,128)(2,1)} %copy-done.1, bf16[2,256,1024]{2,1,0:T(8,128)(2,1)} %copy-done.8, bf16[2,128,1024]{2,1,0:T(8,128)(2,1)S(1)} %copy-done.19, bf16[2,128,1024]{2,1,0:T(8,128)(2,1)S(1)} %copy-done.22, ...), custom_call_target="tpu_custom_call" | custom-call | flops 68719476736 | bytes 184549376 | tf_op jit(solution)/shard_map/block_output/pallas_call | solution.py:930
  327.4 2.0 collective-permute-start.67
  329.5 6.9 %collective-permute-done.60 = bf16[5,128,512]{2,1,0:T(8,128)(2,1)S(1)} collective-permute-done((bf16[5,128,512]{2,1,0:T(8,128)(2,1)S(1)}, bf16[5,128,512]{2,1,0:T(8,128)(2,1)S(1)}, u32[]{:S(2)}, u32[]{:S(2)}) %collective-permute-start.60) | collective-permute-done | bytes 655392 | tf_op jit(solution)/shard_map/ppermute | solution.py:68
  339.5 2.9 place_hidden_first.1
  343.5 5.6 %collective-permute-done.65 = bf16[5,64,512]{2,1,0:T(8,128)(2,1)S(1)} collective-permute-done((bf16[5,64,512]{2,1,0:T(8,128)(2,1)S(1)}, bf16[5,64,512]{2,1,0:T(8,128)(2,1)S(1)}, u32[]{:S(2)}, u32[]{:S(2)}) %collective-permute-start.65) | collective-permute-done | bytes 327712 | tf_op jit(solution)/shard_map/ppermute | solution.py:68
  350.5 4.5 %collective-permute-done.64 = bf16[3,128,512]{2,1,0:T(8,128)(2,1)S(1)} collective-permute-done((bf16[3,128,512]{2,1,0:T(8,128)(2,1)S(1)}, bf16[3,128,512]{2,1,0:T(8,128)(2,1)S(1)}, u32[]{:S(2)}, u32[]{:S(2)}) %collective-permute-start.64) | collective-permute-done | bytes 393248 | tf_op jit(solution)/shard_map/ppermute | solution.py:68
  355.1 2.0 place_hidden_second.1
  358.8 7.2 %collective-permute-done.70 = bf16[5,64,512]{2,1,0:T(8,128)(2,1)S(1)} collective-permute-done((bf16[5,64,512]{2,1,0:T(8,128)(2,1)S(1)}, bf16[5,64,512]{2,1,0:T(8,128)(2,1)S(1)}, u32[]{:S(2)}, u32[]{:S(2)}) %collective-permute-start.70) | collective-permute-done | bytes 327712 | tf_op jit(solution)/shard_map/ppermute | solution.py:68
  366.1 2.0 collective-permute-start.69
  368.8 3.7 collective-permute-done.63
  372.4 6.7 %collective-permute-done.69 = bf16[3,64,512]{2,1,0:T(8,128)(2,1)S(1)} collective-permute-done((bf16[3,64,512]{2,1,0:T(8,128)(2,1)S(1)}, bf16[3,64,512]{2,1,0:T(8,128)(2,1)S(1)}, u32[]{:S(2)}, u32[]{:S(2)}) %collective-permute-start.69) | collective-permute-done | bytes 196640 | tf_op jit(solution)/shard_map/ppermute | solution.py:68
  381.2 8.3 %collective-permute-done.73 = bf16[3,64,512]{2,1,0:T(8,128)(2,1)S(1)} collective-permute-done((bf16[3,64,512]{2,1,0:T(8,128)(2,1)S(1)}, bf16[3,64,512]{2,1,0:T(8,128)(2,1)S(1)}, u32[]{:S(2)}, u32[]{:S(2)}) %collective-permute-start.73) | collective-permute-done | bytes 196640 | tf_op jit(solution)/shard_map/ppermute | solution.py:68
  389.5 2.0 place_hidden_third.1
  392.1 3.3 collective-permute-done.75
  395.4 1.8 collective-permute-start.76
  397.5 2.0 collective-permute-start.78
  400.8 2.4 collective-permute-done.78
  403.2 1.8 collective-permute-start.79
  406.2 8.7 %collective-permute-done.77.other_ref = bf16[2,5,64,512]{3,2,1,0:T(8,128)(2,1)S(1)} collective-permute-done((bf16[2,5,64,512]{3,2,1,0:T(8,128)(2,1)S(1)}, bf16[2,5,64,512]{3,2,1,0:T(8,128)(2,1)S(1)}, u32[]{:S(2)}, u32[]{:S(2)}) %collective-permute-start.77) | collective-permute-done | bytes 655392 | tf_op jit(solution)/shard_map/ppermute | solution.py:68
  414.9 2.2 place_fourth.1
  417.1 4.0 collective-permute-done.79.other_ref
  421.1 1.8 place_last.1
  (453 shorter events, 80.7 us)
Async XLA Ops:
  7.4 20.3 %collective-permute-start.6 = (bf16[256,1536]{1,0:T(8,128)(2,1)}, bf16[256,1536]{1,0:T(8,128)(2,1)}, u32[]{:S(2)}, u32[]{:S(2)}) collective-permute-start(bf16[256,1536]{1,0:T(8,128)(2,1)} %pad_maximum_fusion.9.refs_0_.refs_6_), channel_id=1, source_target_pairs={{0,16},{8,24},{16,0},{24,8},{1,17},{9,25},{17,1},{25,9},{2,18},{10... | collective-permute-start | bytes 2359304 | tf_op jit(solution)/shard_map/ppermute | solution.py:68
  7.6 21.2 %collective-permute-start.5 = (bf16[256,1536]{1,0:T(8,128)(2,1)}, bf16[256,1536]{1,0:T(8,128)(2,1)}, u32[]{:S(2)}, u32[]{:S(2)}) collective-permute-start(bf16[256,1536]{1,0:T(8,128)(2,1)} %pad_maximum_fusion.9.refs_0_.refs_6_), channel_id=1, source_target_pairs={{0,8},{8,0},{16,24},{24,16},{1,9},{9,1},{17,25},{25,17},{2,10},{10... | collective-permute-start | bytes 2359304 | tf_op jit(solution)/shard_map/ppermute | solution.py:68
  39.5 14.5 %collective-permute-start.8 = (bf16[128,1536]{1,0:T(8,128)(2,1)S(1)}, bf16[128,1536]{1,0:T(8,128)(2,1)S(1)}, u32[]{:S(2)}, u32[]{:S(2)}) collective-permute-start(bf16[128,1536]{1,0:T(8,128)(2,1)S(1)} %collective-permute-done.3.refs_2_.refs_12_), channel_id=1, source_target_pairs={{0,1},{1,0},{2,3},{3,2},{4,5},{5,4},{6,7},{7,6},{8,9},{9,8},{10,11... | collective-permute-start | bytes 1179656 | tf_op jit(solution)/shard_map/ppermute | solution.py:68
  41.1 15.3 %collective-permute-start.10 = (bf16[2,256,1024]{2,1,0:T(8,128)(2,1)S(1)}, bf16[2,256,1024]{2,1,0:T(8,128)(2,1)S(1)}, u32[]{:S(2)}, u32[]{:S(2)}) collective-permute-start(bf16[2,256,1024]{2,1,0:T(8,128)(2,1)S(1)} %pad_maximum_fusion.1.refs_0_), channel_id=1, source_target_pairs={{0,8},{8,0},{16,24},{24,16},{1,9},{9,1},{17,25},{25,17},{2,10},{10... | collective-permute-start | bytes 3145736 | tf_op jit(solution)/shard_map/ppermute | solution.py:68
  41.1 14.3 %collective-permute-start.9 = (bf16[2,128,1024]{2,1,0:T(8,128)(2,1)S(1)}, bf16[2,128,1024]{2,1,0:T(8,128)(2,1)S(1)}, u32[]{:S(2)}, u32[]{:S(2)}) collective-permute-start(bf16[2,128,1024]{2,1,0:T(8,128)(2,1)S(1)} %copy-done.95), channel_id=1, source_target_pairs={{0,16},{8,24},{16,0},{24,8},{1,17},{9,25},{17,1},{25,9},{2,18},{10... | collective-permute-start | bytes 1572872 | tf_op jit(solution)/shard_map/ppermute | solution.py:68
  56.4 21.6 %collective-permute-start.15 = (bf16[2,128,1024]{2,1,0:T(8,128)(2,1)S(1)}, bf16[2,128,1024]{2,1,0:T(8,128)(2,1)S(1)}, u32[]{:S(2)}, u32[]{:S(2)}) collective-permute-start(bf16[2,128,1024]{2,1,0:T(8,128)(2,1)S(1)} %collective-permute-done.9.refs_2_), channel_id=1, source_target_pairs={{0,1},{1,0},{2,3},{3,2},{4,5},{5,4},{6,7},{7,6},{8,9},{9,8},{10,11... | collective-permute-start | bytes 1572872 | tf_op jit(solution)/shard_map/ppermute | solution.py:68
  64.1 14.3 %collective-permute-start.18 = (bf16[2,256,1024]{2,1,0:T(8,128)(2,1)S(1)}, bf16[2,256,1024]{2,1,0:T(8,128)(2,1)S(1)}, u32[]{:S(2)}, u32[]{:S(2)}) collective-permute-start(bf16[2,256,1024]{2,1,0:T(8,128)(2,1)S(1)} %pad_maximum_fusion.2.refs_0_.refs_6_), channel_id=1, source_target_pairs={{0,8},{8,0},{16,24},{24,16},{1,9},{9,1},{17,25},{25,17},{2,10},{10... | collective-permute-start | bytes 3145736 | tf_op jit(solution)/shard_map/ppermute | solution.py:68
  89.0 21.7 %collective-permute-start.23 = (bf16[2,256,1024]{2,1,0:T(8,128)(2,1)S(1)}, bf16[2,256,1024]{2,1,0:T(8,128)(2,1)S(1)}, u32[]{:S(2)}, u32[]{:S(2)}) collective-permute-start(bf16[2,256,1024]{2,1,0:T(8,128)(2,1)S(1)} %pad_maximum_fusion.3.refs_0_.refs_12_), channel_id=1, source_target_pairs={{0,8},{8,0},{16,24},{24,16},{1,9},{9,1},{17,25},{25,17},{2,10},{10... | collective-permute-start | bytes 3145736 | tf_op jit(solution)/shard_map/ppermute | solution.py:68
  89.4 21.0 %collective-permute-start.22 = (bf16[2,128,1024]{2,1,0:T(8,128)(2,1)S(1)}, bf16[2,128,1024]{2,1,0:T(8,128)(2,1)S(1)}, u32[]{:S(2)}, u32[]{:S(2)}) collective-permute-start(bf16[2,128,1024]{2,1,0:T(8,128)(2,1)S(1)} %copy-done.97), channel_id=1, source_target_pairs={{0,16},{8,24},{16,0},{24,8},{1,17},{9,25},{17,1},{25,9},{2,18},{10... | collective-permute-start | bytes 1572872 | tf_op jit(solution)/shard_map/ppermute | solution.py:68
  90.2 19.8 %collective-permute-start.21 = (bf16[2,128,1024]{2,1,0:T(8,128)(2,1)S(1)}, bf16[2,128,1024]{2,1,0:T(8,128)(2,1)S(1)}, u32[]{:S(2)}, u32[]{:S(2)}) collective-permute-start(bf16[2,128,1024]{2,1,0:T(8,128)(2,1)S(1)} %collective-permute-done.17.refs_2_.refs_8_), channel_id=1, source_target_pairs={{0,1},{1,0},{2,3},{3,2},{4,5},{5,4},{6,7},{7,6},{8,9},{9,8},{10,11... | collective-permute-start | bytes 1572872 | tf_op jit(solution)/shard_map/ppermute | solution.py:68
  91.5 23.3 %collective-permute-start.25 = (bf16[2,256,1024]{2,1,0:T(8,128)(2,1)S(1)}, bf16[2,256,1024]{2,1,0:T(8,128)(2,1)S(1)}, u32[]{:S(2)}, u32[]{:S(2)}) collective-permute-start(bf16[2,256,1024]{2,1,0:T(8,128)(2,1)S(1)} %pad_maximum_fusion.4.refs_0_.refs_18_), channel_id=1, source_target_pairs={{0,8},{8,0},{16,24},{24,16},{1,9},{9,1},{17,25},{25,17},{2,10},{10... | collective-permute-start | bytes 3145736 | tf_op jit(solution)/shard_map/ppermute | solution.py:68
  91.5 23.2 %collective-permute-start.24 = (bf16[2,128,1024]{2,1,0:T(8,128)(2,1)S(1)}, bf16[2,128,1024]{2,1,0:T(8,128)(2,1)}, u32[]{:S(2)}, u32[]{:S(2)}) collective-permute-start(bf16[2,128,1024]{2,1,0:T(8,128)(2,1)S(1)} %copy-done.96), channel_id=1, source_target_pairs={{0,16},{8,24},{16,0},{24,8},{1,17},{9,25},{17,1},{25,9},{2,18},{10... | collective-permute-start | bytes 1572872 | tf_op jit(solution)/shard_map/ppermute | solution.py:68
  110.7 21.7 %collective-permute-start.29 = (bf16[2,128,1024]{2,1,0:T(8,128)(2,1)S(1)}, bf16[2,128,1024]{2,1,0:T(8,128)(2,1)S(1)}, u32[]{:S(2)}, u32[]{:S(2)}) collective-permute-start(bf16[2,128,1024]{2,1,0:T(8,128)(2,1)S(1)} %collective-permute-done.22.refs_2_.refs_14_), channel_id=1, source_target_pairs={{0,1},{1,0},{2,3},{3,2},{4,5},{5,4},{6,7},{7,6},{8,9},{9,8},{10,11... | collective-permute-start | bytes 1572872 | tf_op jit(solution)/shard_map/ppermute | solution.py:68
  114.8 20.0 %collective-permute-start.28 = (bf16[2,2,256,1024]{3,2,1,0:T(8,128)(2,1)}, bf16[2,2,256,1024]{3,2,1,0:T(8,128)(2,1)}, u32[]{:S(2)}, u32[]{:S(2)}) collective-permute-start(bf16[2,2,256,1024]{3,2,1,0:T(8,128)(2,1)} %get-tuple-element.300), channel_id=1, source_target_pairs={{0,8},{8,0},{16,24},{24,16},{1,9},{9,1},{17,25},{25,17},{2,10},{10... | collective-permute-start | bytes 6291464 | tf_op jit(solution)/shard_map/ppermute | solution.py:68
  133.1 22.6 %collective-permute-start.33 = (bf16[2,128,1024]{2,1,0:T(8,128)(2,1)}, bf16[2,128,1024]{2,1,0:T(8,128)(2,1)}, u32[]{:S(2)}, u32[]{:S(2)}) collective-permute-start(bf16[2,128,1024]{2,1,0:T(8,128)(2,1)} %collective-permute-done.24.refs_2_.refs_20_), channel_id=1, source_target_pairs={{0,1},{1,0},{2,3},{3,2},{4,5},{5,4},{6,7},{7,6},{8,9},{9,8},{10,11... | collective-permute-start | bytes 1572872 | tf_op jit(solution)/shard_map/ppermute | solution.py:68
  134.6 21.8 %collective-permute-start.32 = (bf16[2,2,256,1024]{3,2,1,0:T(8,128)(2,1)}, bf16[2,2,256,1024]{3,2,1,0:T(8,128)(2,1)}, u32[]{:S(2)}, u32[]{:S(2)}) collective-permute-start(bf16[2,2,256,1024]{3,2,1,0:T(8,128)(2,1)} %get-tuple-element.312), channel_id=1, source_target_pairs={{0,8},{8,0},{16,24},{24,16},{1,9},{9,1},{17,25},{25,17},{2,10},{10... | collective-permute-start | bytes 6291464 | tf_op jit(solution)/shard_map/ppermute | solution.py:68
  138.0 26.2 %collective-permute-start.34 = (bf16[2,256,1024]{2,1,0:T(8,128)(2,1)}, bf16[2,256,1024]{2,1,0:T(8,128)(2,1)S(1)}, u32[]{:S(2)}, u32[]{:S(2)}) collective-permute-start(bf16[2,256,1024]{2,1,0:T(8,128)(2,1)} %get-tuple-element.314), channel_id=1, source_target_pairs={{0,16},{8,24},{16,0},{24,8},{1,17},{9,25},{17,1},{25,9},{2,18},{10... | collective-permute-start | bytes 3145736 | tf_op jit(solution)/shard_map/ppermute | solution.py:68
  156.3 31.8 %collective-permute-start.37 = (bf16[2,2,256,1024]{3,2,1,0:T(8,128)(2,1)}, bf16[2,2,256,1024]{3,2,1,0:T(8,128)(2,1)S(1)}, u32[]{:S(2)}, u32[]{:S(2)}) collective-permute-start(bf16[2,2,256,1024]{3,2,1,0:T(8,128)(2,1)} %get-tuple-element.325), channel_id=1, source_target_pairs={{0,8},{8,0},{16,24},{24,16},{1,9},{9,1},{17,25},{25,17},{2,10},{10... | collective-permute-start | bytes 6291464 | tf_op jit(solution)/shard_map/ppermute | solution.py:68
  158.9 27.2 %collective-permute-start.38 = (bf16[2,256,1024]{2,1,0:T(8,128)(2,1)S(1)}, bf16[2,256,1024]{2,1,0:T(8,128)(2,1)S(1)}, u32[]{:S(2)}, u32[]{:S(2)}) collective-permute-start(bf16[2,256,1024]{2,1,0:T(8,128)(2,1)S(1)} %get-tuple-element.326), channel_id=1, source_target_pairs={{0,16},{8,24},{16,0},{24,8},{1,17},{9,25},{17,1},{25,9},{2,18},{10... | collective-permute-start | bytes 3145736 | tf_op jit(solution)/shard_map/ppermute | solution.py:68
  181.7 38.4 %collective-permute-start.41 = (bf16[2,2,256,1024]{3,2,1,0:T(8,128)(2,1)}, bf16[2,2,256,1024]{3,2,1,0:T(8,128)(2,1)S(1)}, u32[]{:S(2)}, u32[]{:S(2)}) collective-permute-start(bf16[2,2,256,1024]{3,2,1,0:T(8,128)(2,1)} %get-tuple-element.340), channel_id=1, source_target_pairs={{0,8},{8,0},{16,24},{24,16},{1,9},{9,1},{17,25},{25,17},{2,10},{10... | collective-permute-start | bytes 6291464 | tf_op jit(solution)/shard_map/ppermute | solution.py:68
  187.6 30.5 %collective-permute-start.43 = (bf16[4,128,1024]{2,1,0:T(8,128)(2,1)}, bf16[4,128,1024]{2,1,0:T(8,128)(2,1)S(1)}, u32[]{:S(2)}, u32[]{:S(2)}) collective-permute-start(bf16[4,128,1024]{2,1,0:T(8,128)(2,1)} %pad_maximum_fusion.5), channel_id=1, source_target_pairs={{0,1},{1,0},{2,3},{3,2},{4,5},{5,4},{6,7},{7,6},{8,9},{9,8},{10,11... | collective-permute-start | bytes 3145736 | tf_op jit(solution)/shard_map/ppermute | solution.py:68
  189.4 30.8 %collective-permute-start.42 = (bf16[2,256,1024]{2,1,0:T(8,128)(2,1)}, bf16[2,256,1024]{2,1,0:T(8,128)(2,1)S(1)}, u32[]{:S(2)}, u32[]{:S(2)}) collective-permute-start(bf16[2,256,1024]{2,1,0:T(8,128)(2,1)} %get-tuple-element.341), channel_id=1, source_target_pairs={{0,16},{8,24},{16,0},{24,8},{1,17},{9,25},{17,1},{25,9},{2,18},{10... | collective-permute-start | bytes 3145736 | tf_op jit(solution)/shard_map/ppermute | solution.py:68
  218.0 27.7 %collective-permute-start.45 = (bf16[2,2,256,512]{3,2,1,0:T(8,128)(2,1)}, bf16[2,2,256,512]{3,2,1,0:T(8,128)(2,1)S(1)}, u32[]{:S(2)}, u32[]{:S(2)}) collective-permute-start(bf16[2,2,256,512]{3,2,1,0:T(8,128)(2,1)} %get-tuple-element.357), channel_id=1, source_target_pairs={{0,8},{8,0},{16,24},{24,16},{1,9},{9,1},{17,25},{25,17},{2,10},{10... | collective-permute-start | bytes 3145736 | tf_op jit(solution)/shard_map/ppermute | solution.py:68
  218.5 27.0 %collective-permute-start.46 = (bf16[4,64,1024]{2,1,0:T(8,128)(2,1)S(1)}, bf16[4,64,1024]{2,1,0:T(8,128)(2,1)S(1)}, u32[]{:S(2)}, u32[]{:S(2)}) collective-permute-start(bf16[4,64,1024]{2,1,0:T(8,128)(2,1)S(1)} %get-tuple-element.358), channel_id=1, source_target_pairs={{0,2},{1,3},{2,0},{3,1},{4,6},{5,7},{6,4},{7,5},{8,10},{9,11},{10,... | collective-permute-start | bytes 1572872 | tf_op jit(solution)/shard_map/ppermute | solution.py:68
  220.9 31.3 %collective-permute-start.44 = (bf16[2,256,1024]{2,1,0:T(8,128)(2,1)S(1)}, bf16[2,256,1024]{2,1,0:T(8,128)(2,1)S(1)}, u32[]{:S(2)}, u32[]{:S(2)}) collective-permute-start(bf16[2,256,1024]{2,1,0:T(8,128)(2,1)S(1)} %get-tuple-element.355), channel_id=1, source_target_pairs={{0,16},{8,24},{16,0},{24,8},{1,17},{9,25},{17,1},{25,9},{2,18},{10... | collective-permute-start | bytes 3145736 | tf_op jit(solution)/shard_map/ppermute | solution.py:68
  221.7 29.2 %collective-permute-start.47 = (bf16[2,128,1024]{2,1,0:T(8,128)(2,1)S(1)}, bf16[2,128,1024]{2,1,0:T(8,128)(2,1)S(1)}, u32[]{:S(2)}, u32[]{:S(2)}) collective-permute-start(bf16[2,128,1024]{2,1,0:T(8,128)(2,1)S(1)} %get-tuple-element.359), channel_id=1, source_target_pairs={{0,1},{1,0},{2,3},{3,2},{4,5},{5,4},{6,7},{7,6},{8,9},{9,8},{10,11... | collective-permute-start | bytes 1572872 | tf_op jit(solution)/shard_map/ppermute | solution.py:68
  245.7 29.9 %collective-permute-start.50 = (bf16[4,64,1024]{2,1,0:T(8,128)(2,1)S(1)}, bf16[4,64,1024]{2,1,0:T(8,128)(2,1)S(1)}, u32[]{:S(2)}, u32[]{:S(2)}) collective-permute-start(bf16[4,64,1024]{2,1,0:T(8,128)(2,1)S(1)} %add.277), channel_id=1, source_target_pairs={{0,4},{1,5},{2,6},{3,7},{4,0},{5,1},{6,2},{7,3},{8,12},{9,13},{10,... | collective-permute-start | bytes 1572872 | tf_op jit(solution)/shard_map/ppermute | solution.py:68
  248.4 29.5 %collective-permute-start.48 = (bf16[2,3,256,512]{3,2,1,0:T(8,128)(2,1)S(1)}, bf16[2,3,256,512]{3,2,1,0:T(8,128)(2,1)S(1)}, u32[]{:S(2)}, u32[]{:S(2)}) collective-permute-start(bf16[2,3,256,512]{3,2,1,0:T(8,128)(2,1)S(1)} %get-tuple-element.373), channel_id=1, source_target_pairs={{0,8},{8,0},{16,24},{24,16},{1,9},{9,1},{17,25},{25,17},{2,10},{10... | collective-permute-start | bytes 4718600 | tf_op jit(solution)/shard_map/ppermute | solution.py:68
  249.5 28.6 %collective-permute-start.49 = (bf16[2,256,512]{2,1,0:T(8,128)(2,1)}, bf16[2,256,512]{2,1,0:T(8,128)(2,1)S(1)}, u32[]{:S(2)}, u32[]{:S(2)}) collective-permute-start(bf16[2,256,512]{2,1,0:T(8,128)(2,1)} %get-tuple-element.374), channel_id=1, source_target_pairs={{0,16},{8,24},{16,0},{24,8},{1,17},{9,25},{17,1},{25,9},{2,18},{10... | collective-permute-start | bytes 1572872 | tf_op jit(solution)/shard_map/ppermute | solution.py:68
  251.1 24.4 %collective-permute-start.51 = (bf16[2,64,1024]{2,1,0:T(8,128)(2,1)S(1)}, bf16[2,64,1024]{2,1,0:T(8,128)(2,1)S(1)}, u32[]{:S(2)}, u32[]{:S(2)}) collective-permute-start(bf16[2,64,1024]{2,1,0:T(8,128)(2,1)S(1)} %get-tuple-element.376), channel_id=1, source_target_pairs={{0,2},{1,3},{2,0},{3,1},{4,6},{5,7},{6,4},{7,5},{8,10},{9,11},{10,... | collective-permute-start | bytes 786440 | tf_op jit(solution)/shard_map/ppermute | solution.py:68
  252.6 25.3 %collective-permute-start.52 = (bf16[2,128,1024]{2,1,0:T(8,128)(2,1)S(1)}, bf16[2,128,1024]{2,1,0:T(8,128)(2,1)S(1)}, u32[]{:S(2)}, u32[]{:S(2)}) collective-permute-start(bf16[2,128,1024]{2,1,0:T(8,128)(2,1)S(1)} %get-tuple-element.377), channel_id=1, source_target_pairs={{0,1},{1,0},{2,3},{3,2},{4,5},{5,4},{6,7},{7,6},{8,9},{9,8},{10,11... | collective-permute-start | bytes 1572872 | tf_op jit(solution)/shard_map/ppermute | solution.py:68
  275.8 18.1 %collective-permute-start.56 = (bf16[2,64,1024]{2,1,0:T(8,128)(2,1)S(1)}, bf16[2,64,1024]{2,1,0:T(8,128)(2,1)S(1)}, u32[]{:S(2)}, u32[]{:S(2)}) collective-permute-start(bf16[2,64,1024]{2,1,0:T(8,128)(2,1)S(1)} %add.286), channel_id=1, source_target_pairs={{0,4},{1,5},{2,6},{3,7},{4,0},{5,1},{6,2},{7,3},{8,12},{9,13},{10,... | collective-permute-start | bytes 786440 | tf_op jit(solution)/shard_map/ppermute | solution.py:68
  276.8 18.3 %collective-permute-start.55 = (bf16[4,64,1024]{2,1,0:T(8,128)(2,1)S(1)}, bf16[4,64,1024]{2,1,0:T(8,128)(2,1)S(1)}, u32[]{:S(2)}, u32[]{:S(2)}) collective-permute-start(bf16[4,64,1024]{2,1,0:T(8,128)(2,1)S(1)} %add.285), channel_id=1, source_target_pairs={{0,2},{1,3},{2,0},{3,1},{4,6},{5,7},{6,4},{7,5},{8,10},{9,11},{10,... | collective-permute-start | bytes 1572872 | tf_op jit(solution)/shard_map/ppermute | solution.py:68
  277.8 22.3 %collective-permute-start.53 = (bf16[2,3,256,512]{3,2,1,0:T(8,128)(2,1)S(1)}, bf16[2,3,256,512]{3,2,1,0:T(8,128)(2,1)S(1)}, u32[]{:S(2)}, u32[]{:S(2)}) collective-permute-start(bf16[2,3,256,512]{3,2,1,0:T(8,128)(2,1)S(1)} %get-tuple-element.390), channel_id=1, source_target_pairs={{0,8},{8,0},{16,24},{24,16},{1,9},{9,1},{17,25},{25,17},{2,10},{10... | collective-permute-start | bytes 4718600 | tf_op jit(solution)/shard_map/ppermute | solution.py:68
  278.3 20.0 %collective-permute-start.54 = (bf16[3,256,512]{2,1,0:T(8,128)(2,1)S(1)}, bf16[3,256,512]{2,1,0:T(8,128)(2,1)S(1)}, u32[]{:S(2)}, u32[]{:S(2)}) collective-permute-start(bf16[3,256,512]{2,1,0:T(8,128)(2,1)S(1)} %get-tuple-element.391), channel_id=1, source_target_pairs={{0,16},{8,24},{16,0},{24,8},{1,17},{9,25},{17,1},{25,9},{2,18},{10... | collective-permute-start | bytes 2359304 | tf_op jit(solution)/shard_map/ppermute | solution.py:68
  294.0 31.7 %collective-permute-start.62 = (bf16[2,64,1024]{2,1,0:T(8,128)(2,1)S(1)}, bf16[2,64,1024]{2,1,0:T(8,128)(2,1)S(1)}, u32[]{:S(2)}, u32[]{:S(2)}) collective-permute-start(bf16[2,64,1024]{2,1,0:T(8,128)(2,1)S(1)} %add.297), channel_id=1, source_target_pairs={{0,2},{1,3},{2,0},{3,1},{4,6},{5,7},{6,4},{7,5},{8,10},{9,11},{10,... | collective-permute-start | bytes 786440 | tf_op jit(solution)/shard_map/ppermute | solution.py:68
  296.2 43.3 %collective-permute-start.61 = (bf16[2,4,64,1024]{3,2,1,0:T(8,128)(2,1)S(1)}, bf16[2,4,64,1024]{3,2,1,0:T(8,128)(2,1)S(1)}, u32[]{:S(2)}, u32[]{:S(2)}) collective-permute-start(bf16[2,4,64,1024]{3,2,1,0:T(8,128)(2,1)S(1)} %pad_maximum_fusion.6.pair_ref), channel_id=1, source_target_pairs={{0,1},{1,0},{2,3},{3,2},{4,5},{5,4},{6,7},{7,6},{8,9},{9,8},{10,11... | collective-permute-start | bytes 3145736 | tf_op jit(solution)/shard_map/ppermute | solution.py:68
  298.6 37.8 %collective-permute-start.60 = (bf16[5,128,512]{2,1,0:T(8,128)(2,1)S(1)}, bf16[5,128,512]{2,1,0:T(8,128)(2,1)S(1)}, u32[]{:S(2)}, u32[]{:S(2)}) collective-permute-start(bf16[5,128,512]{2,1,0:T(8,128)(2,1)S(1)} %pad_maximum_fusion.10), channel_id=1, source_target_pairs={{0,1},{1,0},{2,3},{3,2},{4,5},{5,4},{6,7},{7,6},{8,9},{9,8},{10,11... | collective-permute-start | bytes 1966088 | tf_op jit(solution)/shard_map/ppermute | solution.py:68
  308.7 27.6 %collective-permute-start.59 = (bf16[3,256,512]{2,1,0:T(8,128)(2,1)S(1)}, bf16[3,256,512]{2,1,0:T(8,128)(2,1)S(1)}, u32[]{:S(2)}, u32[]{:S(2)}) collective-permute-start(bf16[3,256,512]{2,1,0:T(8,128)(2,1)S(1)} %get-tuple-element.417), channel_id=1, source_target_pairs={{0,16},{8,24},{16,0},{24,8},{1,17},{9,25},{17,1},{25,9},{2,18},{10... | collective-permute-start | bytes 2359304 | tf_op jit(solution)/shard_map/ppermute | solution.py:68
  325.8 24.7 %collective-permute-start.66 = (bf16[2,2,64,1024]{3,2,1,0:T(8,128)(2,1)S(1)}, bf16[2,2,64,1024]{3,2,1,0:T(8,128)(2,1)S(1)}, u32[]{:S(2)}, u32[]{:S(2)}) collective-permute-start(bf16[2,2,64,1024]{3,2,1,0:T(8,128)(2,1)S(1)} %pad_maximum_fusion.12.pair_ref), channel_id=1, source_target_pairs={{0,1},{1,0},{2,3},{3,2},{4,5},{5,4},{6,7},{7,6},{8,9},{9,8},{10,11... | collective-permute-start | bytes 1572872 | tf_op jit(solution)/shard_map/ppermute | solution.py:68
  327.4 15.0 %collective-permute-start.67 = (bf16[2,64,1024]{2,1,0:T(8,128)(2,1)S(1)}, bf16[2,64,1024]{2,1,0:T(8,128)(2,1)S(1)}, u32[]{:S(2)}, u32[]{:S(2)}) collective-permute-start(bf16[2,64,1024]{2,1,0:T(8,128)(2,1)S(1)} %add.303), channel_id=1, source_target_pairs={{0,4},{1,5},{2,6},{3,7},{4,0},{5,1},{6,2},{7,3},{8,12},{9,13},{10,... | collective-permute-start | bytes 786440 | tf_op jit(solution)/shard_map/ppermute | solution.py:68
  336.6 18.4 %collective-permute-start.64 = (bf16[3,128,512]{2,1,0:T(8,128)(2,1)S(1)}, bf16[3,128,512]{2,1,0:T(8,128)(2,1)S(1)}, u32[]{:S(2)}, u32[]{:S(2)}) collective-permute-start(bf16[3,128,512]{2,1,0:T(8,128)(2,1)S(1)} %get-tuple-element.434), channel_id=1, source_target_pairs={{0,1},{1,0},{2,3},{3,2},{4,5},{5,4},{6,7},{7,6},{8,9},{9,8},{10,11... | collective-permute-start | bytes 1179656 | tf_op jit(solution)/shard_map/ppermute | solution.py:68
  342.4 14.7 %collective-permute-start.71 = (bf16[2,64,1024]{2,1,0:T(8,128)(2,1)S(1)}, bf16[2,64,1024]{2,1,0:T(8,128)(2,1)S(1)}, u32[]{:S(2)}, u32[]{:S(2)}) collective-permute-start(bf16[2,64,1024]{2,1,0:T(8,128)(2,1)S(1)} %add.308), channel_id=1, source_target_pairs={{0,2},{1,3},{2,0},{3,1},{4,6},{5,7},{6,4},{7,5},{8,10},{9,11},{10,... | collective-permute-start | bytes 786440 | tf_op jit(solution)/shard_map/ppermute | solution.py:68
  349.2 16.8 %collective-permute-start.70 = (bf16[5,64,512]{2,1,0:T(8,128)(2,1)S(1)}, bf16[5,64,512]{2,1,0:T(8,128)(2,1)S(1)}, u32[]{:S(2)}, u32[]{:S(2)}) collective-permute-start(bf16[5,64,512]{2,1,0:T(8,128)(2,1)S(1)} %add.307), channel_id=1, source_target_pairs={{0,4},{1,5},{2,6},{3,7},{4,0},{5,1},{6,2},{7,3},{8,12},{9,13},{10,... | collective-permute-start | bytes 983048 | tf_op jit(solution)/shard_map/ppermute | solution.py:68
  357.2 32.3 %collective-permute-start.74 = (bf16[2,2,64,1024]{3,2,1,0:T(8,128)(2,1)S(1)}, bf16[2,2,64,1024]{3,2,1,0:T(8,128)(2,1)S(1)}, u32[]{:S(2)}, u32[]{:S(2)}) collective-permute-start(bf16[2,2,64,1024]{3,2,1,0:T(8,128)(2,1)S(1)} %pad_maximum_fusion.13.pair_ref), channel_id=1, source_target_pairs={{0,1},{1,0},{2,3},{3,2},{4,5},{5,4},{6,7},{7,6},{8,9},{9,8},{10,11... | collective-permute-start | bytes 1572872 | tf_op jit(solution)/shard_map/ppermute | solution.py:68
  366.1 15.1 %collective-permute-start.72 = (bf16[5,64,512]{2,1,0:T(8,128)(2,1)S(1)}, bf16[5,64,512]{2,1,0:T(8,128)(2,1)S(1)}, u32[]{:S(2)}, u32[]{:S(2)}) collective-permute-start(bf16[5,64,512]{2,1,0:T(8,128)(2,1)S(1)} %add.312), channel_id=1, source_target_pairs={{0,2},{1,3},{2,0},{3,1},{4,6},{5,7},{6,4},{7,5},{8,10},{9,11},{10,... | collective-permute-start | bytes 983048 | tf_op jit(solution)/shard_map/ppermute | solution.py:68
  397.2 17.7 %collective-permute-start.77 = (bf16[2,5,64,512]{3,2,1,0:T(8,128)(2,1)S(1)}, bf16[2,5,64,512]{3,2,1,0:T(8,128)(2,1)S(1)}, u32[]{:S(2)}, u32[]{:S(2)}) collective-permute-start(bf16[2,5,64,512]{3,2,1,0:T(8,128)(2,1)S(1)} %pad_maximum_fusion.11.pair_ref), channel_id=1, source_target_pairs={{0,1},{1,0},{2,3},{3,2},{4,5},{5,4},{6,7},{7,6},{8,9},{9,8},{10,11... | collective-permute-start | bytes 1966088 | tf_op jit(solution)/shard_map/ppermute | solution.py:68
  403.2 17.9 %collective-permute-start.79 = (bf16[2,3,64,512]{3,2,1,0:T(8,128)(2,1)S(1)}, bf16[2,3,64,512]{3,2,1,0:T(8,128)(2,1)S(1)}, u32[]{:S(2)}, u32[]{:S(2)}) collective-permute-start(bf16[2,3,64,512]{3,2,1,0:T(8,128)(2,1)S(1)} %pad_maximum_fusion.14.pair_ref), channel_id=1, source_target_pairs={{0,1},{1,0},{2,3},{3,2},{4,5},{5,4},{6,7},{7,6},{8,9},{9,8},{10,11... | collective-permute-start | bytes 1179656 | tf_op jit(solution)/shard_map/ppermute | solution.py:68
  (155 other events, 1338.2 us)
